TPU v7x, 1024 devices: a whole 4x8x16 slice. The times are simulated.
1024 devices in a mesh: sy: 32 (over y, x), sx: 32 (over z, core).
Axes of the slice: x: 4, y: 8, z: 16, core: 2. Of those that a mesh axis runs over, the one named last changes fastest.
Arguments:
- obj_delta: float32 [2, 2, 4096, 4096], P(None, None, 'sy', 'sx'), may hold values from -1.8 to 1.8
- probe_mean: float32 [2, 128, 128], replicated, may hold values from -6 to 6
- probe_basis: float32 [8, 2, 128, 128], replicated, may hold values from -4.2 to 4.2
- mode_weights: float32 [32, 32, 2, 8], P('sy', 'sx'), may hold values from -3 to 3
- positions: int32 [32, 32, 2, 2], P('sy', 'sx'), may hold values from 0 to 127
- amplitudes: float32 [32, 32, 2, 128, 128], P('sy', 'sx'), may hold values from 0 to 3
Outputs:
- obj_grad: float32 [2, 2, 4096, 4096], P(None, None, 'sy', 'sx')
- new_basis: float32 [8, 2, 128, 128], replicated
Inputs may be any that keep to these rules, and one draw needn't show every extreme that they name: `positions`: offsets of each probe window's centre from its tile's first row and column.
All inputs are finite; a program needn't handle non-finite values.
Results may differ from a plain program's by a relative error of at most 0.00016.
Values sent between devices are 32-bit elements; how exact they have to be, the bound alone decides.
No kernel may reach another device: no remote copies, remote signals or barrier semaphores. Data moves between devices by JAX's collectives and lax.ppermute only.
A program may use at most 32 MiB of HBM per device.

v0:
```python
import math

import jax
import jax.numpy as jnp
from jax import lax
from jax.sharding import PartitionSpec as P

FLOOR = 0.5
PHASE_EDGE = 3.0
HIGHEST = lax.Precision.HIGHEST


def padded(block, sides, width):
    for axis, dim in sides:
        count = lax.axis_size(axis)
        forward = [(i, i + 1) for i in range(count - 1)]
        backward = [(target, source) for source, target in forward]
        low = lax.ppermute(
            lax.slice_in_dim(block, block.shape[dim] - width, None, axis=dim), axis, forward
        )
        high = lax.ppermute(lax.slice_in_dim(block, 0, width, axis=dim), axis, backward)
        block = jnp.concatenate([low, block, high], axis=dim)
    return block


def propagator(probe_len):
    shifted = (jnp.arange(probe_len, dtype=jnp.int32) + probe_len // 2) % probe_len - probe_len // 2
    frequency = shifted.astype(jnp.float32) / (probe_len // 2)
    phases = PHASE_EDGE * (
        frequency[:, None] * frequency[:, None] + frequency[None, :] * frequency[None, :]
    )
    return (jnp.cos(phases), -jnp.sin(phases))


def dft_tables(probe_len):
    indices = jnp.arange(probe_len, dtype=jnp.int32)
    product = indices[:, None] * indices[None, :] % probe_len
    angles = product.astype(jnp.float32) * (2.0 * math.pi / probe_len)
    norming = 1.0 / math.sqrt(probe_len)
    return (jnp.cos(angles) * norming, -jnp.sin(angles) * norming)


def left_product(table, values):
    return jnp.einsum("ij,pjk->pik", table, values, precision=HIGHEST)


def right_product(values, table):
    return jnp.einsum("pij,jk->pik", values, table, precision=HIGHEST)


def transform(wave_real, wave_imag, table_real, table_imag):
    half_real = left_product(table_real, wave_real) - left_product(table_imag, wave_imag)
    half_imag = left_product(table_real, wave_imag) + left_product(table_imag, wave_real)
    result_real = right_product(half_real, table_real) - right_product(half_imag, table_imag)
    result_imag = right_product(half_real, table_imag) + right_product(half_imag, table_real)
    return (result_real, result_imag)


def propagate(wave_real, wave_imag, table_real, table_imag, kernel_real, kernel_imag):
    spectrum_real, spectrum_imag = transform(wave_real, wave_imag, table_real, table_imag)
    scaled_real = spectrum_real * kernel_real - spectrum_imag * kernel_imag
    scaled_imag = spectrum_real * kernel_imag + spectrum_imag * kernel_real
    return transform(scaled_real, scaled_imag, table_real, -table_imag)


def orthonormal(vec_real, vec_imag, count):
    gram_real = (
        jnp.dot(vec_real, vec_real.T, precision=HIGHEST)
        + jnp.dot(vec_imag, vec_imag.T, precision=HIGHEST)
    ) / count
    gram_imag = (
        jnp.dot(vec_real, vec_imag.T, precision=HIGHEST)
        - jnp.dot(vec_imag, vec_real.T, precision=HIGHEST)
    ) / count
    modes = vec_real.shape[0]
    upper_real = [[None] * modes for unused in range(modes)]
    upper_imag = [[None] * modes for unused in range(modes)]
    for row_at in range(modes):
        total_diag = gram_real[row_at, row_at]
        for inner in range(row_at):
            total_diag = (
                total_diag
                - upper_real[inner][row_at] * upper_real[inner][row_at]
                - upper_imag[inner][row_at] * upper_imag[inner][row_at]
            )
        pivot = jnp.sqrt(total_diag)
        upper_real[row_at][row_at] = pivot
        upper_imag[row_at][row_at] = jnp.zeros_like(pivot)
        for column_at in range(row_at + 1, modes):
            entry_real = gram_real[row_at, column_at]
            entry_imag = gram_imag[row_at, column_at]
            for inner in range(row_at):
                left_real = upper_real[inner][row_at]
                left_imag = upper_imag[inner][row_at]
                right_real = upper_real[inner][column_at]
                right_imag = upper_imag[inner][column_at]
                entry_real = entry_real - (left_real * right_real + left_imag * right_imag)
                entry_imag = entry_imag - (left_real * right_imag - left_imag * right_real)
            upper_real[row_at][column_at] = entry_real / pivot
            upper_imag[row_at][column_at] = entry_imag / pivot
    result_real = []
    result_imag = []
    for column_at in range(modes):
        total_real = vec_real[column_at]
        total_imag = vec_imag[column_at]
        for inner in range(column_at):
            factor_real = upper_real[inner][column_at]
            factor_imag = upper_imag[inner][column_at]
            total_real = total_real - (
                factor_real * result_real[inner] - factor_imag * result_imag[inner]
            )
            total_imag = total_imag - (
                factor_real * result_imag[inner] + factor_imag * result_real[inner]
            )
        pivot = upper_real[column_at][column_at]
        result_real.append(total_real / pivot)
        result_imag.append(total_imag / pivot)
    return (jnp.stack(result_real), jnp.stack(result_imag))


def fold(framed, axis_dim, tile_len, probe_len):
    half_len = probe_len // 2
    core = lax.slice_in_dim(framed, probe_len, probe_len + tile_len, axis=axis_dim)
    upper_rim = lax.slice_in_dim(framed, 0, half_len, axis=axis_dim)
    lower_rim = lax.slice_in_dim(
        framed, tile_len + probe_len + half_len, tile_len + 2 * probe_len, axis=axis_dim
    )
    upper_pad = [(0, 0)] * framed.ndim
    upper_pad[axis_dim] = (0, tile_len - half_len)
    lower_pad = [(0, 0)] * framed.ndim
    lower_pad[axis_dim] = (tile_len - half_len, 0)
    return core + jnp.pad(upper_rim, upper_pad) + jnp.pad(lower_rim, lower_pad)


def local(obj_delta, probe_mean, probe_basis, mode_weights, positions, amplitudes):
    slice_count = obj_delta.shape[0]
    tile_len = obj_delta.shape[-1]
    probe_len = probe_mean.shape[-1]
    half_len = probe_len // 2
    modes = probe_basis.shape[0]
    per_tile = positions.shape[2]
    framed = padded(obj_delta, (("sy", 2), ("sx", 3)), half_len)
    row_starts = positions[0, 0, :, 0]
    col_starts = positions[0, 0, :, 1]
    window_shape = (slice_count, 2, probe_len, probe_len)
    windows = jnp.stack(
        [
            lax.dynamic_slice(framed, (0, 0, row_starts[slot], col_starts[slot]), window_shape)
            for slot in range(per_tile)
        ]
    )
    weights = mode_weights[0, 0]
    measured = amplitudes[0, 0]
    mixed = jnp.einsum("pk,kcij->pcij", weights, probe_basis, precision=HIGHEST)
    wave_real = probe_mean[0][None] + mixed[:, 0]
    wave_imag = probe_mean[1][None] + mixed[:, 1]
    table_real, table_imag = dft_tables(probe_len)
    kernel_real, kernel_imag = propagator(probe_len)
    entering = []
    transmit = []
    for layer in range(slice_count):
        if layer > 0:
            wave_real, wave_imag = propagate(
                wave_real, wave_imag, table_real, table_imag, kernel_real, kernel_imag
            )
        entering.append((wave_real, wave_imag))
        trans_real = 1.0 + windows[:, layer, 0]
        trans_imag = windows[:, layer, 1]
        transmit.append((trans_real, trans_imag))
        wave_real, wave_imag = (
            wave_real * trans_real - wave_imag * trans_imag,
            wave_real * trans_imag + wave_imag * trans_real,
        )
    far_real, far_imag = transform(wave_real, wave_imag, table_real, table_imag)
    modulus = jnp.maximum(jnp.sqrt(far_real * far_real + far_imag * far_imag), FLOOR)
    chi_real = far_real - measured * far_real / modulus
    chi_imag = far_imag - measured * far_imag / modulus
    back_real, back_imag = transform(chi_real, chi_imag, table_real, -table_imag)
    slice_grads = [None] * slice_count
    for layer in range(slice_count - 1, -1, -1):
        enter_real, enter_imag = entering[layer]
        slice_grads[layer] = jnp.stack(
            [
                enter_real * back_real + enter_imag * back_imag,
                enter_real * back_imag - enter_imag * back_real,
            ],
            axis=1,
        )
        trans_real, trans_imag = transmit[layer]
        back_real, back_imag = (
            trans_real * back_real + trans_imag * back_imag,
            trans_real * back_imag - trans_imag * back_real,
        )
        if layer > 0:
            back_real, back_imag = propagate(
                back_real, back_imag, table_real, table_imag, kernel_real, -kernel_imag
            )
    gradients = jnp.stack(slice_grads, axis=1)
    extended = jnp.zeros(framed.shape, jnp.float32)
    for slot in range(per_tile):
        start = (0, 0, row_starts[slot], col_starts[slot])
        current = lax.dynamic_slice(extended, start, window_shape)
        extended = lax.dynamic_update_slice(extended, current + gradients[slot], start)
    beside_all = padded(extended, (("sy", 2), ("sx", 3)), half_len)
    obj_grad = fold(fold(beside_all, 2, tile_len, probe_len), 3, tile_len, probe_len)
    probe_grad = jnp.stack([back_real, back_imag], axis=1)
    local_term = jnp.einsum("pk,pcij->kcij", weights, probe_grad, precision=HIGHEST)
    summed = lax.psum(local_term, ("sy", "sx"))
    count_all = per_tile * lax.axis_size("sy") * lax.axis_size("sx")
    step_len = 1.0 / math.sqrt(count_all)
    updated = probe_basis - step_len * summed
    flat_real = updated[:, 0].reshape(modes, -1)
    flat_imag = updated[:, 1].reshape(modes, -1)
    new_real, new_imag = orthonormal(flat_real, flat_imag, probe_len * probe_len)
    new_basis = jnp.stack([new_real, new_imag], axis=1).reshape(probe_basis.shape)
    return (obj_grad, new_basis)


def solution(mesh):
    placed = (
        P(None, None, "sy", "sx"),
        P(),
        P(),
        P("sy", "sx", None, None),
        P("sy", "sx", None, None),
        P("sy", "sx", None, None, None),
    )
    return jax.shard_map(
        local,
        mesh=mesh,
        in_specs=placed,
        out_specs=(P(None, None, "sy", "sx"), P()),
        check_vma=False,
    )
```

profile of v0, /device:TPU:1, one launch (start us, length us, event | category | flops | bytes accessed | tf_op | source)
XLA Modules:
  0.0 650.2 jit_solution(2605919802164777939)
XLA Ops:
  7.2 1.0 fusion.469
  8.3 4.0 collective-permute-start
  12.2 1.3 collective-permute-start.1
  13.9 2.7 fusion.16
  16.6 0.9 slice_bitcast_fusion.3
  17.9 0.9 fusion.468
  18.9 14.5 %collective-permute-start.3 = (f32[2,2,256,64]{3,2,1,0:T(8,128)}, f32[2,2,256,64]{3,2,1,0:T(8,128)S(1)}, u32[]{:S(2)}, u32[]{:S(2)}) collective-permute-start(f32[2,2,256,64]{3,2,1,0:T(8,128)} %get-tuple-element.37), channel_id=1, source_target_pairs={{1,0},{2,1},{3,2},{4,3},{5,4},{6,5},{7,6},{8,7},{9,8},{10,9},{11,1... | collective-permute-start | bytes 786440 | tf_op jit(solution)/shard_map/ppermute | solution.py:21
  33.4 2.1 collective-permute-start.2
  56.3 1.0 fusion.6
  69.7 0.7 fusion.148
  72.3 3.3 dynamic_update_slice.6
  75.7 3.2 dynamic_update_slice.7
  79.0 1.3 collective-permute-start.5
  80.3 4.0 collective-permute-start.4
  84.4 1.1 fusion.37
  85.5 1.2 copy.297
  86.7 1.7 collective-permute-done.5
  88.4 0.9 collective-permute-done.4
  89.2 0.7 copy-done.2
  90.0 1.1 fusion.466
  91.2 2.1 copy.193
  93.3 3.5 collective-permute-start.7
  96.8 1.0 copy.192
  97.8 2.0 collective-permute-start.6
  99.9 474.0 %all-reduce.4.cloned.1.call-done = f32[8,2,128,128]{3,2,1,0:T(8,128)} async-done(((f32[8,2,128,128]{3,2,1,0:T(8,128)}), f32[8,2,128,128]{3,2,1,0:T(8,128)}) %all-reduce.4.cloned.1.call-update) | async-done | bytes 1048592 | tf_op jit(solution)/shard_map/psum | solution.py:208
  573.9 1.4 multiply_subtract_fusion
  575.4 1.3 convolution_bitcast_fusion.2
  576.7 1.6 convolution_bitcast_fusion
  578.3 1.4 fusion.13
  579.6 0.7 fusion.473
  581.1 0.6 constant_dynamic-update-slice_fusion.6
  583.0 1.5 fusion.15
  584.5 0.7 fusion.474
  596.9 0.7 fusion.471
  597.6 0.7 fusion.472
  624.7 0.7 constant_dynamic-update-slice_fusion.5
  625.4 0.7 constant_dynamic-update-slice_fusion.4
  626.7 0.7 constant_dynamic-update-slice_fusion.3
  628.0 0.7 constant_dynamic-update-slice_fusion.8
  628.7 0.7 constant_dynamic-update-slice_fusion.7
  629.4 0.8 fusion.190
  631.0 1.0 fusion.189
  634.4 1.1 fusion.64
  636.3 2.2 pad_maximum_fusion.3
  638.5 1.3 copy.195
  639.8 1.3 copy.194
  641.0 0.9 pad_maximum_fusion
  642.3 0.8 fusion.34
  (100 shorter events, 31.2 us)
Async XLA Ops:
  7.2 6.7 %copy-start = (f32[1,1,2,8]{3,2,1,0:T(2,128)S(1)}, f32[1,1,2,8]{3,2,1,0:T(2,128)}, u32[]{:S(2)}) copy-start(f32[1,1,2,8]{3,2,1,0:T(2,128)} %param.9) | copy-start | bytes 196
  7.2 10.3 %copy-start.4 = (f32[2,2,128,128]{3,2,1,0:T(8,128)S(1)}, f32[2,2,128,128]{3,2,1,0:T(8,128)}, u32[]{:S(2)}) copy-start(f32[2,2,128,128]{3,2,1,0:T(8,128)} %param.6) | copy-start | bytes 786436
  7.2 566.7 %all-reduce.4.cloned.1.call-start = ((), (), s32[]{:S(2)}) async-start(), calls=%async_computation | async-start | bytes 2097152 | tf_op jit(solution)/shard_map/psum | solution.py:208
  8.3 9.2 %collective-permute-start = (f32[2,2,64,128]{3,2,1,0:T(8,128)S(1)}, f32[2,2,64,128]{3,2,1,0:T(8,128)S(1)}, u32[]{:S(2)}, u32[]{:S(2)}) collective-permute-start(f32[2,2,64,128]{3,2,1,0:T(8,128)S(1)} %get-tuple-element.45), channel_id=1, source_target_pairs={{0,32},{32,64},{64,96},{96,128},{128,160},{160,192},{192,224},{224... | collective-permute-start | bytes 393224 | tf_op jit(solution)/shard_map/ppermute | solution.py:18
  12.2 5.7 collective-permute-start.1
  13.9 21.7 %copy-start.6 = (s32[1,1,2,2]{3,2,1,0:T(2,128)S(1)}, s32[1,1,2,2]{3,2,1,0:T(2,128)}, u32[]{:S(2)}) copy-start(s32[1,1,2,2]{3,2,1,0:T(2,128)} %param.10) | copy-start | bytes 52
  18.9 24.8 %collective-permute-start.3 = (f32[2,2,256,64]{3,2,1,0:T(8,128)}, f32[2,2,256,64]{3,2,1,0:T(8,128)S(1)}, u32[]{:S(2)}, u32[]{:S(2)}) collective-permute-start(f32[2,2,256,64]{3,2,1,0:T(8,128)} %get-tuple-element.37), channel_id=1, source_target_pairs={{1,0},{2,1},{3,2},{4,3},{5,4},{6,5},{7,6},{8,7},{9,8},{10,9},{11,1... | collective-permute-start | bytes 786440 | tf_op jit(solution)/shard_map/ppermute | solution.py:21
  33.4 10.2 %collective-permute-start.2 = (f32[2,2,256,64]{3,2,1,0:T(8,128)S(1)}, f32[2,2,256,64]{3,2,1,0:T(8,128)S(1)}, u32[]{:S(2)}, u32[]{:S(2)}) collective-permute-start(f32[2,2,256,64]{3,2,1,0:T(8,128)S(1)} %get-tuple-element.36), channel_id=1, source_target_pairs={{0,1},{1,2},{2,3},{3,4},{4,5},{5,6},{6,7},{7,8},{8,9},{9,10},{10,1... | collective-permute-start | bytes 786440 | tf_op jit(solution)/shard_map/ppermute | solution.py:18
  52.9 5.0 copy-start.8
  79.0 9.3 %collective-permute-start.5 = (f32[2,2,64,256]{3,2,1,0:T(8,128)S(1)}, f32[2,2,64,256]{3,2,1,0:T(8,128)S(1)}, u32[]{:S(2)}, u32[]{:S(2)}) collective-permute-start(f32[2,2,64,256]{3,2,1,0:T(8,128)S(1)} %get-tuple-element.25), channel_id=1, source_target_pairs={{32,0},{64,32},{96,64},{128,96},{160,128},{192,160},{224,192},{256... | collective-permute-start | bytes 786440 | tf_op jit(solution)/shard_map/ppermute | solution.py:21
  80.3 8.9 %collective-permute-start.4 = (f32[2,2,64,256]{3,2,1,0:T(8,128)S(1)}, f32[2,2,64,256]{3,2,1,0:T(8,128)S(1)}, u32[]{:S(2)}, u32[]{:S(2)}) collective-permute-start(f32[2,2,64,256]{3,2,1,0:T(8,128)S(1)} %get-tuple-element.24), channel_id=1, source_target_pairs={{0,32},{32,64},{64,96},{96,128},{128,160},{160,192},{192,224},{224... | collective-permute-start | bytes 786440 | tf_op jit(solution)/shard_map/ppermute | solution.py:18
  89.2 0.7 copy-start.2
  90.0 483.8 %copy-start.1 = (f32[8,2,128,128]{3,2,1,0:T(8,128)S(1)}, f32[8,2,128,128]{3,2,1,0:T(8,128)}, u32[]{:S(2)}) copy-start(f32[8,2,128,128]{3,2,1,0:T(8,128)} %param.8) | copy-start | bytes 3145732
  93.3 545.2 %collective-permute-start.7 = (f32[2,2,384,64]{2,3,1,0:T(8,128)}, f32[2,2,384,64]{2,3,1,0:T(8,128)}, u32[]{:S(2)}, u32[]{:S(2)}) collective-permute-start(f32[2,2,384,64]{2,3,1,0:T(8,128)} %copy.193), channel_id=1, source_target_pairs={{1,0},{2,1},{3,2},{4,3},{5,4},{6,5},{7,6},{8,7},{9,8},{10,9},{11,1... | collective-permute-start | bytes 1179656 | tf_op jit(solution)/shard_map/ppermute | solution.py:21
  97.8 541.9 %collective-permute-start.6 = (f32[2,2,384,64]{2,3,1,0:T(8,128)}, f32[2,2,384,64]{2,3,1,0:T(8,128)}, u32[]{:S(2)}, u32[]{:S(2)}) collective-permute-start(f32[2,2,384,64]{2,3,1,0:T(8,128)} %copy.192), channel_id=1, source_target_pairs={{0,1},{1,2},{2,3},{3,4},{4,5},{5,6},{6,7},{7,8},{8,9},{9,10},{10,1... | collective-permute-start | bytes 1179656 | tf_op jit(solution)/shard_map/ppermute | solution.py:18
  627.4 6.6 %copy-start.5 = (f32[8,1,128,128]{3,2,1,0:T(8,128)S(1)}, f32[8,1,128,128]{3,2,1,0:T(8,128)}, u32[]{:S(2)}) copy-start(f32[8,1,128,128]{3,2,1,0:T(8,128)} %get-tuple-element.6) | copy-start | bytes 1572868
  636.3 4.7 copy-start.3
  641.0 0.9 copy-start.7
Sparse Core Ops, SparseCore 0:
  86.8 487.0 all-reduce.3
where the time goes:
time: 654 us; the launch traced here: 650 us
  waiting for transfers between devices  477 us (73%)
  between operations  65.2 us (10%)
  matrix products  36.9 us (6%)
  starting transfers between devices  32.8 us (5%)
  local copies, waits for them, and re-layouts  23.4 us (4%)
  other arithmetic  15 us (2%)
    psum x1, waiting for transfers between devices, local(): summed = lax.psum(local_term, ('sy', 'sx'))  474 us
    ppermute x4, starting transfers between devices, padded(): lax.ppermute(lax.slice_in_dim(block, 0, width, axis=dim), axis, backward)  20.6 us
    dot_general x24, matrix products, left_product(): return jnp.einsum('ij,pjk->pik', table, values, precision=HIGHEST)  13.7 us
    dot_general x24, matrix products, right_product(): return jnp.einsum('pij,jk->pik', values, table, precision=HIGHEST)  13.6 us
  transfers between devices with their start and end apart: 9, of which 4 were waited for; matrix products, arithmetic and copies ran while one was open for 5% of the time, Pallas kernels for 0%

commit v1 on v0

v1 whole, which is shorter than its diff:
```python
import math

import jax
import jax.numpy as jnp
import numpy as np
from jax import lax
from jax.experimental import pallas as pl
from jax.experimental.pallas import tpu as pltpu
from jax.sharding import PartitionSpec as P

FLOOR = 0.5
PHASE_EDGE = 3.0
VMEM_BYTES = 40 * 1024 * 1024


def block_form(matrix):
    real, imag = matrix.real, matrix.imag
    return np.block([[real, -imag], [imag, real]])


def split_table(values):
    whole = values.astype(np.float32)
    high = whole.astype(jnp.bfloat16)
    low = (whole - high.astype(np.float32)).astype(jnp.bfloat16)
    return (high, low)


def tables(probe_len):
    indices = np.arange(probe_len)
    dft = np.exp(-2j * np.pi * (np.outer(indices, indices) % probe_len) / probe_len)
    dft = dft / math.sqrt(probe_len)
    half = probe_len // 2
    frequency = ((indices + half) % probe_len - half) / half
    phase = np.exp(-1j * PHASE_EDGE * frequency * frequency)
    move = np.conj(dft) @ (phase[:, None] * dft)
    forms = (block_form(dft), block_form(dft).T, block_form(move), block_form(move).T)
    parts = [split_table(form) for form in forms]
    return np.stack([np.stack(pair) for pair in parts])


def dot3(left, right):
    left_high, left_low = left
    right_high, right_low = right
    total = jnp.dot(left_high, right_low, preferred_element_type=jnp.float32)
    total = total + jnp.dot(left_low, right_high, preferred_element_type=jnp.float32)
    return total + jnp.dot(left_high, right_high, preferred_element_type=jnp.float32)


def halves(values):
    high = values.astype(jnp.bfloat16)
    low = (values - high.astype(jnp.float32)).astype(jnp.bfloat16)
    return (high, low)


def both_sides(fields, left_table, right_table):
    (real0, imag0), (real1, imag1) = fields
    n = real0.shape[0]
    upright = jnp.concatenate(
        [jnp.concatenate([real0, real1], axis=1), jnp.concatenate([imag0, imag1], axis=1)], axis=0
    )
    upright = dot3(left_table, halves(upright))
    top, bottom = upright[:n], upright[n:]
    wide = jnp.concatenate(
        [
            jnp.concatenate([top[:, :n], bottom[:, :n]], axis=1),
            jnp.concatenate([top[:, n:], bottom[:, n:]], axis=1),
        ],
        axis=0,
    )
    wide = dot3(halves(wide), right_table)
    return [(wide[:n, :n], wide[:n, n:]), (wide[n:, :n], wide[n:, n:])]


def model_kernel(
    positions, weights, own, beside, above, below, mean, basis, measured, table,
    grad_above, grad_own, grad_below, probe_grad, frame, grads,
):
    n = mean.shape[-1]
    half = n // 2
    modes = basis.shape[0]
    frame[:, 0:half, :] = above[...]
    frame[:, half : half + n, 0:n] = own[...]
    frame[:, half : half + n, n : 2 * n] = beside[...]
    frame[:, half + n : 2 * n, :] = below[...]
    grads[...] = jnp.zeros(grads.shape, jnp.float32)
    dft, dft_t, move, move_t = [(table[at, 0], table[at, 1]) for at in range(4)]
    slots = range(2)
    rows = [positions[slot, 0] for slot in slots]
    offsets = [row & 7 for row in rows]
    bases = [pl.multiple_of(row - offset, 8) for row, offset in zip(rows, offsets)]
    tall = n + 8
    cols = [positions[slot, 1] for slot in slots]

    def window(slot, plane):
        strip = frame[plane, pl.ds(bases[slot], tall), :]
        strip = pltpu.roll(strip, (5 * half - cols[slot]) & (2 * n - 1), 1)[:, :n]
        shift = jnp.where(offsets[slot] == 0, 0, tall - offsets[slot])
        return pltpu.roll(strip, shift, 0)[:n]

    transmit = [
        [(1.0 + window(slot, 2 * layer), window(slot, 2 * layer + 1)) for slot in slots]
        for layer in range(2)
    ]
    probes = []
    for slot in slots:
        real = mean[0]
        imag = mean[1]
        for mode in range(modes):
            real = real + weights[slot, mode] * basis[mode, 0]
            imag = imag + weights[slot, mode] * basis[mode, 1]
        probes.append((real, imag))

    def times(first, second):
        return [(a * c - b * d, a * d + b * c) for (a, b), (c, d) in zip(first, second)]

    def conj_times(first, second):
        return [(a * c + b * d, a * d - b * c) for (a, b), (c, d) in zip(first, second)]

    entered = both_sides(times(probes, transmit[0]), move, move_t)
    far = both_sides(times(entered, transmit[1]), dft, dft_t)
    chi = []
    for slot in slots:
        real, imag = far[slot]
        modulus = jnp.maximum(jnp.sqrt(real * real + imag * imag), FLOOR)
        ratio = measured[slot] / modulus
        chi.append((real - real * ratio, imag - imag * ratio))
    back = both_sides(chi, dft_t, dft)

    def deposit(layer, terms):
        for slot in slots:
            for part in range(2):
                padded = jnp.concatenate(
                    [terms[slot][part], jnp.zeros((8, n), jnp.float32)], axis=0
                )
                lowered = pltpu.roll(padded, offsets[slot], 0)
                padded = jnp.concatenate(
                    [lowered, jnp.zeros((tall, n), jnp.float32)], axis=1
                )
                shifted = pltpu.roll(padded, (cols[slot] + 3 * half) & (2 * n - 1), 1)
                at = (2 * layer + part, pl.ds(bases[slot], tall), slice(None))
                grads[at] = grads[at] + shifted

    deposit(1, conj_times(entered, back))
    back = both_sides(conj_times(transmit[1], back), move_t, move)
    deposit(0, conj_times(probes, back))
    back = conj_times(transmit[0], back)
    blocks = n // 8
    for slot in slots:
        for part in range(2):
            piece = back[slot][part].reshape(blocks, 8, n)
            probe_grad[part * blocks : (part + 1) * blocks, slot] = piece
    grad_above[...] = grads[:, 0:half, :]
    grad_own[...] = grads[:, half : half + n, :]
    grad_below[...] = grads[:, half + n : 2 * n, :]


def mix_kernel(weights, gathered, mixed):
    count, per_tile = gathered.shape[0], gathered.shape[1]
    modes = mixed.shape[0]
    totals = [jnp.zeros(mixed.shape[1:], jnp.float32) for mode in range(modes)]
    for source in range(count):
        for slot in range(per_tile):
            term = gathered[source, slot]
            for mode in range(modes):
                totals[mode] = totals[mode] + weights[source, slot * modes + mode] * term
    for mode in range(modes):
        mixed[mode] = totals[mode]


def ortho_kernel(core, mine, other, basis, out, step_len=None):
    modes, blocks = out.shape[0], out.shape[1]
    part_len = blocks // 2
    some = modes // 2
    pixels = part_len * out.shape[2] * out.shape[3]
    my_base = core[0] * some
    other_base = some - my_base
    for mode in range(some):
        at = my_base + mode
        out[at] = basis[at] - step_len * mine[:, mode]
        at = other_base + mode
        out[at] = basis[at] - step_len * other[:, mode]

    def total(values):
        return jnp.sum(jnp.sum(values, axis=0), axis=(0, 1), keepdims=True)

    for mode in range(modes):
        real = out[mode, 0:part_len]
        imag = out[mode, part_len:blocks]
        norm = total(real * real + imag * imag)
        for later in range(mode + 1, modes):
            later_real = out[later, 0:part_len]
            later_imag = out[later, part_len:blocks]
            factor_real = (total(real * later_real + imag * later_imag) / norm)[None]
            factor_imag = (total(real * later_imag - imag * later_real) / norm)[None]
            out[later, 0:part_len] = later_real - (factor_real * real - factor_imag * imag)
            out[later, part_len:blocks] = later_imag - (factor_real * imag + factor_imag * real)
        scale = (1.0 / jnp.sqrt(norm / pixels))[None]
        out[mode, 0:part_len] = real * scale
        out[mode, part_len:blocks] = imag * scale


def shift_pairs(count):
    forward = [(at, at + 1) for at in range(count - 1)]
    return forward, [(target, source) for source, target in forward]


def exchange(values, axis, groups=None):
    return lax.all_to_all(values, axis, 0, 0, tiled=True, axis_index_groups=groups)


def to_all(values, axis, count, groups=None):
    repeated = jnp.broadcast_to(values[None], (count,) + values.shape)
    return exchange(repeated, axis, groups)


def vmem_specs(count):
    return [pl.BlockSpec(memory_space=pltpu.VMEM)] * count


def local(obj_delta, probe_mean, probe_basis, mode_weights, positions, amplitudes):
    n = probe_mean.shape[-1]
    half = n // 2
    modes = probe_basis.shape[0]
    per_tile = positions.shape[2]
    count_y, count_x = lax.axis_size("sy"), lax.axis_size("sx")
    forward_y, backward_y = shift_pairs(count_y)
    forward_x, backward_x = shift_pairs(count_x)
    planes = obj_delta.shape[0] * obj_delta.shape[1]
    blocks = n // 8
    params = pltpu.CompilerParams(vmem_limit_bytes=VMEM_BYTES)
    smem = pl.BlockSpec(memory_space=pltpu.SMEM)
    weights = mode_weights[0, 0]

    own = obj_delta.reshape(planes, n, n)
    left = lax.ppermute(own, "sx", forward_x)
    right = lax.ppermute(own, "sx", backward_x)
    near = lax.broadcasted_iota(jnp.int32, (1, 1, n), 2) < half
    beside = jnp.where(near, right, left)
    strip = jnp.concatenate([own, beside], axis=2)
    above = lax.ppermute(strip[:, half:], "sy", forward_y)
    below = lax.ppermute(strip[:, :half], "sy", backward_y)

    flat_weights = jnp.pad(weights.reshape(1, per_tile * modes), ((0, 0), (0, 128 - per_tile * modes)))
    all_weights = to_all(flat_weights, "sy", count_y).reshape(count_y, 128)

    f32 = jnp.float32
    grad_above, grad_own, grad_below, probe_grad = pl.pallas_call(
        model_kernel,
        out_shape=(
            jax.ShapeDtypeStruct((planes, half, 2 * n), f32),
            jax.ShapeDtypeStruct((planes, n, 2 * n), f32),
            jax.ShapeDtypeStruct((planes, half, 2 * n), f32),
            jax.ShapeDtypeStruct((2 * blocks, per_tile, 8, n), f32),
        ),
        in_specs=[smem, smem] + vmem_specs(8),
        out_specs=tuple(vmem_specs(4)),
        scratch_shapes=[pltpu.VMEM((planes, 2 * n, 2 * n), f32)] * 2,
        compiler_params=params,
        name="model",
    )(
        positions[0, 0], weights, own, beside, above, below, probe_mean, probe_basis,
        amplitudes[0, 0], jnp.asarray(tables(n)),
    )

    gathered = exchange(probe_grad, "sy")
    mixed = pl.pallas_call(
        mix_kernel,
        out_shape=jax.ShapeDtypeStruct((modes, 8, n), f32),
        in_specs=[smem] + vmem_specs(1),
        out_specs=vmem_specs(1)[0],
        compiler_params=params,
        name="mix",
    )(all_weights, gathered)

    cores = 2
    per_core = count_x // cores
    pairs = [[cores * at + core for core in range(cores)] for at in range(per_core)]
    columns = [[cores * at + core for at in range(per_core)] for core in range(cores)]
    some = modes // cores
    mine = exchange(mixed, "sx", pairs).reshape(cores, some, 8, n).sum(axis=0)
    mine = to_all(mine, "sx", per_core, columns).sum(axis=0)
    mine = to_all(mine, "sy", count_y)
    swap = [(at, at ^ 1) for at in range(count_x)]
    other = lax.ppermute(mine, "sx", swap)
    core = (lax.axis_index("sx") % cores).astype(jnp.int32).reshape(1)
    count_all = per_tile * count_y * count_x
    step_len = 1.0 / math.sqrt(count_all)

    def final_kernel(*refs):
        ortho_kernel(*refs, step_len=step_len)

    new_basis = pl.pallas_call(
        final_kernel,
        out_shape=jax.ShapeDtypeStruct((modes, 2 * blocks, 8, n), f32),
        in_specs=[smem] + vmem_specs(3),
        out_specs=vmem_specs(1)[0],
        compiler_params=params,
        name="orthonormal",
    )(core, mine, other, probe_basis.reshape(modes, 2 * blocks, 8, n))
    new_basis = new_basis.reshape(probe_basis.shape)

    from_below = lax.ppermute(grad_above, "sy", backward_y)
    from_above = lax.ppermute(grad_below, "sy", forward_y)
    joined = grad_own + jnp.concatenate([from_above, from_below], axis=1)
    outer = joined[:, :, n:]
    from_left = lax.ppermute(outer, "sx", forward_x)
    from_right = lax.ppermute(outer, "sx", backward_x)
    obj_grad = joined[:, :, :n] + jnp.where(near, from_left, from_right)
    return (obj_grad.reshape(obj_delta.shape), new_basis)


def solution(mesh):
    placed = (
        P(None, None, "sy", "sx"),
        P(),
        P(),
        P("sy", "sx", None, None),
        P("sy", "sx", None, None),
        P("sy", "sx", None, None, None),
    )
    return jax.shard_map(
        local,
        mesh=mesh,
        in_specs=placed,
        out_specs=(P(None, None, "sy", "sx"), P()),
        check_vma=False,
    )
```

time: 654 us -> 143 us (0.22)
  waiting for transfers between devices: 477 us -> 15.3 us
  between operations: 65.2 us -> 0.92 us
  blocking collectives: 0 us -> 55.8 us
  matrix products: 36.9 us -> 0 us
  starting transfers between devices: 32.8 us -> 55 us
  local copies, waits for them, and re-layouts: 23.4 us -> 4.19 us
  other arithmetic: 15 us -> 2.89 us
  Pallas kernels: 0 us -> 7.97 us
    psum x1 -> x0, waiting for transfers between devices: 474 us -> none  [local(): summed = lax.psum(local_term, ('sy', 'sx'))]
    all_to_all x0 -> x3, blocking collectives: none -> 55.8 us  [exchange(): lax.all_to_all(values, axis, 0, 0, tiled=True, axis_index_groups=groups)]
    dot_general x54 -> x0, matrix products: 36.9 us -> none  [the longest x24 13.7 us: left_product(): return jnp.einsum('ij,pjk->pik', table, values, precision=HIGHEST)]
    ppermute x8 -> x9, starting transfers between devices: 32.7 us -> 44.9 us  [the longest x1 12 us: local(): right = lax.ppermute(own, 'sx', backward_x)]
    all_to_all x0 -> x2, waiting for transfers between devices: none -> 10.7 us  [exchange(): lax.all_to_all(values, axis, 0, 0, tiled=True, axis_index_groups=groups)]
    all_to_all x0 -> x2, starting transfers between devices: none -> 10.1 us  [exchange(): lax.all_to_all(values, axis, 0, 0, tiled=True, axis_index_groups=groups)]
    slice x13 -> x1, local copies, waits for them, and re-layouts: 9.88 us -> 0.02 us  [local(): outer = joined[:, :, n:]]
    pallas_call x0 -> x3, Pallas kernels: none -> 7.97 us  [the longest x1 3.78 us: local(): pl.pallas_call(model_kernel, out_shape=(jax.ShapeDtypeStruct((planes, hal...]
  transfers between devices with their start and end apart: 9 -> 11, of which waited for: 4 -> 5; matrix products, arithmetic and copies ran while one was open for 5% -> 2% of each run, Pallas kernels for 0% -> 3%
where the time goes in v1:
time: 143 us; the launch traced here: 142 us
  blocking collectives  55.8 us (39%)
  starting transfers between devices  55 us (38%)
  waiting for transfers between devices  15.3 us (11%)
  Pallas kernels  7.97 us (6%)
  local copies, waits for them, and re-layouts  4.19 us (3%)
  other arithmetic  2.89 us (2%)
    all_to_all x3, blocking collectives, exchange(): lax.all_to_all(values, axis, 0, 0, tiled=True, axis_index_groups=groups)  55.8 us
    ppermute x1, starting transfers between devices, local(): right = lax.ppermute(own, 'sx', backward_x)  12 us
    ppermute x1, starting transfers between devices, local(): other = lax.ppermute(mine, 'sx', swap)  10.8 us
    all_to_all x2, waiting for transfers between devices, exchange(): lax.all_to_all(values, axis, 0, 0, tiled=True, axis_index_groups=groups)  10.7 us
    all_to_all x2, starting transfers between devices, exchange(): lax.all_to_all(values, axis, 0, 0, tiled=True, axis_index_groups=groups)  10.1 us
    ppermute x1, starting transfers between devices, local(): left = lax.ppermute(own, 'sx', forward_x)  5.52 us
    ppermute x1, starting transfers between devices, local(): from_left = lax.ppermute(outer, 'sx', forward_x)  5.09 us
    ppermute x1, starting transfers between devices, local(): above = lax.ppermute(strip[:, half:], 'sy', forward_y)  4 us
  transfers between devices with their start and end apart: 11, of which 5 were waited for; matrix products, arithmetic and copies ran while one was open for 2% of the time, Pallas kernels for 3%

profile of v1, /device:TPU:1, one launch (start us, length us, event | category | flops | bytes accessed | tf_op | source)
XLA Modules:
  0.0 142.1 jit_solution(15258408948629569646)
XLA Ops:
  0.6 0.0 copy-start
  0.6 5.5 %collective-permute-start.1 = (f32[4,128,128]{2,1,0:T(8,128)}, f32[4,128,128]{2,1,0:T(8,128)S(1)}, u32[]{:S(2)}, u32[]{:S(2)}) collective-permute-start(f32[4,128,128]{2,1,0:T(8,128)} %bitcast.13), channel_id=1, source_target_pairs={{0,1},{1,2},{2,3},{3,4},{4,5},{5,6},{6,7},{7,8},{8,9},{9,10},{10,1... | collective-permute-start | bytes 786440 | tf_op jit(solution)/shard_map/ppermute | solution.py:235
  6.2 12.0 %collective-permute-start = (f32[4,128,128]{2,1,0:T(8,128)}, f32[4,128,128]{2,1,0:T(8,128)S(1)}, u32[]{:S(2)}, u32[]{:S(2)}) collective-permute-start(f32[4,128,128]{2,1,0:T(8,128)} %bitcast.14), channel_id=1, source_target_pairs={{1,0},{2,1},{3,2},{4,3},{5,4},{6,5},{7,6},{8,7},{9,8},{10,9},{11,1... | collective-permute-start | bytes 786440 | tf_op jit(solution)/shard_map/ppermute | solution.py:236
  18.2 0.0 collective-permute-done.1
  18.2 1.3 collective-permute-done
  19.5 0.0 copy-start.2
  19.6 0.0 copy-start.3
  19.6 0.0 copy-start.4
  19.6 1.1 pad_maximum_fusion
  20.6 0.0 copy-start.6
  20.7 1.3 collective-permute-start.3
  22.0 4.0 %collective-permute-start.2 = (f32[4,64,256]{2,1,0:T(8,128)S(1)}, f32[4,64,256]{2,1,0:T(8,128)S(1)}, u32[]{:S(2)}, u32[]{:S(2)}) collective-permute-start(f32[4,64,256]{2,1,0:T(8,128)S(1)} %get-tuple-element.11), channel_id=1, source_target_pairs={{0,32},{32,64},{64,96},{96,128},{128,160},{160,192},{192,224},{224... | collective-permute-start | bytes 786440 | tf_op jit(solution)/shard_map/ppermute | solution.py:240
  26.0 0.0 copy-done.6
  26.0 0.1 reshape_squeeze.3
  26.1 0.6 broadcast_in_dim.35
  26.7 6.1 %all-to-all-start = ((f32[32,1,128]{2,1,0:T(1,128)}), f32[32,1,128]{2,1,0:T(1,128)S(1)}, u32[]{:S(2)}, u32[]{:S(2)}) async-start(f32[32,1,128]{2,1,0:T(1,128)} %broadcast_in_dim.35), calls=%async_computation | async-start | bytes 32768 | tf_op jit(solution)/shard_map/all_to_all | solution.py:208
  32.8 0.0 collective-permute-done.3.below
  32.8 0.0 collective-permute-done.2.above
  32.8 0.0 copy-start.5
  32.8 0.0 copy-done
  32.8 0.0 copy-done.2
  32.8 0.0 copy-done.3
  32.8 0.6 copy-done.5
  33.5 1.2 copy-done.1
  34.7 3.8 %model.1 = (f32[4,64,256]{2,1,0:T(8,128)S(1)}, f32[4,128,256]{2,1,0:T(8,128)S(1)}, f32[4,64,256]{2,1,0:T(8,128)S(1)}, f32[32,2,8,128]{3,2,1,0:T(8,128)S(1)}) custom-call(s32[2,2]{1,0:T(2,128)S(1)} %bitcast.19, f32[2,8]{1,0:T(2,128)S(1)} %bitcast.20, f32[4,128,128]{2,1,0:T(8,128)S(1)} %bitcast.16, f32[4,128,128]{2,1,0:T(8,128)S(1)} %broadcast_select_fusion.beside, ...), custom_call_target="tpu_custom_call" | custom-call | tf_op jit(solution)/shard_map/model/pallas_call | solution.py:247
  38.5 0.0 copy-start.7
  38.5 0.7 copy-done.7
  39.2 2.1 %all-to-all-done = f32[32,1,128]{2,1,0:T(1,128)S(1)} async-done(((f32[32,1,128]{2,1,0:T(1,128)}), f32[32,1,128]{2,1,0:T(1,128)S(1)}, u32[]{:S(2)}, u32[]{:S(2)}) %all-to-all-start) | async-done | bytes 16416 | tf_op jit(solution)/shard_map/all_to_all | solution.py:208
  41.3 19.5 %all_to_all.25.gathered = f32[32,2,8,128]{3,2,1,0:T(8,128)S(1)} all-to-all(f32[32,2,8,128]{3,2,1,0:T(8,128)S(1)} %get-tuple-element.9), channel_id=1, replica_groups=mesh['sy'=32,'sx'=32] {'sy'}, dimensions={0} | all-to-all | bytes 524288 | tf_op jit(solution)/shard_map/all_to_all | solution.py:208
  60.8 1.0 mix.1
  61.8 3.8 %all_to_all.26 = f32[8,8,128]{2,1,0:T(8,128)S(1)} all-to-all(f32[8,8,128]{2,1,0:T(8,128)S(1)} %mix.1), channel_id=1, replica_groups={{0,1},{2,3},{4,5},{6,7},{8,9},{10,11},{12,13},{14,15},{16,17},{18,19},{..., dimensions={0} | all-to-all | bytes 65536 | tf_op jit(solution)/shard_map/all_to_all | solution.py:208
  65.7 32.5 %all_to_all.27 = f32[16,4,8,128]{3,2,1,0:T(8,128)S(1)} all-to-all(f32[16,4,8,128]{3,2,1,0:T(8,128)S(1)} %broadcast_in_dim.36), channel_id=1, replica_groups={{0,2,4,6,8,10,12,14,16,18,20,22,24,26,28,30},{1,3,5,7,9,11,13,15,17,19,..., dimensions={0} | all-to-all | bytes 524288 | tf_op jit(solution)/shard_map/all_to_all | solution.py:208
  98.2 0.9 broadcast_in_dim.37
  99.0 4.0 %all-to-all-start.4 = ((f32[32,4,8,128]{3,2,1,0:T(8,128)}), f32[32,4,8,128]{3,2,1,0:T(8,128)S(1)}, u32[]{:S(2)}, u32[]{:S(2)}) async-start(f32[32,4,8,128]{3,2,1,0:T(8,128)} %broadcast_in_dim.37), calls=%async_computation.4 | async-start | bytes 1048576 | tf_op jit(solution)/shard_map/all_to_all | solution.py:208
  103.1 3.0 %collective-permute-start.4 = (f32[4,64,256]{2,1,0:T(8,128)S(1)}, f32[4,64,256]{2,1,0:T(8,128)S(1)}, u32[]{:S(2)}, u32[]{:S(2)}) collective-permute-start(f32[4,64,256]{2,1,0:T(8,128)S(1)} %copy-done.8), channel_id=1, source_target_pairs={{0,32},{32,64},{64,96},{96,128},{128,160},{160,192},{192,224},{224... | collective-permute-start | bytes 786440 | tf_op jit(solution)/shard_map/ppermute | solution.py:303
  106.1 1.3 collective-permute-start.5
  107.4 8.6 %all-to-all-done.4.refs_1_ = f32[32,4,8,128]{3,2,1,0:T(8,128)S(1)} async-done(((f32[32,4,8,128]{3,2,1,0:T(8,128)}), f32[32,4,8,128]{3,2,1,0:T(8,128)S(1)}, u32[]{:S(2)}, u32[]{:S(2)}) %all-to-all-start.4) | async-done | bytes 524320 | tf_op jit(solution)/shard_map/all_to_all | solution.py:208
  116.0 10.8 %collective-permute-start.8 = (f32[32,4,8,128]{3,2,1,0:T(8,128)S(1)}, f32[32,4,8,128]{3,2,1,0:T(8,128)S(1)}, u32[]{:S(2)}, u32[]{:S(2)}) collective-permute-start(f32[32,4,8,128]{3,2,1,0:T(8,128)S(1)} %all-to-all-done.4.refs_1_), channel_id=1, source_target_pairs={{0,1},{1,0},{2,3},{3,2},{4,5},{5,4},{6,7},{7,6},{8,9},{9,8},{10,11... | collective-permute-start | bytes 1572872 | tf_op jit(solution)/shard_map/ppermute | solution.py:284
  126.8 0.0 collective-permute-done.4
  126.8 0.0 collective-permute-done.5
  126.8 1.0 maximum_add_fusion
  127.9 1.9 %collective-permute-start.7 = (f32[4,128,128]{2,1,0:T(8,128)S(1)}, f32[4,128,128]{2,1,0:T(8,128)S(1)}, u32[]{:S(2)}, u32[]{:S(2)}) collective-permute-start(f32[4,128,128]{2,1,0:T(8,128)S(1)} %slice.19), channel_id=1, source_target_pairs={{1,0},{2,1},{3,2},{4,3},{5,4},{6,5},{7,6},{8,7},{9,8},{10,9},{11,1... | collective-permute-start | bytes 786440 | tf_op jit(solution)/shard_map/ppermute | solution.py:307
  129.8 5.1 %collective-permute-start.6 = (f32[4,128,128]{2,1,0:T(8,128)S(1)}, f32[4,128,128]{2,1,0:T(8,128)S(1)}, u32[]{:S(2)}, u32[]{:S(2)}) collective-permute-start(f32[4,128,128]{2,1,0:T(8,128)S(1)} %slice.19), channel_id=1, source_target_pairs={{0,1},{1,2},{2,3},{3,4},{4,5},{5,6},{6,7},{7,8},{8,9},{9,10},{10,1... | collective-permute-start | bytes 786440 | tf_op jit(solution)/shard_map/ppermute | solution.py:306
  134.9 2.1 %collective-permute-done.7 = f32[4,128,128]{2,1,0:T(8,128)S(1)} collective-permute-done((f32[4,128,128]{2,1,0:T(8,128)S(1)}, f32[4,128,128]{2,1,0:T(8,128)S(1)}, u32[]{:S(2)}, u32[]{:S(2)}) %collective-permute-start.7) | collective-permute-done | bytes 262176 | tf_op jit(solution)/shard_map/ppermute | solution.py:307
  137.0 1.2 collective-permute-done.6
  138.2 0.7 slice_add_fusion
  139.0 0.0 collective-permute-done.8.refs_2_
  139.0 3.2 %orthonormal.1 = f32[8,32,8,128]{3,2,1,0:T(8,128)} custom-call(s32[1]{0:T(128)} %bitcast.5.refs_0_, f32[32,4,8,128]{3,2,1,0:T(8,128)S(1)} %all-to-all-done.4.refs_1_, f32[32,4,8,128]{3,2,1,0:T(8,128)S(1)} %collective-permute-done.8.refs_2_, f32[8,32,8,128]{3,2,1,0:T(8,128)S(1)} %bitcast.12), custom_call_target="tpu_custom_call" | custom-call | tf_op jit(solution)/shard_map/orthonormal/pallas_call | solution.py:292
  (11 shorter events, 0.1 us)
Async XLA Ops:
  0.6 32.2 %copy-start = (f32[8,2,128,128]{3,2,1,0:T(8,128)S(1)}, f32[8,2,128,128]{3,2,1,0:T(8,128)}, u32[]{:S(2)}) copy-start(f32[8,2,128,128]{3,2,1,0:T(8,128)} %basis.1) | copy-start | bytes 3145732
  0.6 17.5 %collective-permute-start.1 = (f32[4,128,128]{2,1,0:T(8,128)}, f32[4,128,128]{2,1,0:T(8,128)S(1)}, u32[]{:S(2)}, u32[]{:S(2)}) collective-permute-start(f32[4,128,128]{2,1,0:T(8,128)} %bitcast.13), channel_id=1, source_target_pairs={{0,1},{1,2},{2,3},{3,4},{4,5},{5,6},{6,7},{7,8},{8,9},{9,10},{10,1... | collective-permute-start | bytes 786440 | tf_op jit(solution)/shard_map/ppermute | solution.py:235
  6.2 13.3 %collective-permute-start = (f32[4,128,128]{2,1,0:T(8,128)}, f32[4,128,128]{2,1,0:T(8,128)S(1)}, u32[]{:S(2)}, u32[]{:S(2)}) collective-permute-start(f32[4,128,128]{2,1,0:T(8,128)} %bitcast.14), channel_id=1, source_target_pairs={{1,0},{2,1},{3,2},{4,3},{5,4},{6,5},{7,6},{8,7},{9,8},{10,9},{11,1... | collective-permute-start | bytes 786440 | tf_op jit(solution)/shard_map/ppermute | solution.py:236
  19.5 13.3 %copy-start.2 = (f32[2,2,128,128]{3,2,1,0:T(8,128)S(1)}, f32[2,2,128,128]{3,2,1,0:T(8,128)}, u32[]{:S(2)}) copy-start(f32[2,2,128,128]{3,2,1,0:T(8,128)} %param.7) | copy-start | bytes 786436
  19.6 13.3 %copy-start.3 = (f32[2,128,128]{2,1,0:T(8,128)S(1)}, f32[2,128,128]{2,1,0:T(8,128)}, u32[]{:S(2)}) copy-start(f32[2,128,128]{2,1,0:T(8,128)} %mean.1) | copy-start | bytes 393220
  19.6 13.3 %copy-start.4 = (f32[1,1,2,128,128]{4,3,2,1,0:T(8,128)S(1)}, f32[1,1,2,128,128]{4,3,2,1,0:T(8,128)}, u32[]{:S(2)}) copy-start(f32[1,1,2,128,128]{4,3,2,1,0:T(8,128)} %param.12) | copy-start | bytes 393220
  20.6 5.3 %copy-start.6 = (f32[1,1,2,8]{3,2,1,0:T(2,128)S(1)}, f32[1,1,2,8]{3,2,1,0:T(2,128)}, u32[]{:S(2)}) copy-start(f32[1,1,2,8]{3,2,1,0:T(2,128)} %param.10) | copy-start | bytes 196
  20.7 12.1 %collective-permute-start.3 = (f32[4,64,256]{2,1,0:T(8,128)S(1)}, f32[4,64,256]{2,1,0:T(8,128)S(1)}, u32[]{:S(2)}, u32[]{:S(2)}) collective-permute-start(f32[4,64,256]{2,1,0:T(8,128)S(1)} %get-tuple-element.10), channel_id=1, source_target_pairs={{32,0},{64,32},{96,64},{128,96},{160,128},{192,160},{224,192},{256... | collective-permute-start | bytes 786440 | tf_op jit(solution)/shard_map/ppermute | solution.py:241
  22.0 10.8 %collective-permute-start.2 = (f32[4,64,256]{2,1,0:T(8,128)S(1)}, f32[4,64,256]{2,1,0:T(8,128)S(1)}, u32[]{:S(2)}, u32[]{:S(2)}) collective-permute-start(f32[4,64,256]{2,1,0:T(8,128)S(1)} %get-tuple-element.11), channel_id=1, source_target_pairs={{0,32},{32,64},{64,96},{96,128},{128,160},{160,192},{192,224},{224... | collective-permute-start | bytes 786440 | tf_op jit(solution)/shard_map/ppermute | solution.py:240
  26.7 14.6 %all-to-all-start = ((f32[32,1,128]{2,1,0:T(1,128)}), f32[32,1,128]{2,1,0:T(1,128)S(1)}, u32[]{:S(2)}, u32[]{:S(2)}) async-start(f32[32,1,128]{2,1,0:T(1,128)} %broadcast_in_dim.35), calls=%async_computation | async-start | bytes 32768 | tf_op jit(solution)/shard_map/all_to_all | solution.py:208
  32.8 0.7 copy-start.5
  33.5 1.2 copy-start.1
  38.5 0.7 copy-start.7
  99.0 4.0 %copy-start.8 = (f32[4,64,256]{2,1,0:T(8,128)S(1)}, f32[4,64,256]{2,1,0:T(8,128)}, u32[]{:S(2)}) copy-start(f32[4,64,256]{2,1,0:T(8,128)} %copy-done.7) | copy-start | bytes 786436
  99.0 17.0 %all-to-all-start.4 = ((f32[32,4,8,128]{3,2,1,0:T(8,128)}), f32[32,4,8,128]{3,2,1,0:T(8,128)S(1)}, u32[]{:S(2)}, u32[]{:S(2)}) async-start(f32[32,4,8,128]{3,2,1,0:T(8,128)} %broadcast_in_dim.37), calls=%async_computation.4 | async-start | bytes 1048576 | tf_op jit(solution)/shard_map/all_to_all | solution.py:208
  103.1 23.7 %collective-permute-start.4 = (f32[4,64,256]{2,1,0:T(8,128)S(1)}, f32[4,64,256]{2,1,0:T(8,128)S(1)}, u32[]{:S(2)}, u32[]{:S(2)}) collective-permute-start(f32[4,64,256]{2,1,0:T(8,128)S(1)} %copy-done.8), channel_id=1, source_target_pairs={{0,32},{32,64},{64,96},{96,128},{128,160},{160,192},{192,224},{224... | collective-permute-start | bytes 786440 | tf_op jit(solution)/shard_map/ppermute | solution.py:303
  106.1 20.7 %collective-permute-start.5 = (f32[4,64,256]{2,1,0:T(8,128)S(1)}, f32[4,64,256]{2,1,0:T(8,128)}, u32[]{:S(2)}, u32[]{:S(2)}) collective-permute-start(f32[4,64,256]{2,1,0:T(8,128)S(1)} %get-tuple-element.8), channel_id=1, source_target_pairs={{32,0},{64,32},{96,64},{128,96},{160,128},{192,160},{224,192},{256... | collective-permute-start | bytes 786440 | tf_op jit(solution)/shard_map/ppermute | solution.py:302
  116.0 22.9 %collective-permute-start.8 = (f32[32,4,8,128]{3,2,1,0:T(8,128)S(1)}, f32[32,4,8,128]{3,2,1,0:T(8,128)S(1)}, u32[]{:S(2)}, u32[]{:S(2)}) collective-permute-start(f32[32,4,8,128]{3,2,1,0:T(8,128)S(1)} %all-to-all-done.4.refs_1_), channel_id=1, source_target_pairs={{0,1},{1,0},{2,3},{3,2},{4,5},{5,4},{6,7},{7,6},{8,9},{9,8},{10,11... | collective-permute-start | bytes 1572872 | tf_op jit(solution)/shard_map/ppermute | solution.py:284
  127.9 9.1 %collective-permute-start.7 = (f32[4,128,128]{2,1,0:T(8,128)S(1)}, f32[4,128,128]{2,1,0:T(8,128)S(1)}, u32[]{:S(2)}, u32[]{:S(2)}) collective-permute-start(f32[4,128,128]{2,1,0:T(8,128)S(1)} %slice.19), channel_id=1, source_target_pairs={{1,0},{2,1},{3,2},{4,3},{5,4},{6,5},{7,6},{8,7},{9,8},{10,9},{11,1... | collective-permute-start | bytes 786440 | tf_op jit(solution)/shard_map/ppermute | solution.py:307
  129.8 8.4 %collective-permute-start.6 = (f32[4,128,128]{2,1,0:T(8,128)S(1)}, f32[4,128,128]{2,1,0:T(8,128)S(1)}, u32[]{:S(2)}, u32[]{:S(2)}) collective-permute-start(f32[4,128,128]{2,1,0:T(8,128)S(1)} %slice.19), channel_id=1, source_target_pairs={{0,1},{1,2},{2,3},{3,4},{4,5},{5,6},{6,7},{7,8},{8,9},{9,10},{10,1... | collective-permute-start | bytes 786440 | tf_op jit(solution)/shard_map/ppermute | solution.py:306

commit v2 on v1

--- a/solution.py
+++ b/solution.py
@@ -13,16 +13,11 @@
 VMEM_BYTES = 40 * 1024 * 1024
 
 
-def block_form(matrix):
-    real, imag = matrix.real, matrix.imag
-    return np.block([[real, -imag], [imag, real]])
-
-
 def split_table(values):
     whole = values.astype(np.float32)
     high = whole.astype(jnp.bfloat16)
     low = (whole - high.astype(np.float32)).astype(jnp.bfloat16)
-    return (high, low)
+    return np.stack([high, low])
 
 
 def tables(probe_len):
@@ -33,9 +28,19 @@
     frequency = ((indices + half) % probe_len - half) / half
     phase = np.exp(-1j * PHASE_EDGE * frequency * frequency)
     move = np.conj(dft) @ (phase[:, None] * dft)
-    forms = (block_form(dft), block_form(dft).T, block_form(move), block_form(move).T)
-    parts = [split_table(form) for form in forms]
-    return np.stack([np.stack(pair) for pair in parts])
+    parts = [split_table(part) for form in (dft, move) for part in (form.real, form.imag)]
+    return np.stack(parts)
+
+
+def block_forms(real, imag):
+    above = jnp.concatenate([real, -imag], axis=1)
+    below = jnp.concatenate([imag, real], axis=1)
+    above_t = jnp.concatenate([real, imag], axis=1)
+    below_t = jnp.concatenate([-imag, real], axis=1)
+    return (
+        jnp.concatenate([above, below], axis=0),
+        jnp.concatenate([above_t, below_t], axis=0),
+    )
 
 
 def dot3(left, right):
@@ -71,36 +76,109 @@
     return [(wide[:n, :n], wide[:n, n:]), (wide[n:, :n], wide[n:, n:])]
 
 
+def near_lanes(shape):
+    return lax.broadcasted_iota(jnp.int32, shape, len(shape) - 1) < shape[-1] // 2
+
+
+def roll_planes(values):
+    return jnp.stack([pltpu.roll(plane, plane.shape[-1] // 2, 1) for plane in values])
+
+
+def split_kernel(source, own, upper, lower, sems):
+    half = upper.shape[1]
+    copies = [
+        pltpu.make_async_copy(source.at[:, 0:half], upper, sems.at[0]),
+        pltpu.make_async_copy(source.at[:, half : 2 * half], lower, sems.at[1]),
+        pltpu.make_async_copy(source, own, sems.at[2]),
+    ]
+    for copy in copies:
+        copy.start()
+    for copy in copies:
+        copy.wait()
+
+
+def repeat_kernel(parts, out):
+    total = parts[0]
+    for at in range(1, parts.shape[0]):
+        total = total + parts[at]
+    for at in range(out.shape[0]):
+        out[at] = total
+
+
+def pack_kernel(own, above, below, to_left, to_right):
+    n = own.shape[-1]
+    half = n // 2
+    near = near_lanes(own.shape)
+    first = jnp.concatenate([above[...], own[:, :half]], axis=1)
+    second = jnp.concatenate([own[:, half:], below[...]], axis=1)
+    second = roll_planes(second)
+    to_left[...] = jnp.where(near, first, second)
+    to_right[...] = jnp.where(near, second, first)
+
+
+def merge_kernel(tall, from_left, from_right, up, middle, down):
+    n = tall.shape[-1]
+    half = n // 2
+    near = near_lanes(from_left.shape)
+    first = tall[:, :n] + jnp.where(near, from_left[...], from_right[...])
+    second = tall[:, n:] + roll_planes(jnp.where(near, from_right[...], from_left[...]))
+    up[...] = first[:, :half]
+    middle[:, :half] = first[:, half:]
+    middle[:, half:] = second[:, :half]
+    down[...] = second[:, half:]
+
+
 def model_kernel(
-    positions, weights, own, beside, above, below, mean, basis, measured, table,
-    grad_above, grad_own, grad_below, probe_grad, frame, grads,
+    positions_in, weights, own, above, below, from_left, from_right, mean_in, basis_in,
+    measured_in, table_in, tall, to_left, to_right, probe_grad,
+    frame, grads, positions, mean, basis, measured, table, sems,
 ):
+    copies = [
+        pltpu.make_async_copy(source, target, sems.at[at])
+        for at, (source, target) in enumerate(
+            [
+                (positions_in, positions),
+                (mean_in, mean),
+                (basis_in, basis),
+                (table_in, table),
+                (measured_in, measured),
+            ]
+        )
+    ]
+    for copy in copies:
+        copy.start()
     n = mean.shape[-1]
     half = n // 2
     modes = basis.shape[0]
-    frame[:, 0:half, :] = above[...]
+    near = near_lanes(own.shape)
+    frame[:, 0:half, 0:n] = above[...]
     frame[:, half : half + n, 0:n] = own[...]
-    frame[:, half : half + n, n : 2 * n] = beside[...]
-    frame[:, half + n : 2 * n, :] = below[...]
+    frame[:, half + n : 2 * n, 0:n] = below[...]
+    frame[:, 0:n, n : 2 * n] = jnp.where(near, from_right[...], from_left[...])
+    frame[:, n : 2 * n, n : 2 * n] = roll_planes(
+        jnp.where(near, from_left[...], from_right[...])
+    )
     grads[...] = jnp.zeros(grads.shape, jnp.float32)
-    dft, dft_t, move, move_t = [(table[at, 0], table[at, 1]) for at in range(4)]
     slots = range(2)
+    copies[0].wait()
     rows = [positions[slot, 0] for slot in slots]
     offsets = [row & 7 for row in rows]
     bases = [pl.multiple_of(row - offset, 8) for row, offset in zip(rows, offsets)]
-    tall = n + 8
+    span = n + 8
     cols = [positions[slot, 1] for slot in slots]
 
     def window(slot, plane):
-        strip = frame[plane, pl.ds(bases[slot], tall), :]
+        strip = frame[plane, pl.ds(bases[slot], span), :]
         strip = pltpu.roll(strip, (5 * half - cols[slot]) & (2 * n - 1), 1)[:, :n]
-        shift = jnp.where(offsets[slot] == 0, 0, tall - offsets[slot])
+        shift = jnp.where(offsets[slot] == 0, 0, span - offsets[slot])
         return pltpu.roll(strip, shift, 0)[:n]
 
     transmit = [
         [(1.0 + window(slot, 2 * layer), window(slot, 2 * layer + 1)) for slot in slots]
         for layer in range(2)
     ]
+    copies[1].wait()
+    copies[2].wait()
     probes = []
     for slot in slots:
         real = mean[0]
@@ -116,8 +194,16 @@
     def conj_times(first, second):
         return [(a * c + b * d, a * d - b * c) for (a, b), (c, d) in zip(first, second)]
 
+    copies[3].wait()
+    dft_high, dft_t_high = block_forms(table[0, 0], table[1, 0])
+    dft_low, dft_t_low = block_forms(table[0, 1], table[1, 1])
+    move_high, move_t_high = block_forms(table[2, 0], table[3, 0])
+    move_low, move_t_low = block_forms(table[2, 1], table[3, 1])
+    dft, dft_t = (dft_high, dft_low), (dft_t_high, dft_t_low)
+    move, move_t = (move_high, move_low), (move_t_high, move_t_low)
     entered = both_sides(times(probes, transmit[0]), move, move_t)
     far = both_sides(times(entered, transmit[1]), dft, dft_t)
+    copies[4].wait()
     chi = []
     for slot in slots:
         real, imag = far[slot]
@@ -134,10 +220,10 @@
                 )
                 lowered = pltpu.roll(padded, offsets[slot], 0)
                 padded = jnp.concatenate(
-                    [lowered, jnp.zeros((tall, n), jnp.float32)], axis=1
+                    [lowered, jnp.zeros((span, n), jnp.float32)], axis=1
                 )
                 shifted = pltpu.roll(padded, (cols[slot] + 3 * half) & (2 * n - 1), 1)
-                at = (2 * layer + part, pl.ds(bases[slot], tall), slice(None))
+                at = (2 * layer + part, pl.ds(bases[slot], span), slice(None))
                 grads[at] = grads[at] + shifted
 
     deposit(1, conj_times(entered, back))
@@ -149,22 +235,35 @@
         for part in range(2):
             piece = back[slot][part].reshape(blocks, 8, n)
             probe_grad[part * blocks : (part + 1) * blocks, slot] = piece
-    grad_above[...] = grads[:, 0:half, :]
-    grad_own[...] = grads[:, half : half + n, :]
-    grad_below[...] = grads[:, half + n : 2 * n, :]
-
-
-def mix_kernel(weights, gathered, mixed):
-    count, per_tile = gathered.shape[0], gathered.shape[1]
-    modes = mixed.shape[0]
-    totals = [jnp.zeros(mixed.shape[1:], jnp.float32) for mode in range(modes)]
+    row_at = lax.broadcasted_iota(jnp.int32, (modes, n), 0)
+    lane_at = lax.broadcasted_iota(jnp.int32, (modes, n), 1)
+    packed = jnp.zeros((modes, n), jnp.float32)
+    for slot in slots:
+        for mode in range(modes):
+            here = (row_at == mode) & ((lane_at >= half) == (slot == 1))
+            packed = jnp.where(here, weights[slot, mode], packed)
+    probe_grad[:, 2] = jnp.broadcast_to(packed[None], (2 * blocks, modes, n))
+    tall[...] = grads[:, :, 0:n]
+    first = grads[:, 0:n, n : 2 * n]
+    second = roll_planes(grads[:, n : 2 * n, n : 2 * n])
+    to_right[...] = jnp.where(near, first, second)
+    to_left[...] = jnp.where(near, second, first)
+
+
+def mix_kernel(gathered, mixed):
+    count, per_tile = gathered.shape[0], gathered.shape[1] - 1
+    modes, rows, n = mixed.shape
+    totals = [jnp.zeros((modes, n), jnp.float32) for row in range(rows)]
     for source in range(count):
+        packed = gathered[source, per_tile]
         for slot in range(per_tile):
-            term = gathered[source, slot]
-            for mode in range(modes):
-                totals[mode] = totals[mode] + weights[source, slot * modes + mode] * term
-    for mode in range(modes):
-        mixed[mode] = totals[mode]
+            lane = slot * (n // 2)
+            factor = jnp.broadcast_to(packed[:, lane : lane + 1], (modes, n))
+            for row in range(rows):
+                term = gathered[source, slot, row : row + 1]
+                totals[row] = totals[row] + factor * term
+    for row in range(rows):
+        mixed[:, row] = totals[row]
 
 
 def ortho_kernel(core, mine, other, basis, out, step_len=None):
@@ -208,9 +307,8 @@
     return lax.all_to_all(values, axis, 0, 0, tiled=True, axis_index_groups=groups)
 
 
-def to_all(values, axis, count, groups=None):
-    repeated = jnp.broadcast_to(values[None], (count,) + values.shape)
-    return exchange(repeated, axis, groups)
+def away(values):
+    return pltpu.with_memory_space_constraint(values, pltpu.HBM)
 
 
 def vmem_specs(count):
@@ -231,55 +329,101 @@
     smem = pl.BlockSpec(memory_space=pltpu.SMEM)
     weights = mode_weights[0, 0]
 
-    own = obj_delta.reshape(planes, n, n)
-    left = lax.ppermute(own, "sx", forward_x)
-    right = lax.ppermute(own, "sx", backward_x)
-    near = lax.broadcasted_iota(jnp.int32, (1, 1, n), 2) < half
-    beside = jnp.where(near, right, left)
-    strip = jnp.concatenate([own, beside], axis=2)
-    above = lax.ppermute(strip[:, half:], "sy", forward_y)
-    below = lax.ppermute(strip[:, :half], "sy", backward_y)
-
-    flat_weights = jnp.pad(weights.reshape(1, per_tile * modes), ((0, 0), (0, 128 - per_tile * modes)))
-    all_weights = to_all(flat_weights, "sy", count_y).reshape(count_y, 128)
-
     f32 = jnp.float32
-    grad_above, grad_own, grad_below, probe_grad = pl.pallas_call(
+    block = jax.ShapeDtypeStruct((planes, n, n), f32)
+    edge = jax.ShapeDtypeStruct((planes, half, n), f32)
+    distant = pl.BlockSpec(memory_space=pltpu.HBM)
+    own, upper, lower = pl.pallas_call(
+        split_kernel,
+        out_shape=(block, edge, edge),
+        in_specs=[distant],
+        out_specs=tuple(vmem_specs(3)),
+        scratch_shapes=[pltpu.SemaphoreType.DMA((3,))],
+        compiler_params=params,
+        name="split",
+    )(away(obj_delta.reshape(planes, n, n)))
+    above = lax.ppermute(lower, "sy", forward_y)
+    below = lax.ppermute(upper, "sy", backward_y)
+    to_left, to_right = pl.pallas_call(
+        pack_kernel,
+        out_shape=(block, block),
+        in_specs=vmem_specs(3),
+        out_specs=tuple(vmem_specs(2)),
+        compiler_params=params,
+        name="pack",
+    )(own, above, below)
+    from_left = lax.ppermute(to_right, "sx", forward_x)
+    from_right = lax.ppermute(to_left, "sx", backward_x)
+
+    tall, to_left, to_right, probe_grad = pl.pallas_call(
         model_kernel,
         out_shape=(
-            jax.ShapeDtypeStruct((planes, half, 2 * n), f32),
-            jax.ShapeDtypeStruct((planes, n, 2 * n), f32),
-            jax.ShapeDtypeStruct((planes, half, 2 * n), f32),
-            jax.ShapeDtypeStruct((2 * blocks, per_tile, 8, n), f32),
+            jax.ShapeDtypeStruct((planes, 2 * n, n), f32),
+            block,
+            block,
+            jax.ShapeDtypeStruct((2 * blocks, per_tile + 1, 8, n), f32),
         ),
-        in_specs=[smem, smem] + vmem_specs(8),
+        in_specs=[distant, smem] + vmem_specs(5) + [distant] * 4,
         out_specs=tuple(vmem_specs(4)),
-        scratch_shapes=[pltpu.VMEM((planes, 2 * n, 2 * n), f32)] * 2,
+        scratch_shapes=[
+            pltpu.VMEM((planes, 2 * n, 2 * n), f32),
+            pltpu.VMEM((planes, 2 * n, 2 * n), f32),
+            pltpu.SMEM((per_tile, 2), jnp.int32),
+            pltpu.VMEM((2, n, n), f32),
+            pltpu.VMEM((modes, 2, n, n), f32),
+            pltpu.VMEM((per_tile, n, n), f32),
+            pltpu.VMEM((4, 2, n, n), jnp.bfloat16),
+            pltpu.SemaphoreType.DMA((5,)),
+        ],
         compiler_params=params,
         name="model",
     )(
-        positions[0, 0], weights, own, beside, above, below, probe_mean, probe_basis,
-        amplitudes[0, 0], jnp.asarray(tables(n)),
+        away(positions[0, 0]), weights, own, above, below, from_left, from_right,
+        away(probe_mean), away(probe_basis), away(amplitudes[0, 0]),
+        away(jnp.asarray(tables(n))),
     )
 
     gathered = exchange(probe_grad, "sy")
+    from_left = lax.ppermute(to_right, "sx", forward_x)
+    from_right = lax.ppermute(to_left, "sx", backward_x)
+    gathered, from_left, from_right = lax.optimization_barrier((gathered, from_left, from_right))
     mixed = pl.pallas_call(
         mix_kernel,
         out_shape=jax.ShapeDtypeStruct((modes, 8, n), f32),
-        in_specs=[smem] + vmem_specs(1),
+        in_specs=vmem_specs(1),
         out_specs=vmem_specs(1)[0],
         compiler_params=params,
         name="mix",
-    )(all_weights, gathered)
-
+    )(gathered)
     cores = 2
     per_core = count_x // cores
     pairs = [[cores * at + core for core in range(cores)] for at in range(per_core)]
     columns = [[cores * at + core for at in range(per_core)] for core in range(cores)]
     some = modes // cores
-    mine = exchange(mixed, "sx", pairs).reshape(cores, some, 8, n).sum(axis=0)
-    mine = to_all(mine, "sx", per_core, columns).sum(axis=0)
-    mine = to_all(mine, "sy", count_y)
+    def summed_copies(parts, count):
+        return pl.pallas_call(
+            repeat_kernel,
+            out_shape=jax.ShapeDtypeStruct((count,) + parts.shape[1:], f32),
+            in_specs=vmem_specs(1),
+            out_specs=vmem_specs(1)[0],
+            compiler_params=params,
+            name="repeat",
+        )(parts)
+
+    parts = exchange(mixed, "sx", pairs).reshape(cores, some, 8, n)
+    parts = exchange(summed_copies(parts, per_core), "sx", columns)
+    up, middle, down = pl.pallas_call(
+        merge_kernel,
+        out_shape=(edge, block, edge),
+        in_specs=vmem_specs(3),
+        out_specs=tuple(vmem_specs(3)),
+        compiler_params=params,
+        name="merge",
+    )(tall, from_left, from_right)
+    from_below = lax.ppermute(up, "sy", backward_y)
+    from_above = lax.ppermute(down, "sy", forward_y)
+    parts, from_below, from_above = lax.optimization_barrier((parts, from_below, from_above))
+    mine = exchange(summed_copies(parts, count_y), "sy")
     swap = [(at, at ^ 1) for at in range(count_x)]
     other = lax.ppermute(mine, "sx", swap)
     core = (lax.axis_index("sx") % cores).astype(jnp.int32).reshape(1)
@@ -299,13 +443,7 @@
     )(core, mine, other, probe_basis.reshape(modes, 2 * blocks, 8, n))
     new_basis = new_basis.reshape(probe_basis.shape)
 
-    from_below = lax.ppermute(grad_above, "sy", backward_y)
-    from_above = lax.ppermute(grad_below, "sy", forward_y)
-    joined = grad_own + jnp.concatenate([from_above, from_below], axis=1)
-    outer = joined[:, :, n:]
-    from_left = lax.ppermute(outer, "sx", forward_x)
-    from_right = lax.ppermute(outer, "sx", backward_x)
-    obj_grad = joined[:, :, :n] + jnp.where(near, from_left, from_right)
+    obj_grad = middle + jnp.concatenate([from_above, from_below], axis=1)
     return (obj_grad.reshape(obj_delta.shape), new_basis)
 
 

time: 143 us -> 130 us (0.909); the launches traced: 142 us -> 127 us
  blocking collectives: 55.8 us -> 21.6 us
  starting transfers between devices: 55 us -> 69 us
  waiting for transfers between devices: 15.3 us -> 23.1 us
  local copies, waits for them, and re-layouts: 4.19 us -> 0.68 us
  Pallas kernels: 7.97 us -> 11.3 us
  other arithmetic: 2.89 us -> 0.73 us
    all_to_all x3 -> x2, blocking collectives: 55.8 us -> 21.6 us  [exchange(): lax.all_to_all(values, axis, 0, 0, tiled=True, axis_index_groups=groups)]
    all_to_all x2, starting transfers between devices: 10.1 us -> 29.8 us  [exchange(): lax.all_to_all(values, axis, 0, 0, tiled=True, axis_index_groups=groups)]
    ppermute x8, waiting for transfers between devices: 4.62 us -> 13.5 us  [the longest x2 6.16 us: local(): from_right = lax.ppermute(to_left, 'sx', backward_x)]
    pallas_call x1 -> x6, Pallas kernels: 3.78 us -> 7.93 us  [the longest x1 5.74 us: local(): pl.pallas_call(model_kernel, out_shape=(jax.ShapeDtypeStruct((planes, 2 *...]
    ppermute x8, starting transfers between devices: 34.1 us -> 30.7 us  [the longest x2 12.2 us: local(): from_right = lax.ppermute(to_left, 'sx', backward_x)]
    ppermute x1, starting transfers between devices: 10.8 us -> 8.5 us  [local(): other = lax.ppermute(mine, 'sx', swap)]
    unnamed x18 -> x4, local copies, waits for them, and re-layouts: 2.59 us -> 0.68 us
    all_to_all x2, waiting for transfers between devices: 10.7 us -> 8.86 us  [exchange(): lax.all_to_all(values, axis, 0, 0, tiled=True, axis_index_groups=groups)]
  transfers between devices with their start and end apart: 11 -> 11, of which waited for: 5 -> 10; matrix products, arithmetic and copies ran while one was open for 2% -> 1% of each run, Pallas kernels for 3% -> 0%
where the time goes in v2:
time: 130 us; the launch traced here: 127 us
  starting transfers between devices  69 us (53%)
  waiting for transfers between devices  23.1 us (18%)
  blocking collectives  21.6 us (17%)
  Pallas kernels  11.3 us (9%)
    all_to_all x2, starting transfers between devices, exchange(): lax.all_to_all(values, axis, 0, 0, tiled=True, axis_index_groups=groups)  29.8 us
    all_to_all x2, blocking collectives, exchange(): lax.all_to_all(values, axis, 0, 0, tiled=True, axis_index_groups=groups)  21.6 us
    ppermute x2, starting transfers between devices, local(): from_right = lax.ppermute(to_left, 'sx', backward_x)  12.2 us
    all_to_all x2, waiting for transfers between devices, exchange(): lax.all_to_all(values, axis, 0, 0, tiled=True, axis_index_groups=groups)  8.86 us
    ppermute x1, starting transfers between devices, local(): other = lax.ppermute(mine, 'sx', swap)  8.5 us
    ppermute x2, starting transfers between devices, local(): from_left = lax.ppermute(to_right, 'sx', forward_x)  8.02 us
    ppermute x2, waiting for transfers between devices, local(): from_right = lax.ppermute(to_left, 'sx', backward_x)  6.16 us
    pallas_call x1, Pallas kernels, local(): pl.pallas_call(model_kernel, out_shape=(jax.ShapeDtypeStruct((planes, 2 *...  5.74 us
  transfers between devices with their start and end apart: 11, of which 10 were waited for; matrix products, arithmetic and copies ran while one was open for 1% of the time, Pallas kernels for 0%

profile of v2, /device:TPU:1, one launch (start us, length us, event | category | flops | bytes accessed | tf_op | source)
XLA Modules:
  0.0 127.2 jit_solution(14833915386098995185)
XLA Ops:
  0.6 1.1 split.1
  1.7 4.0 %collective-permute-start = (f32[4,64,128]{2,1,0:T(8,128)S(1)}, f32[4,64,128]{2,1,0:T(8,128)S(1)}, u32[]{:S(2)}, u32[]{:S(2)}) collective-permute-start(f32[4,64,128]{2,1,0:T(8,128)S(1)} %get-tuple-element.21), channel_id=1, source_target_pairs={{0,32},{32,64},{64,96},{96,128},{128,160},{160,192},{192,224},{224... | collective-permute-start | bytes 393224 | tf_op jit(solution)/shard_map/ppermute | solution.py:345
  5.7 1.3 %collective-permute-start.1 = (f32[4,64,128]{2,1,0:T(8,128)S(1)}, f32[4,64,128]{2,1,0:T(8,128)S(1)}, u32[]{:S(2)}, u32[]{:S(2)}) collective-permute-start(f32[4,64,128]{2,1,0:T(8,128)S(1)} %get-tuple-element.22), channel_id=1, source_target_pairs={{32,0},{64,32},{96,64},{128,96},{160,128},{192,160},{224,192},{256... | collective-permute-start | bytes 393224 | tf_op jit(solution)/shard_map/ppermute | solution.py:346
  7.0 0.6 collective-permute-done.above
  7.6 3.8 %collective-permute-done.1.below = f32[4,64,128]{2,1,0:T(8,128)S(1)} collective-permute-done((f32[4,64,128]{2,1,0:T(8,128)S(1)}, f32[4,64,128]{2,1,0:T(8,128)S(1)}, u32[]{:S(2)}, u32[]{:S(2)}) %collective-permute-start.1) | collective-permute-done | bytes 131104 | tf_op jit(solution)/shard_map/ppermute | solution.py:346
  11.4 0.1 pack.1
  11.6 6.0 %collective-permute-start.2 = (f32[4,128,128]{2,1,0:T(8,128)S(1)}, f32[4,128,128]{2,1,0:T(8,128)S(1)}, u32[]{:S(2)}, u32[]{:S(2)}) collective-permute-start(f32[4,128,128]{2,1,0:T(8,128)S(1)} %get-tuple-element.23), channel_id=1, source_target_pairs={{0,1},{1,2},{2,3},{3,4},{4,5},{5,6},{6,7},{7,8},{8,9},{9,10},{10,1... | collective-permute-start | bytes 786440 | tf_op jit(solution)/shard_map/ppermute | solution.py:355
  17.6 9.9 %collective-permute-start.3 = (f32[4,128,128]{2,1,0:T(8,128)S(1)}, f32[4,128,128]{2,1,0:T(8,128)S(1)}, u32[]{:S(2)}, u32[]{:S(2)}) collective-permute-start(f32[4,128,128]{2,1,0:T(8,128)S(1)} %get-tuple-element.24), channel_id=1, source_target_pairs={{1,0},{2,1},{3,2},{4,3},{5,4},{6,5},{7,6},{8,7},{9,8},{10,9},{11,1... | collective-permute-start | bytes 786440 | tf_op jit(solution)/shard_map/ppermute | solution.py:356
  27.4 0.0 collective-permute-done.2.from_left
  27.5 1.1 collective-permute-done.3.from_right
  28.6 0.0 copy-start.1
  28.6 0.7 copy-done.1
  29.3 5.7 %model.1 = (f32[4,256,128]{2,1,0:T(8,128)S(1)}, f32[4,128,128]{2,1,0:T(8,128)S(1)}, f32[4,128,128]{2,1,0:T(8,128)S(1)}, f32[32,3,8,128]{3,2,1,0:T(8,128)}) custom-call(s32[2,2]{1,0:T(2,128)} %bitcast.16, f32[2,8]{1,0:T(2,128)S(1)} %bitcast.11, f32[4,128,128]{2,1,0:T(8,128)S(1)} %get-tuple-element.20.own, f32[4,64,128]{2,1,0:T(8,128)S(1)} %collective-permute-done.above, ...), custom_call_target="tpu_custom_call" | custom-call | tf_op jit(solution)/shard_map/model/pallas_call | solution.py:358
  35.0 8.4 %all-to-all-start = ((f32[32,3,8,128]{3,2,1,0:T(8,128)}), f32[32,3,8,128]{3,2,1,0:T(8,128)S(1)}, u32[]{:S(2)}, u32[]{:S(2)}) async-start(f32[32,3,8,128]{3,2,1,0:T(8,128)} %get-tuple-element.26), calls=%async_computation | async-start | bytes 786432 | tf_op jit(solution)/shard_map/all_to_all | solution.py:307
  43.4 2.0 %collective-permute-start.4 = (f32[4,128,128]{2,1,0:T(8,128)S(1)}, f32[4,128,128]{2,1,0:T(8,128)S(1)}, u32[]{:S(2)}, u32[]{:S(2)}) collective-permute-start(f32[4,128,128]{2,1,0:T(8,128)S(1)} %get-tuple-element.27), channel_id=1, source_target_pairs={{0,1},{1,2},{2,3},{3,4},{4,5},{5,6},{6,7},{7,8},{8,9},{9,10},{10,1... | collective-permute-start | bytes 786440 | tf_op jit(solution)/shard_map/ppermute | solution.py:387
  45.4 2.3 %collective-permute-start.5 = (f32[4,128,128]{2,1,0:T(8,128)S(1)}, f32[4,128,128]{2,1,0:T(8,128)S(1)}, u32[]{:S(2)}, u32[]{:S(2)}) collective-permute-start(f32[4,128,128]{2,1,0:T(8,128)S(1)} %get-tuple-element.28), channel_id=1, source_target_pairs={{1,0},{2,1},{3,2},{4,3},{5,4},{6,5},{7,6},{8,7},{9,8},{10,9},{11,1... | collective-permute-start | bytes 786440 | tf_op jit(solution)/shard_map/ppermute | solution.py:388
  47.8 1.0 collective-permute-done.4.from_left
  48.7 5.0 %collective-permute-done.5.from_right = f32[4,128,128]{2,1,0:T(8,128)S(1)} collective-permute-done((f32[4,128,128]{2,1,0:T(8,128)S(1)}, f32[4,128,128]{2,1,0:T(8,128)S(1)}, u32[]{:S(2)}, u32[]{:S(2)}) %collective-permute-start.5) | collective-permute-done | bytes 262176 | tf_op jit(solution)/shard_map/ppermute | solution.py:388
  53.8 2.2 %all-to-all-done.gathered = f32[32,3,8,128]{3,2,1,0:T(8,128)S(1)} async-done(((f32[32,3,8,128]{3,2,1,0:T(8,128)}), f32[32,3,8,128]{3,2,1,0:T(8,128)S(1)}, u32[]{:S(2)}, u32[]{:S(2)}) %all-to-all-start) | async-done | bytes 393248 | tf_op jit(solution)/shard_map/all_to_all | solution.py:307
  56.0 0.2 mix.1
  56.2 3.4 %all_to_all.20 = f32[8,8,128]{2,1,0:T(8,128)S(1)} all-to-all(f32[8,8,128]{2,1,0:T(8,128)S(1)} %mix.1), channel_id=1, replica_groups={{0,1},{2,3},{4,5},{6,7},{8,9},{10,11},{12,13},{14,15},{16,17},{18,19},{..., dimensions={0} | all-to-all | bytes 65536 | tf_op jit(solution)/shard_map/all_to_all | solution.py:307
  59.6 0.7 repeat.2
  60.3 21.4 %all-to-all-start.2 = ((f32[16,4,8,128]{3,2,1,0:T(8,128)}), f32[16,4,8,128]{3,2,1,0:T(8,128)S(1)}, u32[]{:S(2)}, u32[]{:S(2)}) async-start(f32[16,4,8,128]{3,2,1,0:T(8,128)} %repeat.2), calls=%async_computation.2 | async-start | bytes 524288 | tf_op jit(solution)/shard_map/all_to_all | solution.py:307
  81.7 0.1 merge.1
  81.9 1.3 %collective-permute-start.6 = (f32[4,64,128]{2,1,0:T(8,128)S(1)}, f32[4,64,128]{2,1,0:T(8,128)S(1)}, u32[]{:S(2)}, u32[]{:S(2)}) collective-permute-start(f32[4,64,128]{2,1,0:T(8,128)S(1)} %get-tuple-element.33), channel_id=1, source_target_pairs={{32,0},{64,32},{96,64},{128,96},{160,128},{192,160},{224,192},{256... | collective-permute-start | bytes 393224 | tf_op jit(solution)/shard_map/ppermute | solution.py:423
  83.2 4.0 %collective-permute-start.7 = (f32[4,64,128]{2,1,0:T(8,128)S(1)}, f32[4,64,128]{2,1,0:T(8,128)S(1)}, u32[]{:S(2)}, u32[]{:S(2)}) collective-permute-start(f32[4,64,128]{2,1,0:T(8,128)S(1)} %get-tuple-element.34), channel_id=1, source_target_pairs={{0,32},{32,64},{64,96},{96,128},{128,160},{160,192},{192,224},{224... | collective-permute-start | bytes 393224 | tf_op jit(solution)/shard_map/ppermute | solution.py:424
  87.2 1.0 collective-permute-done.6
  88.2 0.9 collective-permute-done.7
  89.1 6.7 %all-to-all-done.2.parts = f32[16,4,8,128]{3,2,1,0:T(8,128)S(1)} async-done(((f32[16,4,8,128]{3,2,1,0:T(8,128)}), f32[16,4,8,128]{3,2,1,0:T(8,128)S(1)}, u32[]{:S(2)}, u32[]{:S(2)}) %all-to-all-start.2) | async-done | bytes 262176 | tf_op jit(solution)/shard_map/all_to_all | solution.py:307
  95.7 0.1 repeat.3
  95.8 0.0 copy-start
  95.8 18.2 %all_to_all.21.refs_1_ = f32[32,4,8,128]{3,2,1,0:T(8,128)S(1)} all-to-all(f32[32,4,8,128]{3,2,1,0:T(8,128)S(1)} %repeat.3), channel_id=1, replica_groups=mesh['sy'=32,'sx'=32] {'sy'}, dimensions={0} | all-to-all | bytes 1048576 | tf_op jit(solution)/shard_map/all_to_all | solution.py:307
  114.0 8.5 %collective-permute-start.8 = (f32[32,4,8,128]{3,2,1,0:T(8,128)S(1)}, f32[32,4,8,128]{3,2,1,0:T(8,128)S(1)}, u32[]{:S(2)}, u32[]{:S(2)}) collective-permute-start(f32[32,4,8,128]{3,2,1,0:T(8,128)S(1)} %all_to_all.21.refs_1_), channel_id=1, source_target_pairs={{0,1},{1,0},{2,3},{3,2},{4,5},{5,4},{6,7},{7,6},{8,9},{9,8},{10,11... | collective-permute-start | bytes 1572872 | tf_op jit(solution)/shard_map/ppermute | solution.py:428
  122.5 0.7 maximum_add_fusion
  123.2 0.8 collective-permute-done.8.refs_2_
  124.0 0.0 copy-done
  124.0 3.2 %orthonormal.1 = f32[8,32,8,128]{3,2,1,0:T(8,128)} custom-call(s32[1]{0:T(128)} %bitcast.6.refs_0_, f32[32,4,8,128]{3,2,1,0:T(8,128)S(1)} %all_to_all.21.refs_1_, f32[32,4,8,128]{3,2,1,0:T(8,128)S(1)} %collective-permute-done.8.refs_2_, f32[8,32,8,128]{3,2,1,0:T(8,128)S(1)} %bitcast.9), custom_call_target="tpu_custom_call" | custom-call | tf_op jit(solution)/shard_map/orthonormal/pallas_call | solution.py:436
Async XLA Ops:
  1.7 5.9 %collective-permute-start = (f32[4,64,128]{2,1,0:T(8,128)S(1)}, f32[4,64,128]{2,1,0:T(8,128)S(1)}, u32[]{:S(2)}, u32[]{:S(2)}) collective-permute-start(f32[4,64,128]{2,1,0:T(8,128)S(1)} %get-tuple-element.21), channel_id=1, source_target_pairs={{0,32},{32,64},{64,96},{96,128},{128,160},{160,192},{192,224},{224... | collective-permute-start | bytes 393224 | tf_op jit(solution)/shard_map/ppermute | solution.py:345
  5.7 5.7 %collective-permute-start.1 = (f32[4,64,128]{2,1,0:T(8,128)S(1)}, f32[4,64,128]{2,1,0:T(8,128)S(1)}, u32[]{:S(2)}, u32[]{:S(2)}) collective-permute-start(f32[4,64,128]{2,1,0:T(8,128)S(1)} %get-tuple-element.22), channel_id=1, source_target_pairs={{32,0},{64,32},{96,64},{128,96},{160,128},{192,160},{224,192},{256... | collective-permute-start | bytes 393224 | tf_op jit(solution)/shard_map/ppermute | solution.py:346
  11.6 15.9 %collective-permute-start.2 = (f32[4,128,128]{2,1,0:T(8,128)S(1)}, f32[4,128,128]{2,1,0:T(8,128)S(1)}, u32[]{:S(2)}, u32[]{:S(2)}) collective-permute-start(f32[4,128,128]{2,1,0:T(8,128)S(1)} %get-tuple-element.23), channel_id=1, source_target_pairs={{0,1},{1,2},{2,3},{3,4},{4,5},{5,6},{6,7},{7,8},{8,9},{9,10},{10,1... | collective-permute-start | bytes 786440 | tf_op jit(solution)/shard_map/ppermute | solution.py:355
  17.6 11.0 %collective-permute-start.3 = (f32[4,128,128]{2,1,0:T(8,128)S(1)}, f32[4,128,128]{2,1,0:T(8,128)S(1)}, u32[]{:S(2)}, u32[]{:S(2)}) collective-permute-start(f32[4,128,128]{2,1,0:T(8,128)S(1)} %get-tuple-element.24), channel_id=1, source_target_pairs={{1,0},{2,1},{3,2},{4,3},{5,4},{6,5},{7,6},{8,7},{9,8},{10,9},{11,1... | collective-permute-start | bytes 786440 | tf_op jit(solution)/shard_map/ppermute | solution.py:356
  28.6 0.7 copy-start.1
  35.0 21.0 %all-to-all-start = ((f32[32,3,8,128]{3,2,1,0:T(8,128)}), f32[32,3,8,128]{3,2,1,0:T(8,128)S(1)}, u32[]{:S(2)}, u32[]{:S(2)}) async-start(f32[32,3,8,128]{3,2,1,0:T(8,128)} %get-tuple-element.26), calls=%async_computation | async-start | bytes 786432 | tf_op jit(solution)/shard_map/all_to_all | solution.py:307
  43.4 5.3 %collective-permute-start.4 = (f32[4,128,128]{2,1,0:T(8,128)S(1)}, f32[4,128,128]{2,1,0:T(8,128)S(1)}, u32[]{:S(2)}, u32[]{:S(2)}) collective-permute-start(f32[4,128,128]{2,1,0:T(8,128)S(1)} %get-tuple-element.27), channel_id=1, source_target_pairs={{0,1},{1,2},{2,3},{3,4},{4,5},{5,6},{6,7},{7,8},{8,9},{9,10},{10,1... | collective-permute-start | bytes 786440 | tf_op jit(solution)/shard_map/ppermute | solution.py:387
  45.4 8.3 %collective-permute-start.5 = (f32[4,128,128]{2,1,0:T(8,128)S(1)}, f32[4,128,128]{2,1,0:T(8,128)S(1)}, u32[]{:S(2)}, u32[]{:S(2)}) collective-permute-start(f32[4,128,128]{2,1,0:T(8,128)S(1)} %get-tuple-element.28), channel_id=1, source_target_pairs={{1,0},{2,1},{3,2},{4,3},{5,4},{6,5},{7,6},{8,7},{9,8},{10,9},{11,1... | collective-permute-start | bytes 786440 | tf_op jit(solution)/shard_map/ppermute | solution.py:388
  60.3 35.4 %all-to-all-start.2 = ((f32[16,4,8,128]{3,2,1,0:T(8,128)}), f32[16,4,8,128]{3,2,1,0:T(8,128)S(1)}, u32[]{:S(2)}, u32[]{:S(2)}) async-start(f32[16,4,8,128]{3,2,1,0:T(8,128)} %repeat.2), calls=%async_computation.2 | async-start | bytes 524288 | tf_op jit(solution)/shard_map/all_to_all | solution.py:307
  81.9 6.3 %collective-permute-start.6 = (f32[4,64,128]{2,1,0:T(8,128)S(1)}, f32[4,64,128]{2,1,0:T(8,128)S(1)}, u32[]{:S(2)}, u32[]{:S(2)}) collective-permute-start(f32[4,64,128]{2,1,0:T(8,128)S(1)} %get-tuple-element.33), channel_id=1, source_target_pairs={{32,0},{64,32},{96,64},{128,96},{160,128},{192,160},{224,192},{256... | collective-permute-start | bytes 393224 | tf_op jit(solution)/shard_map/ppermute | solution.py:423
  83.2 5.9 %collective-permute-start.7 = (f32[4,64,128]{2,1,0:T(8,128)S(1)}, f32[4,64,128]{2,1,0:T(8,128)S(1)}, u32[]{:S(2)}, u32[]{:S(2)}) collective-permute-start(f32[4,64,128]{2,1,0:T(8,128)S(1)} %get-tuple-element.34), channel_id=1, source_target_pairs={{0,32},{32,64},{64,96},{96,128},{128,160},{160,192},{192,224},{224... | collective-permute-start | bytes 393224 | tf_op jit(solution)/shard_map/ppermute | solution.py:424
  95.8 28.2 %copy-start = (f32[8,2,128,128]{3,2,1,0:T(8,128)S(1)}, f32[8,2,128,128]{3,2,1,0:T(8,128)}, u32[]{:S(2)}) copy-start(f32[8,2,128,128]{3,2,1,0:T(8,128)} %basis_in.1) | copy-start | bytes 3145732
  114.0 10.0 %collective-permute-start.8 = (f32[32,4,8,128]{3,2,1,0:T(8,128)S(1)}, f32[32,4,8,128]{3,2,1,0:T(8,128)S(1)}, u32[]{:S(2)}, u32[]{:S(2)}) collective-permute-start(f32[32,4,8,128]{3,2,1,0:T(8,128)S(1)} %all_to_all.21.refs_1_), channel_id=1, source_target_pairs={{0,1},{1,0},{2,3},{3,2},{4,5},{5,4},{6,7},{7,6},{8,9},{9,8},{10,11... | collective-permute-start | bytes 1572872 | tf_op jit(solution)/shard_map/ppermute | solution.py:428

commit v3 on v2

--- a/solution.py
+++ b/solution.py
@@ -11,6 +11,7 @@
 FLOOR = 0.5
 PHASE_EDGE = 3.0
 VMEM_BYTES = 40 * 1024 * 1024
+PIECE = 9
 
 
 def split_table(values):
@@ -129,15 +130,16 @@
 
 
 def model_kernel(
-    positions_in, weights, own, above, below, from_left, from_right, mean_in, basis_in,
+    positions_in, weights_in, own, above, below, from_left, from_right, mean_in, basis_in,
     measured_in, table_in, tall, to_left, to_right, probe_grad,
-    frame, grads, positions, mean, basis, measured, table, sems,
+    frame, grads, positions, weights, mean, basis, measured, table, sems,
 ):
     copies = [
         pltpu.make_async_copy(source, target, sems.at[at])
         for at, (source, target) in enumerate(
             [
                 (positions_in, positions),
+                (weights_in, weights),
                 (mean_in, mean),
                 (basis_in, basis),
                 (table_in, table),
@@ -177,8 +179,8 @@
         [(1.0 + window(slot, 2 * layer), window(slot, 2 * layer + 1)) for slot in slots]
         for layer in range(2)
     ]
-    copies[1].wait()
-    copies[2].wait()
+    for at in (1, 2, 3):
+        copies[at].wait()
     probes = []
     for slot in slots:
         real = mean[0]
@@ -194,7 +196,7 @@
     def conj_times(first, second):
         return [(a * c + b * d, a * d - b * c) for (a, b), (c, d) in zip(first, second)]
 
-    copies[3].wait()
+    copies[4].wait()
     dft_high, dft_t_high = block_forms(table[0, 0], table[1, 0])
     dft_low, dft_t_low = block_forms(table[0, 1], table[1, 1])
     move_high, move_t_high = block_forms(table[2, 0], table[3, 0])
@@ -203,7 +205,7 @@
     move, move_t = (move_high, move_low), (move_t_high, move_t_low)
     entered = both_sides(times(probes, transmit[0]), move, move_t)
     far = both_sides(times(entered, transmit[1]), dft, dft_t)
-    copies[4].wait()
+    copies[5].wait()
     chi = []
     for slot in slots:
         real, imag = far[slot]
@@ -231,18 +233,25 @@
     deposit(0, conj_times(probes, back))
     back = conj_times(transmit[0], back)
     blocks = n // 8
-    for slot in slots:
-        for part in range(2):
-            piece = back[slot][part].reshape(blocks, 8, n)
-            probe_grad[part * blocks : (part + 1) * blocks, slot] = piece
-    row_at = lax.broadcasted_iota(jnp.int32, (modes, n), 0)
-    lane_at = lax.broadcasted_iota(jnp.int32, (modes, n), 1)
-    packed = jnp.zeros((modes, n), jnp.float32)
+    upper_rows = lax.broadcasted_iota(jnp.int32, (8, n), 0) < 4
+    lane_at = lax.broadcasted_iota(jnp.int32, (1, n), 1)
+    packed = jnp.zeros((1, n), jnp.float32)
     for slot in slots:
         for mode in range(modes):
-            here = (row_at == mode) & ((lane_at >= half) == (slot == 1))
-            packed = jnp.where(here, weights[slot, mode], packed)
-    probe_grad[:, 2] = jnp.broadcast_to(packed[None], (2 * blocks, modes, n))
+            packed = jnp.where(lane_at == slot * modes + mode, weights[slot, mode], packed)
+    for part in range(2):
+        for block in range(blocks):
+            first = back[0][part][8 * block : 8 * block + 8]
+            second = back[1][part][8 * block : 8 * block + 8]
+            at = 2 * PIECE * (part * blocks + block)
+            probe_grad[pl.ds(at, 8), 0, :] = jnp.where(
+                upper_rows, first, pltpu.roll(second, 4, 0)
+            )
+            probe_grad[at + 8] = packed
+            probe_grad[pl.ds(at + PIECE, 8), 0, :] = jnp.where(
+                upper_rows, pltpu.roll(first, 4, 0), second
+            )
+            probe_grad[at + PIECE + 8] = packed
     tall[...] = grads[:, :, 0:n]
     first = grads[:, 0:n, n : 2 * n]
     second = roll_planes(grads[:, n : 2 * n, n : 2 * n])
@@ -250,34 +259,44 @@
     to_left[...] = jnp.where(near, second, first)
 
 
-def mix_kernel(gathered, mixed):
-    count, per_tile = gathered.shape[0], gathered.shape[1] - 1
-    modes, rows, n = mixed.shape
-    totals = [jnp.zeros((modes, n), jnp.float32) for row in range(rows)]
-    for source in range(count):
-        packed = gathered[source, per_tile]
-        for slot in range(per_tile):
-            lane = slot * (n // 2)
-            factor = jnp.broadcast_to(packed[:, lane : lane + 1], (modes, n))
-            for row in range(rows):
-                term = gathered[source, slot, row : row + 1]
-                totals[row] = totals[row] + factor * term
-    for row in range(rows):
-        mixed[:, row] = totals[row]
+def mix_kernel(gathered, out, ordered):
+    copies, pairs, rows, n = out.shape
+    modes = 2 * pairs
+    some = rows // 2
+    count = gathered.shape[0] // PIECE
+
+    def row_of_all(at):
+        return gathered[pl.ds(at, count, stride=PIECE), 0, :]
+
+    factors = row_of_all(rows).T[: 2 * modes]
+    terms = jnp.concatenate([row_of_all(at) for at in range(rows)], axis=1)
+    product = jnp.dot(
+        factors, terms, precision=lax.Precision.HIGHEST, preferred_element_type=jnp.float32
+    )
+    for row in range(some):
+        first = product[:modes, row * n : (row + 1) * n]
+        second = product[modes:, (some + row) * n : (some + row + 1) * n]
+        ordered[pl.ds(row, modes, stride=some), :] = first + second
+    for pair in range(pairs):
+        tile = ordered[pair * rows : (pair + 1) * rows]
+        for copy in range(copies):
+            out[copy, pair] = tile
 
 
 def ortho_kernel(core, mine, other, basis, out, step_len=None):
-    modes, blocks = out.shape[0], out.shape[1]
+    modes, blocks, rows, n = out.shape
     part_len = blocks // 2
-    some = modes // 2
-    pixels = part_len * out.shape[2] * out.shape[3]
-    my_base = core[0] * some
-    other_base = some - my_base
-    for mode in range(some):
-        at = my_base + mode
-        out[at] = basis[at] - step_len * mine[:, mode]
-        at = other_base + mode
-        out[at] = basis[at] - step_len * other[:, mode]
+    pixels = part_len * rows * n
+    upper_rows = lax.broadcasted_iota(jnp.int32, (rows, n), 0) < rows // 2
+    first_core = core[0] == 0
+    for block in range(blocks):
+        for pair in range(modes // 2):
+            low = jnp.where(first_core, mine[block, pair], other[block, pair])
+            high = jnp.where(first_core, other[block, pair], mine[block, pair])
+            even = jnp.where(upper_rows, low, pltpu.roll(high, rows // 2, 0))
+            odd = jnp.where(upper_rows, pltpu.roll(low, rows // 2, 0), high)
+            out[2 * pair, block] = basis[2 * pair, block] - step_len * even
+            out[2 * pair + 1, block] = basis[2 * pair + 1, block] - step_len * odd
 
     def total(values):
         return jnp.sum(jnp.sum(values, axis=0), axis=(0, 1), keepdims=True)
@@ -327,7 +346,6 @@
     blocks = n // 8
     params = pltpu.CompilerParams(vmem_limit_bytes=VMEM_BYTES)
     smem = pl.BlockSpec(memory_space=pltpu.SMEM)
-    weights = mode_weights[0, 0]
 
     f32 = jnp.float32
     block = jax.ShapeDtypeStruct((planes, n, n), f32)
@@ -361,57 +379,50 @@
             jax.ShapeDtypeStruct((planes, 2 * n, n), f32),
             block,
             block,
-            jax.ShapeDtypeStruct((2 * blocks, per_tile + 1, 8, n), f32),
+            jax.ShapeDtypeStruct((4 * blocks * PIECE, 1, n), f32),
         ),
-        in_specs=[distant, smem] + vmem_specs(5) + [distant] * 4,
+        in_specs=[distant] * 2 + vmem_specs(5) + [distant] * 4,
         out_specs=tuple(vmem_specs(4)),
         scratch_shapes=[
             pltpu.VMEM((planes, 2 * n, 2 * n), f32),
             pltpu.VMEM((planes, 2 * n, 2 * n), f32),
             pltpu.SMEM((per_tile, 2), jnp.int32),
+            pltpu.SMEM((per_tile, modes), f32),
             pltpu.VMEM((2, n, n), f32),
             pltpu.VMEM((modes, 2, n, n), f32),
             pltpu.VMEM((per_tile, n, n), f32),
             pltpu.VMEM((4, 2, n, n), jnp.bfloat16),
-            pltpu.SemaphoreType.DMA((5,)),
+            pltpu.SemaphoreType.DMA((6,)),
         ],
         compiler_params=params,
         name="model",
     )(
-        away(positions[0, 0]), weights, own, above, below, from_left, from_right,
+        away(positions[0, 0]), away(mode_weights[0, 0]), own, above, below, from_left, from_right,
         away(probe_mean), away(probe_basis), away(amplitudes[0, 0]),
         away(jnp.asarray(tables(n))),
     )
 
-    gathered = exchange(probe_grad, "sy")
+    cores = 2
+    per_core = count_x // cores
+    columns = [[cores * at + core for at in range(per_core)] for core in range(cores)]
+    layers = [
+        [row * count_x + cores * at + core for row in range(count_y) for core in range(cores)]
+        for at in range(per_core)
+    ]
+    gathered = exchange(probe_grad, ("sy", "sx"), layers)
     from_left = lax.ppermute(to_right, "sx", forward_x)
     from_right = lax.ppermute(to_left, "sx", backward_x)
     gathered, from_left, from_right = lax.optimization_barrier((gathered, from_left, from_right))
-    mixed = pl.pallas_call(
+    parts = pl.pallas_call(
         mix_kernel,
-        out_shape=jax.ShapeDtypeStruct((modes, 8, n), f32),
+        out_shape=jax.ShapeDtypeStruct((per_core, modes // 2, 8, n), f32),
         in_specs=vmem_specs(1),
         out_specs=vmem_specs(1)[0],
+        scratch_shapes=[pltpu.VMEM((4 * modes, n), f32)],
         compiler_params=params,
         name="mix",
     )(gathered)
-    cores = 2
-    per_core = count_x // cores
-    pairs = [[cores * at + core for core in range(cores)] for at in range(per_core)]
-    columns = [[cores * at + core for at in range(per_core)] for core in range(cores)]
-    some = modes // cores
-    def summed_copies(parts, count):
-        return pl.pallas_call(
-            repeat_kernel,
-            out_shape=jax.ShapeDtypeStruct((count,) + parts.shape[1:], f32),
-            in_specs=vmem_specs(1),
-            out_specs=vmem_specs(1)[0],
-            compiler_params=params,
-            name="repeat",
-        )(parts)
-
-    parts = exchange(mixed, "sx", pairs).reshape(cores, some, 8, n)
-    parts = exchange(summed_copies(parts, per_core), "sx", columns)
+    parts = exchange(parts, "sx", columns)
     up, middle, down = pl.pallas_call(
         merge_kernel,
         out_shape=(edge, block, edge),
@@ -423,7 +434,15 @@
     from_below = lax.ppermute(up, "sy", backward_y)
     from_above = lax.ppermute(down, "sy", forward_y)
     parts, from_below, from_above = lax.optimization_barrier((parts, from_below, from_above))
-    mine = exchange(summed_copies(parts, count_y), "sy")
+    parts = pl.pallas_call(
+        repeat_kernel,
+        out_shape=jax.ShapeDtypeStruct((count_y,) + parts.shape[1:], f32),
+        in_specs=vmem_specs(1),
+        out_specs=vmem_specs(1)[0],
+        compiler_params=params,
+        name="repeat",
+    )(parts)
+    mine = exchange(parts, "sy")
     swap = [(at, at ^ 1) for at in range(count_x)]
     other = lax.ppermute(mine, "sx", swap)
     core = (lax.axis_index("sx") % cores).astype(jnp.int32).reshape(1)

time: 130 us -> 126 us (0.969); the launches traced: 127 us -> 125 us
  starting transfers between devices: 69 us -> 62.7 us
  blocking collectives: 21.6 us -> 27.4 us
    ppermute x1, starting transfers between devices: 8.5 us -> 2.22 us  [local(): other = lax.ppermute(mine, 'sx', swap)]
    all_to_all x2 -> x1, blocking collectives: 21.6 us -> 27.4 us  [exchange(): lax.all_to_all(values, axis, 0, 0, tiled=True, axis_index_groups=groups)]
    ppermute x2, starting transfers between devices: 8.02 us -> 10.3 us  [local(): from_left = lax.ppermute(to_right, 'sx', forward_x)]
    all_to_all x2, starting transfers between devices: 29.8 us -> 27.8 us  [exchange(): lax.all_to_all(values, axis, 0, 0, tiled=True, axis_index_groups=groups)]
where the time goes in v3:
time: 126 us; the launch traced here: 125 us
  starting transfers between devices  62.7 us (50%)
  blocking collectives  27.4 us (22%)
  waiting for transfers between devices  22.6 us (18%)
  Pallas kernels  11.1 us (9%)
    all_to_all x2, starting transfers between devices, exchange(): lax.all_to_all(values, axis, 0, 0, tiled=True, axis_index_groups=groups)  27.8 us
    all_to_all x1, blocking collectives, exchange(): lax.all_to_all(values, axis, 0, 0, tiled=True, axis_index_groups=groups)  27.4 us
    ppermute x2, starting transfers between devices, local(): from_right = lax.ppermute(to_left, 'sx', backward_x)  11.8 us
    ppermute x2, starting transfers between devices, local(): from_left = lax.ppermute(to_right, 'sx', forward_x)  10.3 us
    all_to_all x2, waiting for transfers between devices, exchange(): lax.all_to_all(values, axis, 0, 0, tiled=True, axis_index_groups=groups)  8.04 us
    ppermute x2, waiting for transfers between devices, local(): from_right = lax.ppermute(to_left, 'sx', backward_x)  5.82 us
    pallas_call x1, Pallas kernels, local(): pl.pallas_call(model_kernel, out_shape=(jax.ShapeDtypeStruct((planes, 2 *...  5.36 us
    ppermute x1, starting transfers between devices, local(): from_above = lax.ppermute(down, 'sy', forward_y)  3.99 us
  transfers between devices with their start and end apart: 11, of which 10 were waited for; matrix products, arithmetic and copies ran while one was open for 1% of the time, Pallas kernels for 0%

profile of v3, /device:TPU:1, one launch (start us, length us, event | category | flops | bytes accessed | tf_op | source)
XLA Modules:
  0.0 125.3 jit_solution(13856098610077202814)
XLA Ops:
  0.6 1.1 split.1
  1.7 4.0 %collective-permute-start = (f32[4,64,128]{2,1,0:T(8,128)S(1)}, f32[4,64,128]{2,1,0:T(8,128)S(1)}, u32[]{:S(2)}, u32[]{:S(2)}) collective-permute-start(f32[4,64,128]{2,1,0:T(8,128)S(1)} %get-tuple-element.21), channel_id=1, source_target_pairs={{0,32},{32,64},{64,96},{96,128},{128,160},{160,192},{192,224},{224... | collective-permute-start | bytes 393224 | tf_op jit(solution)/shard_map/ppermute | solution.py:363
  5.7 1.3 %collective-permute-start.1 = (f32[4,64,128]{2,1,0:T(8,128)S(1)}, f32[4,64,128]{2,1,0:T(8,128)S(1)}, u32[]{:S(2)}, u32[]{:S(2)}) collective-permute-start(f32[4,64,128]{2,1,0:T(8,128)S(1)} %get-tuple-element.22), channel_id=1, source_target_pairs={{32,0},{64,32},{96,64},{128,96},{160,128},{192,160},{224,192},{256... | collective-permute-start | bytes 393224 | tf_op jit(solution)/shard_map/ppermute | solution.py:364
  7.0 0.6 collective-permute-done.above
  7.6 3.8 %collective-permute-done.1.below = f32[4,64,128]{2,1,0:T(8,128)S(1)} collective-permute-done((f32[4,64,128]{2,1,0:T(8,128)S(1)}, f32[4,64,128]{2,1,0:T(8,128)S(1)}, u32[]{:S(2)}, u32[]{:S(2)}) %collective-permute-start.1) | collective-permute-done | bytes 131104 | tf_op jit(solution)/shard_map/ppermute | solution.py:364
  11.4 0.1 pack.1
  11.6 6.0 %collective-permute-start.2 = (f32[4,128,128]{2,1,0:T(8,128)S(1)}, f32[4,128,128]{2,1,0:T(8,128)S(1)}, u32[]{:S(2)}, u32[]{:S(2)}) collective-permute-start(f32[4,128,128]{2,1,0:T(8,128)S(1)} %get-tuple-element.23), channel_id=1, source_target_pairs={{0,1},{1,2},{2,3},{3,4},{4,5},{5,6},{6,7},{7,8},{8,9},{9,10},{10,1... | collective-permute-start | bytes 786440 | tf_op jit(solution)/shard_map/ppermute | solution.py:373
  17.6 9.9 %collective-permute-start.3 = (f32[4,128,128]{2,1,0:T(8,128)S(1)}, f32[4,128,128]{2,1,0:T(8,128)S(1)}, u32[]{:S(2)}, u32[]{:S(2)}) collective-permute-start(f32[4,128,128]{2,1,0:T(8,128)S(1)} %get-tuple-element.24), channel_id=1, source_target_pairs={{1,0},{2,1},{3,2},{4,3},{5,4},{6,5},{7,6},{8,7},{9,8},{10,9},{11,1... | collective-permute-start | bytes 786440 | tf_op jit(solution)/shard_map/ppermute | solution.py:374
  27.4 0.0 collective-permute-done.2.from_left
  27.4 1.1 collective-permute-done.3.from_right
  28.6 5.4 %model.1 = (f32[4,256,128]{2,1,0:T(8,128)S(1)}, f32[4,128,128]{2,1,0:T(8,128)S(1)}, f32[4,128,128]{2,1,0:T(8,128)S(1)}, f32[576,1,128]{2,1,0:T(1,128)}) custom-call(s32[2,2]{1,0:T(2,128)} %bitcast.13, f32[2,8]{1,0:T(2,128)} %bitcast.14, f32[4,128,128]{2,1,0:T(8,128)S(1)} %get-tuple-element.20.own, f32[4,64,128]{2,1,0:T(8,128)S(1)} %collective-permute-done.above, ...), custom_call_target="tpu_custom_call" | custom-call | tf_op jit(solution)/shard_map/model/pallas_call | solution.py:376
  34.0 8.9 %all-to-all-start = ((f32[576,1,128]{2,1,0:T(1,128)}), f32[576,1,128]{2,1,0:T(1,128)S(1)}, u32[]{:S(2)}, u32[]{:S(2)}) async-start(f32[576,1,128]{2,1,0:T(1,128)} %get-tuple-element.26), calls=%async_computation | async-start | bytes 589824 | tf_op jit(solution)/shard_map/all_to_all | solution.py:326
  42.9 4.3 %collective-permute-start.4 = (f32[4,128,128]{2,1,0:T(8,128)S(1)}, f32[4,128,128]{2,1,0:T(8,128)S(1)}, u32[]{:S(2)}, u32[]{:S(2)}) collective-permute-start(f32[4,128,128]{2,1,0:T(8,128)S(1)} %get-tuple-element.27), channel_id=1, source_target_pairs={{0,1},{1,2},{2,3},{3,4},{4,5},{5,6},{6,7},{7,8},{8,9},{9,10},{10,1... | collective-permute-start | bytes 786440 | tf_op jit(solution)/shard_map/ppermute | solution.py:413
  47.3 1.9 %collective-permute-start.5 = (f32[4,128,128]{2,1,0:T(8,128)S(1)}, f32[4,128,128]{2,1,0:T(8,128)S(1)}, u32[]{:S(2)}, u32[]{:S(2)}) collective-permute-start(f32[4,128,128]{2,1,0:T(8,128)S(1)} %get-tuple-element.28), channel_id=1, source_target_pairs={{1,0},{2,1},{3,2},{4,3},{5,4},{6,5},{7,6},{8,7},{9,8},{10,9},{11,1... | collective-permute-start | bytes 786440 | tf_op jit(solution)/shard_map/ppermute | solution.py:414
  49.2 1.4 %collective-permute-done.4.from_left = f32[4,128,128]{2,1,0:T(8,128)S(1)} collective-permute-done((f32[4,128,128]{2,1,0:T(8,128)S(1)}, f32[4,128,128]{2,1,0:T(8,128)S(1)}, u32[]{:S(2)}, u32[]{:S(2)}) %collective-permute-start.4) | collective-permute-done | bytes 262176 | tf_op jit(solution)/shard_map/ppermute | solution.py:413
  50.6 4.7 %collective-permute-done.5.from_right = f32[4,128,128]{2,1,0:T(8,128)S(1)} collective-permute-done((f32[4,128,128]{2,1,0:T(8,128)S(1)}, f32[4,128,128]{2,1,0:T(8,128)S(1)}, u32[]{:S(2)}, u32[]{:S(2)}) %collective-permute-start.5) | collective-permute-done | bytes 262176 | tf_op jit(solution)/shard_map/ppermute | solution.py:414
  55.2 1.4 %all-to-all-done.gathered = f32[576,1,128]{2,1,0:T(1,128)S(1)} async-done(((f32[576,1,128]{2,1,0:T(1,128)}), f32[576,1,128]{2,1,0:T(1,128)S(1)}, u32[]{:S(2)}, u32[]{:S(2)}) %all-to-all-start) | async-done | bytes 294944 | tf_op jit(solution)/shard_map/all_to_all | solution.py:326
  56.6 1.1 mix.1
  57.7 18.9 %all-to-all-start.1 = ((f32[16,4,8,128]{3,2,1,0:T(8,128)}), f32[16,4,8,128]{3,2,1,0:T(8,128)S(1)}, u32[]{:S(2)}, u32[]{:S(2)}) async-start(f32[16,4,8,128]{3,2,1,0:T(8,128)} %mix.1), calls=%async_computation.1 | async-start | bytes 524288 | tf_op jit(solution)/shard_map/all_to_all | solution.py:326
  76.6 0.1 merge.1
  76.8 1.3 %collective-permute-start.6 = (f32[4,64,128]{2,1,0:T(8,128)S(1)}, f32[4,64,128]{2,1,0:T(8,128)S(1)}, u32[]{:S(2)}, u32[]{:S(2)}) collective-permute-start(f32[4,64,128]{2,1,0:T(8,128)S(1)} %get-tuple-element.33), channel_id=1, source_target_pairs={{32,0},{64,32},{96,64},{128,96},{160,128},{192,160},{224,192},{256... | collective-permute-start | bytes 393224 | tf_op jit(solution)/shard_map/ppermute | solution.py:434
  78.1 4.0 %collective-permute-start.7 = (f32[4,64,128]{2,1,0:T(8,128)S(1)}, f32[4,64,128]{2,1,0:T(8,128)S(1)}, u32[]{:S(2)}, u32[]{:S(2)}) collective-permute-start(f32[4,64,128]{2,1,0:T(8,128)S(1)} %get-tuple-element.34), channel_id=1, source_target_pairs={{0,32},{32,64},{64,96},{96,128},{128,160},{160,192},{192,224},{224... | collective-permute-start | bytes 393224 | tf_op jit(solution)/shard_map/ppermute | solution.py:435
  82.1 1.2 collective-permute-done.6
  83.3 0.9 collective-permute-done.7
  84.2 6.7 %all-to-all-done.1.parts = f32[16,4,8,128]{3,2,1,0:T(8,128)S(1)} async-done(((f32[16,4,8,128]{3,2,1,0:T(8,128)}), f32[16,4,8,128]{3,2,1,0:T(8,128)S(1)}, u32[]{:S(2)}, u32[]{:S(2)}) %all-to-all-start.1) | async-done | bytes 262176 | tf_op jit(solution)/shard_map/all_to_all | solution.py:326
  90.8 0.1 repeat.1
  90.9 0.0 copy-start
  90.9 27.4 %all_to_all.15.refs_1_ = f32[32,4,8,128]{3,2,1,0:T(8,128)S(1)} all-to-all(f32[32,4,8,128]{3,2,1,0:T(8,128)S(1)} %repeat.1), channel_id=1, replica_groups=mesh['sy'=32,'sx'=32] {'sy'}, dimensions={0} | all-to-all | bytes 1048576 | tf_op jit(solution)/shard_map/all_to_all | solution.py:326
  118.4 2.2 %collective-permute-start.8 = (f32[32,4,8,128]{3,2,1,0:T(8,128)S(1)}, f32[32,4,8,128]{3,2,1,0:T(8,128)S(1)}, u32[]{:S(2)}, u32[]{:S(2)}) collective-permute-start(f32[32,4,8,128]{3,2,1,0:T(8,128)S(1)} %all_to_all.15.refs_1_), channel_id=1, source_target_pairs={{0,1},{1,0},{2,3},{3,2},{4,5},{5,4},{6,7},{7,6},{8,9},{9,8},{10,11... | collective-permute-start | bytes 1572872 | tf_op jit(solution)/shard_map/ppermute | solution.py:447
  120.6 0.7 maximum_add_fusion
  121.3 0.8 collective-permute-done.8.refs_2_
  122.2 0.0 copy-done
  122.2 3.2 %orthonormal.1 = f32[8,32,8,128]{3,2,1,0:T(8,128)} custom-call(s32[1]{0:T(128)} %bitcast.5.refs_0_, f32[32,4,8,128]{3,2,1,0:T(8,128)S(1)} %all_to_all.15.refs_1_, f32[32,4,8,128]{3,2,1,0:T(8,128)S(1)} %collective-permute-done.8.refs_2_, f32[8,32,8,128]{3,2,1,0:T(8,128)S(1)} %bitcast.8), custom_call_target="tpu_custom_call" | custom-call | tf_op jit(solution)/shard_map/orthonormal/pallas_call | solution.py:455
Async XLA Ops:
  1.7 5.9 %collective-permute-start = (f32[4,64,128]{2,1,0:T(8,128)S(1)}, f32[4,64,128]{2,1,0:T(8,128)S(1)}, u32[]{:S(2)}, u32[]{:S(2)}) collective-permute-start(f32[4,64,128]{2,1,0:T(8,128)S(1)} %get-tuple-element.21), channel_id=1, source_target_pairs={{0,32},{32,64},{64,96},{96,128},{128,160},{160,192},{192,224},{224... | collective-permute-start | bytes 393224 | tf_op jit(solution)/shard_map/ppermute | solution.py:363
  5.7 5.7 %collective-permute-start.1 = (f32[4,64,128]{2,1,0:T(8,128)S(1)}, f32[4,64,128]{2,1,0:T(8,128)S(1)}, u32[]{:S(2)}, u32[]{:S(2)}) collective-permute-start(f32[4,64,128]{2,1,0:T(8,128)S(1)} %get-tuple-element.22), channel_id=1, source_target_pairs={{32,0},{64,32},{96,64},{128,96},{160,128},{192,160},{224,192},{256... | collective-permute-start | bytes 393224 | tf_op jit(solution)/shard_map/ppermute | solution.py:364
  11.6 15.9 %collective-permute-start.2 = (f32[4,128,128]{2,1,0:T(8,128)S(1)}, f32[4,128,128]{2,1,0:T(8,128)S(1)}, u32[]{:S(2)}, u32[]{:S(2)}) collective-permute-start(f32[4,128,128]{2,1,0:T(8,128)S(1)} %get-tuple-element.23), channel_id=1, source_target_pairs={{0,1},{1,2},{2,3},{3,4},{4,5},{5,6},{6,7},{7,8},{8,9},{9,10},{10,1... | collective-permute-start | bytes 786440 | tf_op jit(solution)/shard_map/ppermute | solution.py:373
  17.6 11.0 %collective-permute-start.3 = (f32[4,128,128]{2,1,0:T(8,128)S(1)}, f32[4,128,128]{2,1,0:T(8,128)S(1)}, u32[]{:S(2)}, u32[]{:S(2)}) collective-permute-start(f32[4,128,128]{2,1,0:T(8,128)S(1)} %get-tuple-element.24), channel_id=1, source_target_pairs={{1,0},{2,1},{3,2},{4,3},{5,4},{6,5},{7,6},{8,7},{9,8},{10,9},{11,1... | collective-permute-start | bytes 786440 | tf_op jit(solution)/shard_map/ppermute | solution.py:374
  34.0 22.7 %all-to-all-start = ((f32[576,1,128]{2,1,0:T(1,128)}), f32[576,1,128]{2,1,0:T(1,128)S(1)}, u32[]{:S(2)}, u32[]{:S(2)}) async-start(f32[576,1,128]{2,1,0:T(1,128)} %get-tuple-element.26), calls=%async_computation | async-start | bytes 589824 | tf_op jit(solution)/shard_map/all_to_all | solution.py:326
  42.9 7.7 %collective-permute-start.4 = (f32[4,128,128]{2,1,0:T(8,128)S(1)}, f32[4,128,128]{2,1,0:T(8,128)S(1)}, u32[]{:S(2)}, u32[]{:S(2)}) collective-permute-start(f32[4,128,128]{2,1,0:T(8,128)S(1)} %get-tuple-element.27), channel_id=1, source_target_pairs={{0,1},{1,2},{2,3},{3,4},{4,5},{5,6},{6,7},{7,8},{8,9},{9,10},{10,1... | collective-permute-start | bytes 786440 | tf_op jit(solution)/shard_map/ppermute | solution.py:413
  47.3 8.0 %collective-permute-start.5 = (f32[4,128,128]{2,1,0:T(8,128)S(1)}, f32[4,128,128]{2,1,0:T(8,128)S(1)}, u32[]{:S(2)}, u32[]{:S(2)}) collective-permute-start(f32[4,128,128]{2,1,0:T(8,128)S(1)} %get-tuple-element.28), channel_id=1, source_target_pairs={{1,0},{2,1},{3,2},{4,3},{5,4},{6,5},{7,6},{8,7},{9,8},{10,9},{11,1... | collective-permute-start | bytes 786440 | tf_op jit(solution)/shard_map/ppermute | solution.py:414
  57.7 33.1 %all-to-all-start.1 = ((f32[16,4,8,128]{3,2,1,0:T(8,128)}), f32[16,4,8,128]{3,2,1,0:T(8,128)S(1)}, u32[]{:S(2)}, u32[]{:S(2)}) async-start(f32[16,4,8,128]{3,2,1,0:T(8,128)} %mix.1), calls=%async_computation.1 | async-start | bytes 524288 | tf_op jit(solution)/shard_map/all_to_all | solution.py:326
  76.8 6.5 %collective-permute-start.6 = (f32[4,64,128]{2,1,0:T(8,128)S(1)}, f32[4,64,128]{2,1,0:T(8,128)S(1)}, u32[]{:S(2)}, u32[]{:S(2)}) collective-permute-start(f32[4,64,128]{2,1,0:T(8,128)S(1)} %get-tuple-element.33), channel_id=1, source_target_pairs={{32,0},{64,32},{96,64},{128,96},{160,128},{192,160},{224,192},{256... | collective-permute-start | bytes 393224 | tf_op jit(solution)/shard_map/ppermute | solution.py:434
  78.1 6.1 %collective-permute-start.7 = (f32[4,64,128]{2,1,0:T(8,128)S(1)}, f32[4,64,128]{2,1,0:T(8,128)S(1)}, u32[]{:S(2)}, u32[]{:S(2)}) collective-permute-start(f32[4,64,128]{2,1,0:T(8,128)S(1)} %get-tuple-element.34), channel_id=1, source_target_pairs={{0,32},{32,64},{64,96},{96,128},{128,160},{160,192},{192,224},{224... | collective-permute-start | bytes 393224 | tf_op jit(solution)/shard_map/ppermute | solution.py:435
  90.9 31.3 %copy-start = (f32[8,2,128,128]{3,2,1,0:T(8,128)S(1)}, f32[8,2,128,128]{3,2,1,0:T(8,128)}, u32[]{:S(2)}) copy-start(f32[8,2,128,128]{3,2,1,0:T(8,128)} %basis_in.1) | copy-start | bytes 3145732
  118.4 3.8 %collective-permute-start.8 = (f32[32,4,8,128]{3,2,1,0:T(8,128)S(1)}, f32[32,4,8,128]{3,2,1,0:T(8,128)S(1)}, u32[]{:S(2)}, u32[]{:S(2)}) collective-permute-start(f32[32,4,8,128]{3,2,1,0:T(8,128)S(1)} %all_to_all.15.refs_1_), channel_id=1, source_target_pairs={{0,1},{1,0},{2,3},{3,2},{4,5},{5,4},{6,7},{7,6},{8,9},{9,8},{10,11... | collective-permute-start | bytes 1572872 | tf_op jit(solution)/shard_map/ppermute | solution.py:447

commit v4 on v3

--- a/solution.py
+++ b/solution.py
@@ -47,9 +47,11 @@
 def dot3(left, right):
     left_high, left_low = left
     right_high, right_low = right
-    total = jnp.dot(left_high, right_low, preferred_element_type=jnp.float32)
-    total = total + jnp.dot(left_low, right_high, preferred_element_type=jnp.float32)
-    return total + jnp.dot(left_high, right_high, preferred_element_type=jnp.float32)
+    return jnp.dot(
+        jnp.concatenate([left_high, left_low, left_high], axis=1),
+        jnp.concatenate([right_low, right_high, right_high], axis=0),
+        preferred_element_type=jnp.float32,
+    )
 
 
 def halves(values):
@@ -117,32 +119,41 @@
     to_right[...] = jnp.where(near, second, first)
 
 
-def merge_kernel(tall, from_left, from_right, up, middle, down):
-    n = tall.shape[-1]
+def merge_kernel(wide, from_above, from_below, middle, to_left, to_right):
+    n = middle.shape[-1]
     half = n // 2
+    upper = wide[:, :half] + from_above[...]
+    lower = wide[:, half:] + from_below[...]
+    middle[:, :half] = upper[:, :, :n]
+    middle[:, half:] = lower[:, :, :n]
+    first = upper[:, :, n:]
+    second = roll_planes(lower[:, :, n:])
+    near = near_lanes(first.shape)
+    to_right[...] = jnp.where(near, first, second)
+    to_left[...] = jnp.where(near, second, first)
+
+
+def finish_kernel(middle, from_left, from_right, out):
+    half = middle.shape[1] // 2
     near = near_lanes(from_left.shape)
-    first = tall[:, :n] + jnp.where(near, from_left[...], from_right[...])
-    second = tall[:, n:] + roll_planes(jnp.where(near, from_right[...], from_left[...]))
-    up[...] = first[:, :half]
-    middle[:, :half] = first[:, half:]
-    middle[:, half:] = second[:, :half]
-    down[...] = second[:, half:]
-
-
-def model_kernel(
-    positions_in, weights_in, own, above, below, from_left, from_right, mean_in, basis_in,
-    measured_in, table_in, tall, to_left, to_right, probe_grad,
-    frame, grads, positions, weights, mean, basis, measured, table, sems,
+    left, right = from_left[...], from_right[...]
+    out[:, :half] = middle[:, :half] + jnp.where(near, left, right)
+    out[:, half:] = middle[:, half:] + roll_planes(jnp.where(near, right, left))
+
+
+def prepare_kernel(
+    after, weights_in, mean_in, basis_in, measured_in, table_in,
+    probes, forms, measured, packed, weights, mean, basis, table, sems,
 ):
+    del after
     copies = [
         pltpu.make_async_copy(source, target, sems.at[at])
         for at, (source, target) in enumerate(
             [
-                (positions_in, positions),
                 (weights_in, weights),
+                (table_in, table),
                 (mean_in, mean),
                 (basis_in, basis),
-                (table_in, table),
                 (measured_in, measured),
             ]
         )
@@ -150,8 +161,42 @@
     for copy in copies:
         copy.start()
     n = mean.shape[-1]
+    modes = basis.shape[0]
+    slots = range(2)
+    copies[0].wait()
+    lane_at = lax.broadcasted_iota(jnp.int32, (1, n), 1)
+    row = jnp.zeros((1, n), jnp.float32)
+    for slot in slots:
+        for mode in range(modes):
+            row = jnp.where(lane_at == slot * modes + mode, weights[slot, mode], row)
+    packed[...] = row
+    copies[1].wait()
+    for at in range(2):
+        for part in range(2):
+            form, form_t = block_forms(table[2 * at, part], table[2 * at + 1, part])
+            forms[2 * at, part] = form
+            forms[2 * at + 1, part] = form_t
+    copies[2].wait()
+    copies[3].wait()
+    for slot in slots:
+        real = mean[0]
+        imag = mean[1]
+        for mode in range(modes):
+            real = real + weights[slot, mode] * basis[mode, 0]
+            imag = imag + weights[slot, mode] * basis[mode, 1]
+        probes[slot, 0] = real
+        probes[slot, 1] = imag
+    copies[4].wait()
+
+
+def model_kernel(
+    positions_in, own, above, below, from_left, from_right, probes_in, forms, measured, packed,
+    probe_grad, terms, frame, positions, sem,
+):
+    copy = pltpu.make_async_copy(positions_in, positions, sem)
+    copy.start()
+    n = measured.shape[-1]
     half = n // 2
-    modes = basis.shape[0]
     near = near_lanes(own.shape)
     frame[:, 0:half, 0:n] = above[...]
     frame[:, half : half + n, 0:n] = own[...]
@@ -160,14 +205,13 @@
     frame[:, n : 2 * n, n : 2 * n] = roll_planes(
         jnp.where(near, from_left[...], from_right[...])
     )
-    grads[...] = jnp.zeros(grads.shape, jnp.float32)
     slots = range(2)
-    copies[0].wait()
+    copy.wait()
     rows = [positions[slot, 0] for slot in slots]
+    cols = [positions[slot, 1] for slot in slots]
     offsets = [row & 7 for row in rows]
     bases = [pl.multiple_of(row - offset, 8) for row, offset in zip(rows, offsets)]
     span = n + 8
-    cols = [positions[slot, 1] for slot in slots]
 
     def window(slot, plane):
         strip = frame[plane, pl.ds(bases[slot], span), :]
@@ -179,16 +223,8 @@
         [(1.0 + window(slot, 2 * layer), window(slot, 2 * layer + 1)) for slot in slots]
         for layer in range(2)
     ]
-    for at in (1, 2, 3):
-        copies[at].wait()
-    probes = []
-    for slot in slots:
-        real = mean[0]
-        imag = mean[1]
-        for mode in range(modes):
-            real = real + weights[slot, mode] * basis[mode, 0]
-            imag = imag + weights[slot, mode] * basis[mode, 1]
-        probes.append((real, imag))
+    probes = [(probes_in[slot, 0], probes_in[slot, 1]) for slot in slots]
+    dft, dft_t, move, move_t = [(forms[at, 0], forms[at, 1]) for at in range(4)]
 
     def times(first, second):
         return [(a * c - b * d, a * d + b * c) for (a, b), (c, d) in zip(first, second)]
@@ -196,16 +232,13 @@
     def conj_times(first, second):
         return [(a * c + b * d, a * d - b * c) for (a, b), (c, d) in zip(first, second)]
 
-    copies[4].wait()
-    dft_high, dft_t_high = block_forms(table[0, 0], table[1, 0])
-    dft_low, dft_t_low = block_forms(table[0, 1], table[1, 1])
-    move_high, move_t_high = block_forms(table[2, 0], table[3, 0])
-    move_low, move_t_low = block_forms(table[2, 1], table[3, 1])
-    dft, dft_t = (dft_high, dft_low), (dft_t_high, dft_t_low)
-    move, move_t = (move_high, move_low), (move_t_high, move_t_low)
+    def keep(layer, pairs):
+        for slot in slots:
+            for part in range(2):
+                terms[layer, slot, part] = pairs[slot][part]
+
     entered = both_sides(times(probes, transmit[0]), move, move_t)
     far = both_sides(times(entered, transmit[1]), dft, dft_t)
-    copies[5].wait()
     chi = []
     for slot in slots:
         real, imag = far[slot]
@@ -213,32 +246,12 @@
         ratio = measured[slot] / modulus
         chi.append((real - real * ratio, imag - imag * ratio))
     back = both_sides(chi, dft_t, dft)
-
-    def deposit(layer, terms):
-        for slot in slots:
-            for part in range(2):
-                padded = jnp.concatenate(
-                    [terms[slot][part], jnp.zeros((8, n), jnp.float32)], axis=0
-                )
-                lowered = pltpu.roll(padded, offsets[slot], 0)
-                padded = jnp.concatenate(
-                    [lowered, jnp.zeros((span, n), jnp.float32)], axis=1
-                )
-                shifted = pltpu.roll(padded, (cols[slot] + 3 * half) & (2 * n - 1), 1)
-                at = (2 * layer + part, pl.ds(bases[slot], span), slice(None))
-                grads[at] = grads[at] + shifted
-
-    deposit(1, conj_times(entered, back))
+    keep(1, conj_times(entered, back))
     back = both_sides(conj_times(transmit[1], back), move_t, move)
-    deposit(0, conj_times(probes, back))
+    keep(0, conj_times(probes, back))
     back = conj_times(transmit[0], back)
     blocks = n // 8
     upper_rows = lax.broadcasted_iota(jnp.int32, (8, n), 0) < 4
-    lane_at = lax.broadcasted_iota(jnp.int32, (1, n), 1)
-    packed = jnp.zeros((1, n), jnp.float32)
-    for slot in slots:
-        for mode in range(modes):
-            packed = jnp.where(lane_at == slot * modes + mode, weights[slot, mode], packed)
     for part in range(2):
         for block in range(blocks):
             first = back[0][part][8 * block : 8 * block + 8]
@@ -247,16 +260,37 @@
             probe_grad[pl.ds(at, 8), 0, :] = jnp.where(
                 upper_rows, first, pltpu.roll(second, 4, 0)
             )
-            probe_grad[at + 8] = packed
+            probe_grad[at + 8] = packed[...]
             probe_grad[pl.ds(at + PIECE, 8), 0, :] = jnp.where(
                 upper_rows, pltpu.roll(first, 4, 0), second
             )
-            probe_grad[at + PIECE + 8] = packed
-    tall[...] = grads[:, :, 0:n]
-    first = grads[:, 0:n, n : 2 * n]
-    second = roll_planes(grads[:, n : 2 * n, n : 2 * n])
-    to_right[...] = jnp.where(near, first, second)
-    to_left[...] = jnp.where(near, second, first)
+            probe_grad[at + PIECE + 8] = packed[...]
+
+
+def deposit_kernel(positions_in, terms, up, wide, down, grads, positions, sem):
+    copy = pltpu.make_async_copy(positions_in, positions, sem)
+    copy.start()
+    n = terms.shape[-1]
+    half = n // 2
+    span = n + 8
+    grads[...] = jnp.zeros(grads.shape, jnp.float32)
+    copy.wait()
+    for slot in range(2):
+        row, col = positions[slot, 0], positions[slot, 1]
+        offset = row & 7
+        base = pl.multiple_of(row - offset, 8)
+        for plane in range(4):
+            padded = jnp.concatenate(
+                [terms[plane // 2, slot, plane % 2], jnp.zeros((8, n), jnp.float32)], axis=0
+            )
+            lowered = pltpu.roll(padded, offset, 0)
+            padded = jnp.concatenate([lowered, jnp.zeros((span, n), jnp.float32)], axis=1)
+            shifted = pltpu.roll(padded, (col + 3 * half) & (2 * n - 1), 1)
+            at = (plane, pl.ds(base, span), slice(None))
+            grads[at] = grads[at] + shifted
+    up[...] = grads[:, 0:half]
+    wide[...] = grads[:, half : half + n]
+    down[...] = grads[:, half + n : 2 * n]
 
 
 def mix_kernel(gathered, out, ordered):
@@ -362,6 +396,33 @@
     )(away(obj_delta.reshape(planes, n, n)))
     above = lax.ppermute(lower, "sy", forward_y)
     below = lax.ppermute(upper, "sy", backward_y)
+    bf16 = jnp.bfloat16
+    probes, forms, measured, packed = pl.pallas_call(
+        prepare_kernel,
+        out_shape=(
+            jax.ShapeDtypeStruct((per_tile, 2, n, n), f32),
+            jax.ShapeDtypeStruct((4, 2, 2 * n, 2 * n), bf16),
+            jax.ShapeDtypeStruct((per_tile, n, n), f32),
+            jax.ShapeDtypeStruct((1, n), f32),
+        ),
+        in_specs=vmem_specs(1) + [distant] * 5,
+        out_specs=tuple(vmem_specs(4)),
+        scratch_shapes=[
+            pltpu.SMEM((per_tile, modes), f32),
+            pltpu.VMEM((2, n, n), f32),
+            pltpu.VMEM((modes, 2, n, n), f32),
+            pltpu.VMEM((4, 2, n, n), bf16),
+            pltpu.SemaphoreType.DMA((5,)),
+        ],
+        compiler_params=params,
+        name="prepare",
+    )(
+        upper, away(mode_weights[0, 0]), away(probe_mean), away(probe_basis),
+        away(amplitudes[0, 0]), away(jnp.asarray(tables(n))),
+    )
+    above, below, probes, forms, measured, packed = lax.optimization_barrier(
+        (above, below, probes, forms, measured, packed)
+    )
     to_left, to_right = pl.pallas_call(
         pack_kernel,
         out_shape=(block, block),
@@ -373,34 +434,39 @@
     from_left = lax.ppermute(to_right, "sx", forward_x)
     from_right = lax.ppermute(to_left, "sx", backward_x)
 
-    tall, to_left, to_right, probe_grad = pl.pallas_call(
+    probe_grad, terms = pl.pallas_call(
         model_kernel,
         out_shape=(
-            jax.ShapeDtypeStruct((planes, 2 * n, n), f32),
-            block,
-            block,
             jax.ShapeDtypeStruct((4 * blocks * PIECE, 1, n), f32),
+            jax.ShapeDtypeStruct((2, per_tile, 2, n, n), f32),
         ),
-        in_specs=[distant] * 2 + vmem_specs(5) + [distant] * 4,
-        out_specs=tuple(vmem_specs(4)),
+        in_specs=[distant] + vmem_specs(9),
+        out_specs=tuple(vmem_specs(2)),
         scratch_shapes=[
             pltpu.VMEM((planes, 2 * n, 2 * n), f32),
+            pltpu.SMEM((per_tile, 2), jnp.int32),
+            pltpu.SemaphoreType.DMA(()),
+        ],
+        compiler_params=params,
+        name="model",
+    )(
+        away(positions[0, 0]), own, above, below, from_left, from_right,
+        probes, forms, measured, packed,
+    )
+    wide_edge = jax.ShapeDtypeStruct((planes, half, 2 * n), f32)
+    up, wide, down = pl.pallas_call(
+        deposit_kernel,
+        out_shape=(wide_edge, jax.ShapeDtypeStruct((planes, n, 2 * n), f32), wide_edge),
+        in_specs=[distant] + vmem_specs(1),
+        out_specs=tuple(vmem_specs(3)),
+        scratch_shapes=[
             pltpu.VMEM((planes, 2 * n, 2 * n), f32),
             pltpu.SMEM((per_tile, 2), jnp.int32),
-            pltpu.SMEM((per_tile, modes), f32),
-            pltpu.VMEM((2, n, n), f32),
-            pltpu.VMEM((modes, 2, n, n), f32),
-            pltpu.VMEM((per_tile, n, n), f32),
-            pltpu.VMEM((4, 2, n, n), jnp.bfloat16),
-            pltpu.SemaphoreType.DMA((6,)),
+            pltpu.SemaphoreType.DMA(()),
         ],
         compiler_params=params,
-        name="model",
-    )(
-        away(positions[0, 0]), away(mode_weights[0, 0]), own, above, below, from_left, from_right,
-        away(probe_mean), away(probe_basis), away(amplitudes[0, 0]),
-        away(jnp.asarray(tables(n))),
-    )
+        name="deposit",
+    )(away(positions[0, 0]), terms)
 
     cores = 2
     per_core = count_x // cores
@@ -410,9 +476,6 @@
         for at in range(per_core)
     ]
     gathered = exchange(probe_grad, ("sy", "sx"), layers)
-    from_left = lax.ppermute(to_right, "sx", forward_x)
-    from_right = lax.ppermute(to_left, "sx", backward_x)
-    gathered, from_left, from_right = lax.optimization_barrier((gathered, from_left, from_right))
     parts = pl.pallas_call(
         mix_kernel,
         out_shape=jax.ShapeDtypeStruct((per_core, modes // 2, 8, n), f32),
@@ -423,17 +486,17 @@
         name="mix",
     )(gathered)
     parts = exchange(parts, "sx", columns)
-    up, middle, down = pl.pallas_call(
-        merge_kernel,
-        out_shape=(edge, block, edge),
-        in_specs=vmem_specs(3),
-        out_specs=tuple(vmem_specs(3)),
-        compiler_params=params,
-        name="merge",
-    )(tall, from_left, from_right)
     from_below = lax.ppermute(up, "sy", backward_y)
     from_above = lax.ppermute(down, "sy", forward_y)
     parts, from_below, from_above = lax.optimization_barrier((parts, from_below, from_above))
+    middle, to_left, to_right = pl.pallas_call(
+        merge_kernel,
+        out_shape=(block, edge, edge),
+        in_specs=vmem_specs(3),
+        out_specs=tuple(vmem_specs(3)),
+        compiler_params=params,
+        name="merge",
+    )(wide, from_above, from_below)
     parts = pl.pallas_call(
         repeat_kernel,
         out_shape=jax.ShapeDtypeStruct((count_y,) + parts.shape[1:], f32),
@@ -443,6 +506,17 @@
         name="repeat",
     )(parts)
     mine = exchange(parts, "sy")
+    from_left = lax.ppermute(to_right, "sx", forward_x)
+    from_right = lax.ppermute(to_left, "sx", backward_x)
+    obj_grad = pl.pallas_call(
+        finish_kernel,
+        out_shape=block,
+        in_specs=vmem_specs(3),
+        out_specs=vmem_specs(1)[0],
+        compiler_params=params,
+        name="finish",
+    )(middle, from_left, from_right)
+    mine, obj_grad = lax.optimization_barrier((mine, obj_grad))
     swap = [(at, at ^ 1) for at in range(count_x)]
     other = lax.ppermute(mine, "sx", swap)
     core = (lax.axis_index("sx") % cores).astype(jnp.int32).reshape(1)
@@ -462,7 +536,6 @@
     )(core, mine, other, probe_basis.reshape(modes, 2 * blocks, 8, n))
     new_basis = new_basis.reshape(probe_basis.shape)
 
-    obj_grad = middle + jnp.concatenate([from_above, from_below], axis=1)
     return (obj_grad.reshape(obj_delta.shape), new_basis)
 
 

time: 126 us -> 122 us (0.968)
  waiting for transfers between devices: 22.6 us -> 15.5 us
  starting transfers between devices: 62.7 us -> 68.8 us
  blocking collectives: 27.4 us -> 22.2 us
  Pallas kernels: 11.1 us -> 13.6 us
    all_to_all x1, blocking collectives: 27.4 us -> 22.2 us  [exchange(): lax.all_to_all(values, axis, 0, 0, tiled=True, axis_index_groups=groups)]
    all_to_all x2, waiting for transfers between devices: 8.04 us -> 2.94 us  [exchange(): lax.all_to_all(values, axis, 0, 0, tiled=True, axis_index_groups=groups)]
    ppermute x1, starting transfers between devices: 2.22 us -> 6.42 us  [local(): other = lax.ppermute(mine, 'sx', swap)]
    ppermute x1, waiting for transfers between devices: 3.79 us -> 0.01 us  [local(): below = lax.ppermute(upper, 'sy', backward_y)]
    all_to_all x2, starting transfers between devices: 27.8 us -> 24.5 us  [exchange(): lax.all_to_all(values, axis, 0, 0, tiled=True, axis_index_groups=groups)]
    ppermute x1, waiting for transfers between devices: 1.24 us -> 4.04 us  [local(): from_below = lax.ppermute(up, 'sy', backward_y)]
    ppermute x2, starting transfers between devices: 10.3 us -> 12.9 us  [local(): from_left = lax.ppermute(to_right, 'sx', forward_x)]
    ppermute x2, starting transfers between devices: 11.8 us -> 13.9 us  [local(): from_right = lax.ppermute(to_left, 'sx', backward_x)]
  transfers between devices with their start and end apart: 11 -> 11, of which waited for: 10 -> 7; matrix products, arithmetic and copies ran while one was open for 1% -> 0% of each run, Pallas kernels for 0% -> 3%
where the time goes in v4:
time: 122 us; the launch traced here: 121 us
  starting transfers between devices  68.8 us (56%)
  blocking collectives  22.2 us (18%)
  waiting for transfers between devices  15.5 us (13%)
  Pallas kernels  13.6 us (11%)
    all_to_all x2, starting transfers between devices, exchange(): lax.all_to_all(values, axis, 0, 0, tiled=True, axis_index_groups=groups)  24.5 us
    all_to_all x1, blocking collectives, exchange(): lax.all_to_all(values, axis, 0, 0, tiled=True, axis_index_groups=groups)  22.2 us
    ppermute x2, starting transfers between devices, local(): from_right = lax.ppermute(to_left, 'sx', backward_x)  13.9 us
    ppermute x2, starting transfers between devices, local(): from_left = lax.ppermute(to_right, 'sx', forward_x)  12.9 us
    ppermute x1, starting transfers between devices, local(): other = lax.ppermute(mine, 'sx', swap)  6.42 us
    ppermute x2, waiting for transfers between devices, local(): from_right = lax.ppermute(to_left, 'sx', backward_x)  5.77 us
    ppermute x1, starting transfers between devices, local(): above = lax.ppermute(lower, 'sy', forward_y)  4.58 us
    ppermute x1, waiting for transfers between devices, local(): from_below = lax.ppermute(up, 'sy', backward_y)  4.04 us
  transfers between devices with their start and end apart: 11, of which 7 were waited for; matrix products, arithmetic and copies ran while one was open for 0% of the time, Pallas kernels for 3%

profile of v4, /device:TPU:1, one launch (start us, length us, event | category | flops | bytes accessed | tf_op | source)
XLA Modules:
  0.0 121.0 jit_solution(5980247834015330978)
XLA Ops:
  0.6 1.1 split.1
  1.7 1.3 %collective-permute-start.1 = (f32[4,64,128]{2,1,0:T(8,128)S(1)}, f32[4,64,128]{2,1,0:T(8,128)S(1)}, u32[]{:S(2)}, u32[]{:S(2)}) collective-permute-start(f32[4,64,128]{2,1,0:T(8,128)S(1)} %get-tuple-element.32.after), channel_id=1, source_target_pairs={{32,0},{64,32},{96,64},{128,96},{160,128},{192,160},{224,192},{256... | collective-permute-start | bytes 393224 | tf_op jit(solution)/shard_map/ppermute | solution.py:398
  3.0 4.6 %collective-permute-start = (f32[4,64,128]{2,1,0:T(8,128)S(1)}, f32[4,64,128]{2,1,0:T(8,128)S(1)}, u32[]{:S(2)}, u32[]{:S(2)}) collective-permute-start(f32[4,64,128]{2,1,0:T(8,128)S(1)} %get-tuple-element.31), channel_id=1, source_target_pairs={{0,32},{32,64},{64,96},{96,128},{128,160},{160,192},{192,224},{224... | collective-permute-start | bytes 393224 | tf_op jit(solution)/shard_map/ppermute | solution.py:397
  7.6 1.6 %prepare.1 = (f32[2,2,128,128]{3,2,1,0:T(8,128)S(1)}, bf16[4,2,256,256]{3,2,1,0:T(8,128)(2,1)S(1)}, f32[2,128,128]{2,1,0:T(8,128)S(1)}, f32[1,128]{1,0:T(1,128)S(1)}) custom-call(f32[4,64,128]{2,1,0:T(8,128)S(1)} %get-tuple-element.32.after, f32[2,8]{1,0:T(2,128)} %bitcast.15, f32[2,128,128]{2,1,0:T(8,128)} %mean_in.1, f32[8,2,128,128]{3,2,1,0:T(8,128)} %basis_in.1, ...), custom_call_target="tpu_custom_call" | custom-call | tf_op jit(solution)/shard_map/prepare/pallas_call | solution.py:400
  9.2 0.0 collective-permute-done.1.below
  9.2 0.3 collective-permute-done.above
  9.6 0.1 pack.1
  9.7 5.9 %collective-permute-start.2 = (f32[4,128,128]{2,1,0:T(8,128)S(1)}, f32[4,128,128]{2,1,0:T(8,128)S(1)}, u32[]{:S(2)}, u32[]{:S(2)}) collective-permute-start(f32[4,128,128]{2,1,0:T(8,128)S(1)} %get-tuple-element.39), channel_id=1, source_target_pairs={{0,1},{1,2},{2,3},{3,4},{4,5},{5,6},{6,7},{7,8},{8,9},{9,10},{10,1... | collective-permute-start | bytes 786440 | tf_op jit(solution)/shard_map/ppermute | solution.py:434
  15.6 12.0 %collective-permute-start.3 = (f32[4,128,128]{2,1,0:T(8,128)S(1)}, f32[4,128,128]{2,1,0:T(8,128)S(1)}, u32[]{:S(2)}, u32[]{:S(2)}) collective-permute-start(f32[4,128,128]{2,1,0:T(8,128)S(1)} %get-tuple-element.40), channel_id=1, source_target_pairs={{1,0},{2,1},{3,2},{4,3},{5,4},{6,5},{7,6},{8,7},{9,8},{10,9},{11,1... | collective-permute-start | bytes 786440 | tf_op jit(solution)/shard_map/ppermute | solution.py:435
  27.6 0.0 collective-permute-done.2.from_left
  27.6 1.1 collective-permute-done.3.from_right
  28.8 3.7 %model.1 = (f32[576,1,128]{2,1,0:T(1,128)S(1)}, f32[2,2,2,128,128]{4,3,2,1,0:T(8,128)S(1)}) custom-call(s32[2,2]{1,0:T(2,128)} %bitcast.13, f32[4,128,128]{2,1,0:T(8,128)S(1)} %get-tuple-element.30.own, f32[4,64,128]{2,1,0:T(8,128)S(1)} %collective-permute-done.above, f32[4,64,128]{2,1,0:T(8,128)S(1)} %collective-permute-done.1.below, ...), custom_call_target="tpu_custom_call" | custom-call | tf_op jit(solution)/shard_map/model/pallas_call | solution.py:437
  32.5 22.2 %all_to_all.15.gathered = f32[576,1,128]{2,1,0:T(1,128)S(1)} all-to-all(f32[576,1,128]{2,1,0:T(1,128)S(1)} %get-tuple-element.45), channel_id=1, replica_groups={{0,1,32,33,64,65,96,97,128,129,160,161,192,193,224,225,256,257,288,289,..., dimensions={0} | all-to-all | bytes 589824 | tf_op jit(solution)/shard_map/all_to_all | solution.py:360
  54.7 1.1 mix.1
  55.8 18.9 %all-to-all-start.1 = ((f32[16,4,8,128]{3,2,1,0:T(8,128)}), f32[16,4,8,128]{3,2,1,0:T(8,128)S(1)}, u32[]{:S(2)}, u32[]{:S(2)}) async-start(f32[16,4,8,128]{3,2,1,0:T(8,128)} %mix.1), calls=%async_computation.1 | async-start | bytes 524288 | tf_op jit(solution)/shard_map/all_to_all | solution.py:360
  74.7 1.1 deposit.1
  75.8 1.3 %collective-permute-start.4 = (f32[4,64,256]{2,1,0:T(8,128)S(1)}, f32[4,64,256]{2,1,0:T(8,128)S(1)}, u32[]{:S(2)}, u32[]{:S(2)}) collective-permute-start(f32[4,64,256]{2,1,0:T(8,128)S(1)} %get-tuple-element.47), channel_id=1, source_target_pairs={{32,0},{64,32},{96,64},{128,96},{160,128},{192,160},{224,192},{256... | collective-permute-start | bytes 786440 | tf_op jit(solution)/shard_map/ppermute | solution.py:489
  77.1 4.0 %collective-permute-start.5 = (f32[4,64,256]{2,1,0:T(8,128)S(1)}, f32[4,64,256]{2,1,0:T(8,128)S(1)}, u32[]{:S(2)}, u32[]{:S(2)}) collective-permute-start(f32[4,64,256]{2,1,0:T(8,128)S(1)} %get-tuple-element.48), channel_id=1, source_target_pairs={{0,32},{32,64},{64,96},{96,128},{128,160},{160,192},{192,224},{224... | collective-permute-start | bytes 786440 | tf_op jit(solution)/shard_map/ppermute | solution.py:490
  81.1 4.0 %collective-permute-done.4.from_below = f32[4,64,256]{2,1,0:T(8,128)S(1)} collective-permute-done((f32[4,64,256]{2,1,0:T(8,128)S(1)}, f32[4,64,256]{2,1,0:T(8,128)S(1)}, u32[]{:S(2)}, u32[]{:S(2)}) %collective-permute-start.4) | collective-permute-done | bytes 262176 | tf_op jit(solution)/shard_map/ppermute | solution.py:489
  85.1 0.9 collective-permute-done.5.from_above
  86.0 2.9 %all-to-all-done.1.parts = f32[16,4,8,128]{3,2,1,0:T(8,128)S(1)} async-done(((f32[16,4,8,128]{3,2,1,0:T(8,128)}), f32[16,4,8,128]{3,2,1,0:T(8,128)S(1)}, u32[]{:S(2)}, u32[]{:S(2)}) %all-to-all-start.1) | async-done | bytes 262176 | tf_op jit(solution)/shard_map/all_to_all | solution.py:360
  88.9 0.9 repeat.1
  89.8 5.5 %all-to-all-start.2 = ((f32[32,4,8,128]{3,2,1,0:T(8,128)}), f32[32,4,8,128]{3,2,1,0:T(8,128)S(1)}, u32[]{:S(2)}, u32[]{:S(2)}) async-start(f32[32,4,8,128]{3,2,1,0:T(8,128)} %repeat.1), calls=%async_computation.2 | async-start | bytes 1048576 | tf_op jit(solution)/shard_map/all_to_all | solution.py:360
  95.4 0.0 copy-start
  95.4 0.1 merge.1
  95.5 6.9 %collective-permute-start.6 = (f32[4,64,128]{2,1,0:T(8,128)S(1)}, f32[4,64,128]{2,1,0:T(8,128)S(1)}, u32[]{:S(2)}, u32[]{:S(2)}) collective-permute-start(f32[4,64,128]{2,1,0:T(8,128)S(1)} %get-tuple-element.54), channel_id=1, source_target_pairs={{0,1},{1,2},{2,3},{3,4},{4,5},{5,6},{6,7},{7,8},{8,9},{9,10},{10,1... | collective-permute-start | bytes 393224 | tf_op jit(solution)/shard_map/ppermute | solution.py:509
  102.4 1.9 %collective-permute-start.7 = (f32[4,64,128]{2,1,0:T(8,128)S(1)}, f32[4,64,128]{2,1,0:T(8,128)S(1)}, u32[]{:S(2)}, u32[]{:S(2)}) collective-permute-start(f32[4,64,128]{2,1,0:T(8,128)S(1)} %get-tuple-element.55), channel_id=1, source_target_pairs={{1,0},{2,1},{3,2},{4,3},{5,4},{6,5},{7,6},{8,7},{9,8},{10,9},{11,1... | collective-permute-start | bytes 393224 | tf_op jit(solution)/shard_map/ppermute | solution.py:510
  104.4 0.0 collective-permute-done.6.from_left
  104.4 4.6 %collective-permute-done.7.from_right = f32[4,64,128]{2,1,0:T(8,128)S(1)} collective-permute-done((f32[4,64,128]{2,1,0:T(8,128)S(1)}, f32[4,64,128]{2,1,0:T(8,128)S(1)}, u32[]{:S(2)}, u32[]{:S(2)}) %collective-permute-start.7) | collective-permute-done | bytes 131104 | tf_op jit(solution)/shard_map/ppermute | solution.py:510
  109.0 0.8 finish.1
  109.8 0.0 all-to-all-done.2.refs_1_
  109.8 6.4 %collective-permute-start.8 = (f32[32,4,8,128]{3,2,1,0:T(8,128)S(1)}, f32[32,4,8,128]{3,2,1,0:T(8,128)S(1)}, u32[]{:S(2)}, u32[]{:S(2)}) collective-permute-start(f32[32,4,8,128]{3,2,1,0:T(8,128)S(1)} %all-to-all-done.2.refs_1_), channel_id=1, source_target_pairs={{0,1},{1,0},{2,3},{3,2},{4,5},{5,4},{6,7},{7,6},{8,9},{9,8},{10,11... | collective-permute-start | bytes 1572872 | tf_op jit(solution)/shard_map/ppermute | solution.py:521
  116.3 1.5 %collective-permute-done.8.refs_2_ = f32[32,4,8,128]{3,2,1,0:T(8,128)S(1)} collective-permute-done((f32[32,4,8,128]{3,2,1,0:T(8,128)S(1)}, f32[32,4,8,128]{3,2,1,0:T(8,128)S(1)}, u32[]{:S(2)}, u32[]{:S(2)}) %collective-permute-start.8) | collective-permute-done | bytes 524320 | tf_op jit(solution)/shard_map/ppermute | solution.py:521
  117.8 0.0 copy-done
  117.8 3.2 %orthonormal.1 = f32[8,32,8,128]{3,2,1,0:T(8,128)} custom-call(s32[1]{0:T(128)} %bitcast.5.refs_0_, f32[32,4,8,128]{3,2,1,0:T(8,128)S(1)} %all-to-all-done.2.refs_1_, f32[32,4,8,128]{3,2,1,0:T(8,128)S(1)} %collective-permute-done.8.refs_2_, f32[8,32,8,128]{3,2,1,0:T(8,128)S(1)} %bitcast.8), custom_call_target="tpu_custom_call" | custom-call | tf_op jit(solution)/shard_map/orthonormal/pallas_call | solution.py:529
Async XLA Ops:
  1.7 7.5 %collective-permute-start.1 = (f32[4,64,128]{2,1,0:T(8,128)S(1)}, f32[4,64,128]{2,1,0:T(8,128)S(1)}, u32[]{:S(2)}, u32[]{:S(2)}) collective-permute-start(f32[4,64,128]{2,1,0:T(8,128)S(1)} %get-tuple-element.32.after), channel_id=1, source_target_pairs={{32,0},{64,32},{96,64},{128,96},{160,128},{192,160},{224,192},{256... | collective-permute-start | bytes 393224 | tf_op jit(solution)/shard_map/ppermute | solution.py:398
  3.0 6.5 %collective-permute-start = (f32[4,64,128]{2,1,0:T(8,128)S(1)}, f32[4,64,128]{2,1,0:T(8,128)S(1)}, u32[]{:S(2)}, u32[]{:S(2)}) collective-permute-start(f32[4,64,128]{2,1,0:T(8,128)S(1)} %get-tuple-element.31), channel_id=1, source_target_pairs={{0,32},{32,64},{64,96},{96,128},{128,160},{160,192},{192,224},{224... | collective-permute-start | bytes 393224 | tf_op jit(solution)/shard_map/ppermute | solution.py:397
  9.7 17.9 %collective-permute-start.2 = (f32[4,128,128]{2,1,0:T(8,128)S(1)}, f32[4,128,128]{2,1,0:T(8,128)S(1)}, u32[]{:S(2)}, u32[]{:S(2)}) collective-permute-start(f32[4,128,128]{2,1,0:T(8,128)S(1)} %get-tuple-element.39), channel_id=1, source_target_pairs={{0,1},{1,2},{2,3},{3,4},{4,5},{5,6},{6,7},{7,8},{8,9},{9,10},{10,1... | collective-permute-start | bytes 786440 | tf_op jit(solution)/shard_map/ppermute | solution.py:434
  15.6 13.1 %collective-permute-start.3 = (f32[4,128,128]{2,1,0:T(8,128)S(1)}, f32[4,128,128]{2,1,0:T(8,128)S(1)}, u32[]{:S(2)}, u32[]{:S(2)}) collective-permute-start(f32[4,128,128]{2,1,0:T(8,128)S(1)} %get-tuple-element.40), channel_id=1, source_target_pairs={{1,0},{2,1},{3,2},{4,3},{5,4},{6,5},{7,6},{8,7},{9,8},{10,9},{11,1... | collective-permute-start | bytes 786440 | tf_op jit(solution)/shard_map/ppermute | solution.py:435
  55.8 33.1 %all-to-all-start.1 = ((f32[16,4,8,128]{3,2,1,0:T(8,128)}), f32[16,4,8,128]{3,2,1,0:T(8,128)S(1)}, u32[]{:S(2)}, u32[]{:S(2)}) async-start(f32[16,4,8,128]{3,2,1,0:T(8,128)} %mix.1), calls=%async_computation.1 | async-start | bytes 524288 | tf_op jit(solution)/shard_map/all_to_all | solution.py:360
  75.8 9.3 %collective-permute-start.4 = (f32[4,64,256]{2,1,0:T(8,128)S(1)}, f32[4,64,256]{2,1,0:T(8,128)S(1)}, u32[]{:S(2)}, u32[]{:S(2)}) collective-permute-start(f32[4,64,256]{2,1,0:T(8,128)S(1)} %get-tuple-element.47), channel_id=1, source_target_pairs={{32,0},{64,32},{96,64},{128,96},{160,128},{192,160},{224,192},{256... | collective-permute-start | bytes 786440 | tf_op jit(solution)/shard_map/ppermute | solution.py:489
  77.1 8.9 %collective-permute-start.5 = (f32[4,64,256]{2,1,0:T(8,128)S(1)}, f32[4,64,256]{2,1,0:T(8,128)S(1)}, u32[]{:S(2)}, u32[]{:S(2)}) collective-permute-start(f32[4,64,256]{2,1,0:T(8,128)S(1)} %get-tuple-element.48), channel_id=1, source_target_pairs={{0,32},{32,64},{64,96},{96,128},{128,160},{160,192},{192,224},{224... | collective-permute-start | bytes 786440 | tf_op jit(solution)/shard_map/ppermute | solution.py:490
  89.8 20.0 %all-to-all-start.2 = ((f32[32,4,8,128]{3,2,1,0:T(8,128)}), f32[32,4,8,128]{3,2,1,0:T(8,128)S(1)}, u32[]{:S(2)}, u32[]{:S(2)}) async-start(f32[32,4,8,128]{3,2,1,0:T(8,128)} %repeat.1), calls=%async_computation.2 | async-start | bytes 1048576 | tf_op jit(solution)/shard_map/all_to_all | solution.py:360
  95.4 22.4 %copy-start = (f32[8,2,128,128]{3,2,1,0:T(8,128)S(1)}, f32[8,2,128,128]{3,2,1,0:T(8,128)}, u32[]{:S(2)}) copy-start(f32[8,2,128,128]{3,2,1,0:T(8,128)} %basis_in.1) | copy-start | bytes 3145732
  95.5 8.9 %collective-permute-start.6 = (f32[4,64,128]{2,1,0:T(8,128)S(1)}, f32[4,64,128]{2,1,0:T(8,128)S(1)}, u32[]{:S(2)}, u32[]{:S(2)}) collective-permute-start(f32[4,64,128]{2,1,0:T(8,128)S(1)} %get-tuple-element.54), channel_id=1, source_target_pairs={{0,1},{1,2},{2,3},{3,4},{4,5},{5,6},{6,7},{7,8},{8,9},{9,10},{10,1... | collective-permute-start | bytes 393224 | tf_op jit(solution)/shard_map/ppermute | solution.py:509
  102.4 6.6 %collective-permute-start.7 = (f32[4,64,128]{2,1,0:T(8,128)S(1)}, f32[4,64,128]{2,1,0:T(8,128)S(1)}, u32[]{:S(2)}, u32[]{:S(2)}) collective-permute-start(f32[4,64,128]{2,1,0:T(8,128)S(1)} %get-tuple-element.55), channel_id=1, source_target_pairs={{1,0},{2,1},{3,2},{4,3},{5,4},{6,5},{7,6},{8,7},{9,8},{10,9},{11,1... | collective-permute-start | bytes 393224 | tf_op jit(solution)/shard_map/ppermute | solution.py:510
  109.8 7.9 %collective-permute-start.8 = (f32[32,4,8,128]{3,2,1,0:T(8,128)S(1)}, f32[32,4,8,128]{3,2,1,0:T(8,128)S(1)}, u32[]{:S(2)}, u32[]{:S(2)}) collective-permute-start(f32[32,4,8,128]{3,2,1,0:T(8,128)S(1)} %all-to-all-done.2.refs_1_), channel_id=1, source_target_pairs={{0,1},{1,0},{2,3},{3,2},{4,5},{5,4},{6,7},{7,6},{8,9},{9,8},{10,11... | collective-permute-start | bytes 1572872 | tf_op jit(solution)/shard_map/ppermute | solution.py:521

commit v5 on v4

--- a/solution.py
+++ b/solution.py
@@ -1,3 +1,4 @@
+import functools
 import math
 
 import jax
@@ -87,12 +88,11 @@
     return jnp.stack([pltpu.roll(plane, plane.shape[-1] // 2, 1) for plane in values])
 
 
-def split_kernel(source, own, upper, lower, sems):
+def split_kernel(source, upper, lower, sems):
     half = upper.shape[1]
     copies = [
         pltpu.make_async_copy(source.at[:, 0:half], upper, sems.at[0]),
         pltpu.make_async_copy(source.at[:, half : 2 * half], lower, sems.at[1]),
-        pltpu.make_async_copy(source, own, sems.at[2]),
     ]
     for copy in copies:
         copy.start()
@@ -108,12 +108,10 @@
         out[at] = total
 
 
-def pack_kernel(own, above, below, to_left, to_right):
-    n = own.shape[-1]
-    half = n // 2
-    near = near_lanes(own.shape)
-    first = jnp.concatenate([above[...], own[:, :half]], axis=1)
-    second = jnp.concatenate([own[:, half:], below[...]], axis=1)
+def pack_kernel(upper, lower, above, below, to_left, to_right):
+    near = near_lanes(to_left.shape)
+    first = jnp.concatenate([above[...], upper[...]], axis=1)
+    second = jnp.concatenate([lower[...], below[...]], axis=1)
     second = roll_planes(second)
     to_left[...] = jnp.where(near, first, second)
     to_right[...] = jnp.where(near, second, first)
@@ -190,16 +188,17 @@
 
 
 def model_kernel(
-    positions_in, own, above, below, from_left, from_right, probes_in, forms, measured, packed,
+    positions_in, upper, lower, above, below, from_left, from_right, probes_in, forms, measured, packed,
     probe_grad, terms, frame, positions, sem,
 ):
     copy = pltpu.make_async_copy(positions_in, positions, sem)
     copy.start()
     n = measured.shape[-1]
     half = n // 2
-    near = near_lanes(own.shape)
+    near = near_lanes(from_left.shape)
     frame[:, 0:half, 0:n] = above[...]
-    frame[:, half : half + n, 0:n] = own[...]
+    frame[:, half:n, 0:n] = upper[...]
+    frame[:, n : n + half, 0:n] = lower[...]
     frame[:, half + n : 2 * n, 0:n] = below[...]
     frame[:, 0:n, n : 2 * n] = jnp.where(near, from_right[...], from_left[...])
     frame[:, n : 2 * n, n : 2 * n] = roll_planes(
@@ -317,38 +316,134 @@
             out[copy, pair] = tile
 
 
-def ortho_kernel(core, mine, other, basis, out, step_len=None):
-    modes, blocks, rows, n = out.shape
-    part_len = blocks // 2
-    pixels = part_len * rows * n
+def products(pairs, sums):
+    tiles, blocks, rows = pairs.shape[0], pairs.shape[1], pairs.shape[2]
+    parts = blocks // 2
+    sums = list(sums)
+    for block in range(parts):
+        real = [pairs[at, block] for at in range(tiles)]
+        imag = [pairs[at, parts + block] for at in range(tiles)]
+        turned_real = [pltpu.roll(values, rows // 2, 0) for values in real]
+        turned_imag = [pltpu.roll(values, rows // 2, 0) for values in imag]
+        at = 0
+        for first in range(tiles):
+            a, b = real[first], imag[first]
+            for second in range(first, tiles):
+                c, d = real[second], imag[second]
+                sums[at] = sums[at] + (a * c + b * d)
+                at += 1
+                if second > first:
+                    sums[at] = sums[at] + (a * d - b * c)
+                    at += 1
+                c, d = turned_real[second], turned_imag[second]
+                sums[at] = sums[at] + (a * c + b * d)
+                sums[at + 1] = sums[at + 1] + (a * d - b * c)
+                at += 2
+    return sums
+
+
+def own_kernel(core, mine, basis, own_pairs, base_pairs, sums_out, step_len=None):
+    tiles, blocks, rows, n = own_pairs.shape
     upper_rows = lax.broadcasted_iota(jnp.int32, (rows, n), 0) < rows // 2
     first_core = core[0] == 0
     for block in range(blocks):
-        for pair in range(modes // 2):
-            low = jnp.where(first_core, mine[block, pair], other[block, pair])
-            high = jnp.where(first_core, other[block, pair], mine[block, pair])
-            even = jnp.where(upper_rows, low, pltpu.roll(high, rows // 2, 0))
-            odd = jnp.where(upper_rows, pltpu.roll(low, rows // 2, 0), high)
-            out[2 * pair, block] = basis[2 * pair, block] - step_len * even
-            out[2 * pair + 1, block] = basis[2 * pair + 1, block] - step_len * odd
+        for at in range(tiles):
+            even, odd = basis[2 * at, block], basis[2 * at + 1, block]
+            low = jnp.where(upper_rows, even, pltpu.roll(odd, rows // 2, 0))
+            high = jnp.where(upper_rows, pltpu.roll(even, rows // 2, 0), odd)
+            base = jnp.where(first_core, low, high)
+            own_pairs[at, block] = base - step_len * mine[block, at]
+            base_pairs[at, block] = jnp.where(first_core, high, low)
+    zero = jnp.zeros((rows, n), jnp.float32)
+    sums = products(own_pairs, [zero] * sums_out.shape[0])
+    for at, values in enumerate(sums):
+        sums_out[at] = values
+
+
+def ortho_kernel(
+    core, other, own_pairs, base_pairs, sums_in, out, other_pairs, result, sems, step_len=None
+):
+    tiles, blocks, rows, n = own_pairs.shape
+    modes = 2 * tiles
+    parts = blocks // 2
+    pixels = parts * rows * n
+    half = rows // 2
+    upper_rows = lax.broadcasted_iota(jnp.int32, (rows, n), 0) < half
+    first_core = core[0] == 0
+    for block in range(blocks):
+        for at in range(tiles):
+            other_pairs[at, block] = base_pairs[at, block] - step_len * other[block, at]
+    sums = products(other_pairs, [sums_in[at] for at in range(sums_in.shape[0])])
 
     def total(values):
-        return jnp.sum(jnp.sum(values, axis=0), axis=(0, 1), keepdims=True)
-
-    for mode in range(modes):
-        real = out[mode, 0:part_len]
-        imag = out[mode, part_len:blocks]
-        norm = total(real * real + imag * imag)
-        for later in range(mode + 1, modes):
-            later_real = out[later, 0:part_len]
-            later_imag = out[later, part_len:blocks]
-            factor_real = (total(real * later_real + imag * later_imag) / norm)[None]
-            factor_imag = (total(real * later_imag - imag * later_real) / norm)[None]
-            out[later, 0:part_len] = later_real - (factor_real * real - factor_imag * imag)
-            out[later, part_len:blocks] = later_imag - (factor_real * imag + factor_imag * real)
-        scale = (1.0 / jnp.sqrt(norm / pixels))[None]
-        out[mode, 0:part_len] = real * scale
-        out[mode, part_len:blocks] = imag * scale
+        return jnp.sum(values, axis=(0, 1), keepdims=True) / pixels
+
+    gram = {}
+    at = 0
+    for first in range(tiles):
+        for second in range(first, tiles):
+            direct = [sums[at]]
+            at += 1
+            if second > first:
+                direct.append(sums[at])
+                at += 1
+            crossed = [sums[at], sums[at + 1]]
+            at += 2
+            low, high = 2 * first, 2 * second
+            gram[low, high] = [total(values[:half]) for values in direct]
+            gram[low + 1, high + 1] = [total(values[half:]) for values in direct]
+            gram[low, high + 1] = [total(values[:half]) for values in crossed]
+            if second > first:
+                gram[low + 1, high] = [total(values[half:]) for values in crossed]
+
+    factors = {}
+    inverse = []
+    for row in range(modes):
+        diagonal = gram[row, row][0]
+        for inner in range(row):
+            real, imag = factors[inner, row]
+            diagonal = diagonal - real * real - imag * imag
+        inverse.append(lax.rsqrt(diagonal))
+        for column in range(row + 1, modes):
+            real, imag = gram[row, column]
+            for inner in range(row):
+                a, b = factors[inner, row]
+                c, d = factors[inner, column]
+                real = real - (a * c + b * d)
+                imag = imag - (a * d - b * c)
+            factors[row, column] = (real * inverse[row], imag * inverse[row])
+
+    def apart(block):
+        values = []
+        for at in range(tiles):
+            own, far = own_pairs[at, block], other_pairs[at, block]
+            low = jnp.where(first_core, own, far)
+            high = jnp.where(first_core, far, own)
+            values.append(jnp.where(upper_rows, low, pltpu.roll(high, half, 0)))
+            values.append(jnp.where(upper_rows, pltpu.roll(low, half, 0), high))
+        return values
+
+    groups = sems.shape[0]
+    some = parts // groups
+    copies = []
+    for group in range(groups):
+        for block in range(group * some, (group + 1) * some):
+            reals, imags = apart(block), apart(parts + block)
+            for mode in range(modes):
+                real, imag = reals[mode], imags[mode]
+                for inner in range(mode):
+                    a, b = factors[inner, mode]
+                    real = real - (a * reals[inner] - b * imags[inner])
+                    imag = imag - (a * imags[inner] + b * reals[inner])
+                reals[mode] = real * inverse[mode]
+                imags[mode] = imag * inverse[mode]
+                result[mode, 0, block] = reals[mode]
+                result[mode, 1, block] = imags[mode]
+        here = (slice(None), slice(None), pl.ds(group * some, some))
+        copies.append(pltpu.make_async_copy(result.at[here], out.at[here], sems.at[group]))
+        copies[-1].start()
+    for copy in copies:
+        copy.wait()
 
 
 def shift_pairs(count):
@@ -385,12 +480,12 @@
     block = jax.ShapeDtypeStruct((planes, n, n), f32)
     edge = jax.ShapeDtypeStruct((planes, half, n), f32)
     distant = pl.BlockSpec(memory_space=pltpu.HBM)
-    own, upper, lower = pl.pallas_call(
+    upper, lower = pl.pallas_call(
         split_kernel,
-        out_shape=(block, edge, edge),
+        out_shape=(edge, edge),
         in_specs=[distant],
-        out_specs=tuple(vmem_specs(3)),
-        scratch_shapes=[pltpu.SemaphoreType.DMA((3,))],
+        out_specs=tuple(vmem_specs(2)),
+        scratch_shapes=[pltpu.SemaphoreType.DMA((2,))],
         compiler_params=params,
         name="split",
     )(away(obj_delta.reshape(planes, n, n)))
@@ -426,11 +521,11 @@
     to_left, to_right = pl.pallas_call(
         pack_kernel,
         out_shape=(block, block),
-        in_specs=vmem_specs(3),
+        in_specs=vmem_specs(4),
         out_specs=tuple(vmem_specs(2)),
         compiler_params=params,
         name="pack",
-    )(own, above, below)
+    )(upper, lower, above, below)
     from_left = lax.ppermute(to_right, "sx", forward_x)
     from_right = lax.ppermute(to_left, "sx", backward_x)
 
@@ -440,7 +535,7 @@
             jax.ShapeDtypeStruct((4 * blocks * PIECE, 1, n), f32),
             jax.ShapeDtypeStruct((2, per_tile, 2, n, n), f32),
         ),
-        in_specs=[distant] + vmem_specs(9),
+        in_specs=[distant] + vmem_specs(10),
         out_specs=tuple(vmem_specs(2)),
         scratch_shapes=[
             pltpu.VMEM((planes, 2 * n, 2 * n), f32),
@@ -450,7 +545,7 @@
         compiler_params=params,
         name="model",
     )(
-        away(positions[0, 0]), own, above, below, from_left, from_right,
+        away(positions[0, 0]), upper, lower, above, below, from_left, from_right,
         probes, forms, measured, packed,
     )
     wide_edge = jax.ShapeDtypeStruct((planes, half, 2 * n), f32)
@@ -488,6 +583,14 @@
     parts = exchange(parts, "sx", columns)
     from_below = lax.ppermute(up, "sy", backward_y)
     from_above = lax.ppermute(down, "sy", forward_y)
+    parts = pl.pallas_call(
+        repeat_kernel,
+        out_shape=jax.ShapeDtypeStruct((count_y,) + parts.shape[1:], f32),
+        in_specs=vmem_specs(1),
+        out_specs=vmem_specs(1)[0],
+        compiler_params=params,
+        name="repeat",
+    )(parts)
     parts, from_below, from_above = lax.optimization_barrier((parts, from_below, from_above))
     middle, to_left, to_right = pl.pallas_call(
         merge_kernel,
@@ -497,17 +600,10 @@
         compiler_params=params,
         name="merge",
     )(wide, from_above, from_below)
-    parts = pl.pallas_call(
-        repeat_kernel,
-        out_shape=jax.ShapeDtypeStruct((count_y,) + parts.shape[1:], f32),
-        in_specs=vmem_specs(1),
-        out_specs=vmem_specs(1)[0],
-        compiler_params=params,
-        name="repeat",
-    )(parts)
     mine = exchange(parts, "sy")
     from_left = lax.ppermute(to_right, "sx", forward_x)
     from_right = lax.ppermute(to_left, "sx", backward_x)
+    mine, from_left, from_right = lax.optimization_barrier((mine, from_left, from_right))
     obj_grad = pl.pallas_call(
         finish_kernel,
         out_shape=block,
@@ -516,26 +612,42 @@
         compiler_params=params,
         name="finish",
     )(middle, from_left, from_right)
-    mine, obj_grad = lax.optimization_barrier((mine, obj_grad))
     swap = [(at, at ^ 1) for at in range(count_x)]
     other = lax.ppermute(mine, "sx", swap)
+    other, obj_grad = lax.optimization_barrier((other, obj_grad))
     core = (lax.axis_index("sx") % cores).astype(jnp.int32).reshape(1)
     count_all = per_tile * count_y * count_x
     step_len = 1.0 / math.sqrt(count_all)
 
-    def final_kernel(*refs):
-        ortho_kernel(*refs, step_len=step_len)
-
+    tiles = modes // 2
+    pair_shape = (tiles, 2 * blocks, 8, n)
+    sum_count = 2 * tiles * tiles + tiles
+    own_pairs, base_pairs, sums = pl.pallas_call(
+        functools.partial(own_kernel, step_len=step_len),
+        out_shape=(
+            jax.ShapeDtypeStruct(pair_shape, f32),
+            jax.ShapeDtypeStruct(pair_shape, f32),
+            jax.ShapeDtypeStruct((sum_count, 8, n), f32),
+        ),
+        in_specs=[smem] + vmem_specs(2),
+        out_specs=tuple(vmem_specs(3)),
+        compiler_params=params,
+        name="own_half",
+    )(core, mine, probe_basis.reshape(modes, 2 * blocks, 8, n))
     new_basis = pl.pallas_call(
-        final_kernel,
-        out_shape=jax.ShapeDtypeStruct((modes, 2 * blocks, 8, n), f32),
-        in_specs=[smem] + vmem_specs(3),
-        out_specs=vmem_specs(1)[0],
+        functools.partial(ortho_kernel, step_len=step_len),
+        out_shape=jax.ShapeDtypeStruct((modes, 2, blocks, 8, n), f32),
+        in_specs=[smem] + vmem_specs(4),
+        out_specs=distant,
+        scratch_shapes=[
+            pltpu.VMEM(pair_shape, f32),
+            pltpu.VMEM((modes, 2, blocks, 8, n), f32),
+            pltpu.SemaphoreType.DMA((4,)),
+        ],
         compiler_params=params,
         name="orthonormal",
-    )(core, mine, other, probe_basis.reshape(modes, 2 * blocks, 8, n))
+    )(core, other, own_pairs, base_pairs, sums)
     new_basis = new_basis.reshape(probe_basis.shape)
-
     return (obj_grad.reshape(obj_delta.shape), new_basis)
 
 

time: 122 us -> 122 us (level); the launches traced: 121 us -> 120 us
  waiting for transfers between devices: 15.5 us -> 14.2 us
    all_to_all x2, waiting for transfers between devices: 2.94 us -> 7.85 us  [exchange(): lax.all_to_all(values, axis, 0, 0, tiled=True, axis_index_groups=groups)]
    ppermute x1, waiting for transfers between devices: 4.04 us -> 0.01 us  [local(): from_below = lax.ppermute(up, 'sy', backward_y)]
    ppermute x1, waiting for transfers between devices: 1.5 us -> 0.22 us  [local(): other = lax.ppermute(mine, 'sx', swap)]
    pallas_call x2 -> x3, Pallas kernels: 4.29 us -> 3.97 us  [the longest x1 2.52 us: local(): pl.pallas_call(functools.partial(ortho_kernel, step_len=step_len), out_sh...]
  transfers between devices with their start and end apart: 11 -> 11, of which waited for: 7 -> 5; matrix products, arithmetic and copies ran while one was open for 0% -> 0% of each run, Pallas kernels for 3% -> 4%
where the time goes in v5:
time: 122 us; the launch traced here: 120 us
  starting transfers between devices  69.1 us (57%)
  blocking collectives  22.2 us (18%)
  waiting for transfers between devices  14.2 us (12%)
  Pallas kernels  13.3 us (11%)
    all_to_all x2, starting transfers between devices, exchange(): lax.all_to_all(values, axis, 0, 0, tiled=True, axis_index_groups=groups)  23.6 us
    all_to_all x1, blocking collectives, exchange(): lax.all_to_all(values, axis, 0, 0, tiled=True, axis_index_groups=groups)  22.2 us
    ppermute x2, starting transfers between devices, local(): from_right = lax.ppermute(to_left, 'sx', backward_x)  13.9 us
    ppermute x2, starting transfers between devices, local(): from_left = lax.ppermute(to_right, 'sx', forward_x)  13.8 us
    all_to_all x2, waiting for transfers between devices, exchange(): lax.all_to_all(values, axis, 0, 0, tiled=True, axis_index_groups=groups)  7.85 us
    ppermute x1, starting transfers between devices, local(): other = lax.ppermute(mine, 'sx', swap)  6.69 us
    ppermute x2, waiting for transfers between devices, local(): from_right = lax.ppermute(to_left, 'sx', backward_x)  5.77 us
    ppermute x1, starting transfers between devices, local(): above = lax.ppermute(lower, 'sy', forward_y)  4.58 us
  transfers between devices with their start and end apart: 11, of which 5 were waited for; matrix products, arithmetic and copies ran while one was open for 0% of the time, Pallas kernels for 4%

profile of v5, /device:TPU:1, one launch (start us, length us, event | category | flops | bytes accessed | tf_op | source)
XLA Modules:
  0.0 119.7 jit_solution(17065570674757944771)
XLA Ops:
  0.6 1.0 split.1
  1.6 1.3 %collective-permute-start.1 = (f32[4,64,128]{2,1,0:T(8,128)S(1)}, f32[4,64,128]{2,1,0:T(8,128)S(1)}, u32[]{:S(2)}, u32[]{:S(2)}) collective-permute-start(f32[4,64,128]{2,1,0:T(8,128)S(1)} %get-tuple-element.35.after.upper), channel_id=1, source_target_pairs={{32,0},{64,32},{96,64},{128,96},{160,128},{192,160},{224,192},{256... | collective-permute-start | bytes 393224 | tf_op jit(solution)/shard_map/ppermute | solution.py:493
  2.9 4.6 %collective-permute-start = (f32[4,64,128]{2,1,0:T(8,128)S(1)}, f32[4,64,128]{2,1,0:T(8,128)S(1)}, u32[]{:S(2)}, u32[]{:S(2)}) collective-permute-start(f32[4,64,128]{2,1,0:T(8,128)S(1)} %get-tuple-element.36.lower), channel_id=1, source_target_pairs={{0,32},{32,64},{64,96},{96,128},{128,160},{160,192},{192,224},{224... | collective-permute-start | bytes 393224 | tf_op jit(solution)/shard_map/ppermute | solution.py:492
  7.5 1.6 %prepare.1 = (f32[2,2,128,128]{3,2,1,0:T(8,128)S(1)}, bf16[4,2,256,256]{3,2,1,0:T(8,128)(2,1)S(1)}, f32[2,128,128]{2,1,0:T(8,128)S(1)}, f32[1,128]{1,0:T(1,128)S(1)}) custom-call(f32[4,64,128]{2,1,0:T(8,128)S(1)} %get-tuple-element.35.after.upper, f32[2,8]{1,0:T(2,128)} %bitcast.15, f32[2,128,128]{2,1,0:T(8,128)} %mean_in.1, f32[8,2,128,128]{3,2,1,0:T(8,128)} %basis_in.1, ...), custom_call_target="tpu_custom_call" | custom-call | tf_op jit(solution)/shard_map/prepare/pallas_call | solution.py:495
  9.1 0.0 collective-permute-done.1.below
  9.1 0.3 collective-permute-done.above
  9.4 0.1 pack.1
  9.6 5.9 %collective-permute-start.2 = (f32[4,128,128]{2,1,0:T(8,128)S(1)}, f32[4,128,128]{2,1,0:T(8,128)S(1)}, u32[]{:S(2)}, u32[]{:S(2)}) collective-permute-start(f32[4,128,128]{2,1,0:T(8,128)S(1)} %get-tuple-element.43), channel_id=1, source_target_pairs={{0,1},{1,2},{2,3},{3,4},{4,5},{5,6},{6,7},{7,8},{8,9},{9,10},{10,1... | collective-permute-start | bytes 786440 | tf_op jit(solution)/shard_map/ppermute | solution.py:529
  15.5 12.0 %collective-permute-start.3 = (f32[4,128,128]{2,1,0:T(8,128)S(1)}, f32[4,128,128]{2,1,0:T(8,128)S(1)}, u32[]{:S(2)}, u32[]{:S(2)}) collective-permute-start(f32[4,128,128]{2,1,0:T(8,128)S(1)} %get-tuple-element.44), channel_id=1, source_target_pairs={{1,0},{2,1},{3,2},{4,3},{5,4},{6,5},{7,6},{8,7},{9,8},{10,9},{11,1... | collective-permute-start | bytes 786440 | tf_op jit(solution)/shard_map/ppermute | solution.py:530
  27.5 0.0 collective-permute-done.2.from_left
  27.5 1.1 collective-permute-done.3.from_right
  28.6 3.7 %model.1 = (f32[576,1,128]{2,1,0:T(1,128)S(1)}, f32[2,2,2,128,128]{4,3,2,1,0:T(8,128)S(1)}) custom-call(s32[2,2]{1,0:T(2,128)} %bitcast.13, f32[4,64,128]{2,1,0:T(8,128)S(1)} %get-tuple-element.35.after.upper, f32[4,64,128]{2,1,0:T(8,128)S(1)} %get-tuple-element.36.lower, f32[4,64,128]{2,1,0:T(8,128)S(1)} %collective-permute-done.above, ...), custom_call_target="tpu_custom_call" | custom-call | tf_op jit(solution)/shard_map/model/pallas_call | solution.py:532
  32.4 22.2 %all_to_all.15.gathered = f32[576,1,128]{2,1,0:T(1,128)S(1)} all-to-all(f32[576,1,128]{2,1,0:T(1,128)S(1)} %get-tuple-element.49), channel_id=1, replica_groups={{0,1,32,33,64,65,96,97,128,129,160,161,192,193,224,225,256,257,288,289,..., dimensions={0} | all-to-all | bytes 589824 | tf_op jit(solution)/shard_map/all_to_all | solution.py:455
  54.6 1.1 mix.1
  55.7 18.9 %all-to-all-start.1 = ((f32[16,4,8,128]{3,2,1,0:T(8,128)}), f32[16,4,8,128]{3,2,1,0:T(8,128)S(1)}, u32[]{:S(2)}, u32[]{:S(2)}) async-start(f32[16,4,8,128]{3,2,1,0:T(8,128)} %mix.1), calls=%async_computation.1 | async-start | bytes 524288 | tf_op jit(solution)/shard_map/all_to_all | solution.py:455
  74.6 1.1 deposit.1
  75.7 1.3 %collective-permute-start.4 = (f32[4,64,256]{2,1,0:T(8,128)S(1)}, f32[4,64,256]{2,1,0:T(8,128)S(1)}, u32[]{:S(2)}, u32[]{:S(2)}) collective-permute-start(f32[4,64,256]{2,1,0:T(8,128)S(1)} %get-tuple-element.51), channel_id=1, source_target_pairs={{32,0},{64,32},{96,64},{128,96},{160,128},{192,160},{224,192},{256... | collective-permute-start | bytes 786440 | tf_op jit(solution)/shard_map/ppermute | solution.py:584
  77.0 4.0 %collective-permute-start.5 = (f32[4,64,256]{2,1,0:T(8,128)S(1)}, f32[4,64,256]{2,1,0:T(8,128)S(1)}, u32[]{:S(2)}, u32[]{:S(2)}) collective-permute-start(f32[4,64,256]{2,1,0:T(8,128)S(1)} %get-tuple-element.52), channel_id=1, source_target_pairs={{0,32},{32,64},{64,96},{96,128},{128,160},{160,192},{192,224},{224... | collective-permute-start | bytes 786440 | tf_op jit(solution)/shard_map/ppermute | solution.py:585
  81.0 7.8 %all-to-all-done.1.parts = f32[16,4,8,128]{3,2,1,0:T(8,128)S(1)} async-done(((f32[16,4,8,128]{3,2,1,0:T(8,128)}), f32[16,4,8,128]{3,2,1,0:T(8,128)S(1)}, u32[]{:S(2)}, u32[]{:S(2)}) %all-to-all-start.1) | async-done | bytes 262176 | tf_op jit(solution)/shard_map/all_to_all | solution.py:455
  88.8 0.9 repeat.1
  89.7 0.0 copy-start
  89.7 0.0 collective-permute-done.4.from_below
  89.7 0.0 collective-permute-done.5.from_above
  89.7 4.7 %all-to-all-start.2 = ((f32[32,4,8,128]{3,2,1,0:T(8,128)}), f32[32,4,8,128]{3,2,1,0:T(8,128)S(1)}, u32[]{:S(2)}, u32[]{:S(2)}) async-start(f32[32,4,8,128]{3,2,1,0:T(8,128)} %repeat.1), calls=%async_computation.2 | async-start | bytes 1048576 | tf_op jit(solution)/shard_map/all_to_all | solution.py:455
  94.4 0.1 merge.1
  94.5 7.8 %collective-permute-start.6 = (f32[4,64,128]{2,1,0:T(8,128)S(1)}, f32[4,64,128]{2,1,0:T(8,128)S(1)}, u32[]{:S(2)}, u32[]{:S(2)}) collective-permute-start(f32[4,64,128]{2,1,0:T(8,128)S(1)} %get-tuple-element.57), channel_id=1, source_target_pairs={{0,1},{1,2},{2,3},{3,4},{4,5},{5,6},{6,7},{7,8},{8,9},{9,10},{10,1... | collective-permute-start | bytes 393224 | tf_op jit(solution)/shard_map/ppermute | solution.py:604
  102.3 1.9 %collective-permute-start.7 = (f32[4,64,128]{2,1,0:T(8,128)S(1)}, f32[4,64,128]{2,1,0:T(8,128)S(1)}, u32[]{:S(2)}, u32[]{:S(2)}) collective-permute-start(f32[4,64,128]{2,1,0:T(8,128)S(1)} %get-tuple-element.58), channel_id=1, source_target_pairs={{1,0},{2,1},{3,2},{4,3},{5,4},{6,5},{7,6},{8,7},{9,8},{10,9},{11,1... | collective-permute-start | bytes 393224 | tf_op jit(solution)/shard_map/ppermute | solution.py:605
  104.3 0.0 collective-permute-done.6.from_left
  104.3 4.6 %collective-permute-done.7.from_right = f32[4,64,128]{2,1,0:T(8,128)S(1)} collective-permute-done((f32[4,64,128]{2,1,0:T(8,128)S(1)}, f32[4,64,128]{2,1,0:T(8,128)S(1)}, u32[]{:S(2)}, u32[]{:S(2)}) %collective-permute-start.7) | collective-permute-done | bytes 131104 | tf_op jit(solution)/shard_map/ppermute | solution.py:605
  108.9 0.0 all-to-all-done.2.mine
  108.9 6.7 %collective-permute-start.8 = (f32[32,4,8,128]{3,2,1,0:T(8,128)S(1)}, f32[32,4,8,128]{3,2,1,0:T(8,128)S(1)}, u32[]{:S(2)}, u32[]{:S(2)}) collective-permute-start(f32[32,4,8,128]{3,2,1,0:T(8,128)S(1)} %all-to-all-done.2.mine), channel_id=1, source_target_pairs={{0,1},{1,0},{2,3},{3,2},{4,5},{5,4},{6,7},{7,6},{8,9},{9,8},{10,11... | collective-permute-start | bytes 1572872 | tf_op jit(solution)/shard_map/ppermute | solution.py:616
  115.6 0.0 copy-done
  115.6 0.5 own_half.1
  116.1 0.8 finish.1
  116.9 0.2 collective-permute-done.8.other
  117.1 2.5 %orthonormal.1 = f32[8,2,16,8,128]{4,3,2,1,0:T(8,128)} custom-call(s32[1]{0:T(128)} %bitcast.5.core, f32[32,4,8,128]{3,2,1,0:T(8,128)S(1)} %collective-permute-done.8.other, f32[4,32,8,128]{3,2,1,0:T(8,128)S(1)} %get-tuple-element.65.own_pairs, f32[4,32,8,128]{3,2,1,0:T(8,128)S(1)} %get-tuple-element.66.base_pairs, f32[36,8,128]{2,1,0:T(8,128)S(1)} %get-tuple-element.67.sums_in), custom_call_target="tpu_custom_call" | custom-call | tf_op jit(solution)/shard_map/orthonormal/pallas_call | solution.py:637
Async XLA Ops:
  1.6 7.5 %collective-permute-start.1 = (f32[4,64,128]{2,1,0:T(8,128)S(1)}, f32[4,64,128]{2,1,0:T(8,128)S(1)}, u32[]{:S(2)}, u32[]{:S(2)}) collective-permute-start(f32[4,64,128]{2,1,0:T(8,128)S(1)} %get-tuple-element.35.after.upper), channel_id=1, source_target_pairs={{32,0},{64,32},{96,64},{128,96},{160,128},{192,160},{224,192},{256... | collective-permute-start | bytes 393224 | tf_op jit(solution)/shard_map/ppermute | solution.py:493
  2.9 6.5 %collective-permute-start = (f32[4,64,128]{2,1,0:T(8,128)S(1)}, f32[4,64,128]{2,1,0:T(8,128)S(1)}, u32[]{:S(2)}, u32[]{:S(2)}) collective-permute-start(f32[4,64,128]{2,1,0:T(8,128)S(1)} %get-tuple-element.36.lower), channel_id=1, source_target_pairs={{0,32},{32,64},{64,96},{96,128},{128,160},{160,192},{192,224},{224... | collective-permute-start | bytes 393224 | tf_op jit(solution)/shard_map/ppermute | solution.py:492
  9.6 17.9 %collective-permute-start.2 = (f32[4,128,128]{2,1,0:T(8,128)S(1)}, f32[4,128,128]{2,1,0:T(8,128)S(1)}, u32[]{:S(2)}, u32[]{:S(2)}) collective-permute-start(f32[4,128,128]{2,1,0:T(8,128)S(1)} %get-tuple-element.43), channel_id=1, source_target_pairs={{0,1},{1,2},{2,3},{3,4},{4,5},{5,6},{6,7},{7,8},{8,9},{9,10},{10,1... | collective-permute-start | bytes 786440 | tf_op jit(solution)/shard_map/ppermute | solution.py:529
  15.5 13.1 %collective-permute-start.3 = (f32[4,128,128]{2,1,0:T(8,128)S(1)}, f32[4,128,128]{2,1,0:T(8,128)S(1)}, u32[]{:S(2)}, u32[]{:S(2)}) collective-permute-start(f32[4,128,128]{2,1,0:T(8,128)S(1)} %get-tuple-element.44), channel_id=1, source_target_pairs={{1,0},{2,1},{3,2},{4,3},{5,4},{6,5},{7,6},{8,7},{9,8},{10,9},{11,1... | collective-permute-start | bytes 786440 | tf_op jit(solution)/shard_map/ppermute | solution.py:530
  55.7 33.1 %all-to-all-start.1 = ((f32[16,4,8,128]{3,2,1,0:T(8,128)}), f32[16,4,8,128]{3,2,1,0:T(8,128)S(1)}, u32[]{:S(2)}, u32[]{:S(2)}) async-start(f32[16,4,8,128]{3,2,1,0:T(8,128)} %mix.1), calls=%async_computation.1 | async-start | bytes 524288 | tf_op jit(solution)/shard_map/all_to_all | solution.py:455
  75.7 14.0 %collective-permute-start.4 = (f32[4,64,256]{2,1,0:T(8,128)S(1)}, f32[4,64,256]{2,1,0:T(8,128)S(1)}, u32[]{:S(2)}, u32[]{:S(2)}) collective-permute-start(f32[4,64,256]{2,1,0:T(8,128)S(1)} %get-tuple-element.51), channel_id=1, source_target_pairs={{32,0},{64,32},{96,64},{128,96},{160,128},{192,160},{224,192},{256... | collective-permute-start | bytes 786440 | tf_op jit(solution)/shard_map/ppermute | solution.py:584
  77.0 12.7 %collective-permute-start.5 = (f32[4,64,256]{2,1,0:T(8,128)S(1)}, f32[4,64,256]{2,1,0:T(8,128)S(1)}, u32[]{:S(2)}, u32[]{:S(2)}) collective-permute-start(f32[4,64,256]{2,1,0:T(8,128)S(1)} %get-tuple-element.52), channel_id=1, source_target_pairs={{0,32},{32,64},{64,96},{96,128},{128,160},{160,192},{192,224},{224... | collective-permute-start | bytes 786440 | tf_op jit(solution)/shard_map/ppermute | solution.py:585
  89.7 25.9 %copy-start = (f32[8,2,128,128]{3,2,1,0:T(8,128)S(1)}, f32[8,2,128,128]{3,2,1,0:T(8,128)}, u32[]{:S(2)}) copy-start(f32[8,2,128,128]{3,2,1,0:T(8,128)} %basis_in.1) | copy-start | bytes 3145732
  89.7 19.2 %all-to-all-start.2 = ((f32[32,4,8,128]{3,2,1,0:T(8,128)}), f32[32,4,8,128]{3,2,1,0:T(8,128)S(1)}, u32[]{:S(2)}, u32[]{:S(2)}) async-start(f32[32,4,8,128]{3,2,1,0:T(8,128)} %repeat.1), calls=%async_computation.2 | async-start | bytes 1048576 | tf_op jit(solution)/shard_map/all_to_all | solution.py:455
  94.5 9.8 %collective-permute-start.6 = (f32[4,64,128]{2,1,0:T(8,128)S(1)}, f32[4,64,128]{2,1,0:T(8,128)S(1)}, u32[]{:S(2)}, u32[]{:S(2)}) collective-permute-start(f32[4,64,128]{2,1,0:T(8,128)S(1)} %get-tuple-element.57), channel_id=1, source_target_pairs={{0,1},{1,2},{2,3},{3,4},{4,5},{5,6},{6,7},{7,8},{8,9},{9,10},{10,1... | collective-permute-start | bytes 393224 | tf_op jit(solution)/shard_map/ppermute | solution.py:604
  102.3 6.6 %collective-permute-start.7 = (f32[4,64,128]{2,1,0:T(8,128)S(1)}, f32[4,64,128]{2,1,0:T(8,128)S(1)}, u32[]{:S(2)}, u32[]{:S(2)}) collective-permute-start(f32[4,64,128]{2,1,0:T(8,128)S(1)} %get-tuple-element.58), channel_id=1, source_target_pairs={{1,0},{2,1},{3,2},{4,3},{5,4},{6,5},{7,6},{8,7},{9,8},{10,9},{11,1... | collective-permute-start | bytes 393224 | tf_op jit(solution)/shard_map/ppermute | solution.py:605
  108.9 8.2 %collective-permute-start.8 = (f32[32,4,8,128]{3,2,1,0:T(8,128)S(1)}, f32[32,4,8,128]{3,2,1,0:T(8,128)S(1)}, u32[]{:S(2)}, u32[]{:S(2)}) collective-permute-start(f32[32,4,8,128]{3,2,1,0:T(8,128)S(1)} %all-to-all-done.2.mine), channel_id=1, source_target_pairs={{0,1},{1,0},{2,3},{3,2},{4,5},{5,4},{6,7},{7,6},{8,9},{9,8},{10,11... | collective-permute-start | bytes 1572872 | tf_op jit(solution)/shard_map/ppermute | solution.py:616

commit v6 on v5

--- a/solution.py
+++ b/solution.py
@@ -100,12 +100,25 @@
         copy.wait()
 
 
-def repeat_kernel(parts, out):
+def spread(several, out, sems):
+    some = several.shape[0]
+    copies = [
+        pltpu.make_async_copy(several, out.at[pl.ds(at * some, some)], sems.at[at])
+        for at in range(sems.shape[0])
+    ]
+    for copy in copies:
+        copy.start()
+    for copy in copies:
+        copy.wait()
+
+
+def repeat_kernel(parts, out, several, sems):
     total = parts[0]
     for at in range(1, parts.shape[0]):
         total = total + parts[at]
-    for at in range(out.shape[0]):
-        out[at] = total
+    for at in range(several.shape[0]):
+        several[at] = total
+    spread(several, out, sems)
 
 
 def pack_kernel(upper, lower, above, below, to_left, to_right):
@@ -241,8 +254,8 @@
     chi = []
     for slot in slots:
         real, imag = far[slot]
-        modulus = jnp.maximum(jnp.sqrt(real * real + imag * imag), FLOOR)
-        ratio = measured[slot] / modulus
+        inverse = jnp.minimum(lax.rsqrt(real * real + imag * imag), 1.0 / FLOOR)
+        ratio = measured[slot] * inverse
         chi.append((real - real * ratio, imag - imag * ratio))
     back = both_sides(chi, dft_t, dft)
     keep(1, conj_times(entered, back))
@@ -292,8 +305,8 @@
     down[...] = grads[:, half + n : 2 * n]
 
 
-def mix_kernel(gathered, out, ordered):
-    copies, pairs, rows, n = out.shape
+def mix_kernel(gathered, out, ordered, several, sems):
+    copies, pairs, rows, n = several.shape
     modes = 2 * pairs
     some = rows // 2
     count = gathered.shape[0] // PIECE
@@ -313,7 +326,8 @@
     for pair in range(pairs):
         tile = ordered[pair * rows : (pair + 1) * rows]
         for copy in range(copies):
-            out[copy, pair] = tile
+            several[copy, pair] = tile
+    spread(several, out, sems)
 
 
 def products(pairs, sums):
@@ -376,7 +390,7 @@
     sums = products(other_pairs, [sums_in[at] for at in range(sums_in.shape[0])])
 
     def total(values):
-        return jnp.sum(values, axis=(0, 1), keepdims=True) / pixels
+        return jnp.sum(values, axis=(0, 1), keepdims=True) * (1.0 / pixels)
 
     gram = {}
     at = 0
@@ -575,8 +589,12 @@
         mix_kernel,
         out_shape=jax.ShapeDtypeStruct((per_core, modes // 2, 8, n), f32),
         in_specs=vmem_specs(1),
-        out_specs=vmem_specs(1)[0],
-        scratch_shapes=[pltpu.VMEM((4 * modes, n), f32)],
+        out_specs=distant,
+        scratch_shapes=[
+            pltpu.VMEM((4 * modes, n), f32),
+            pltpu.VMEM((per_core // 4, modes // 2, 8, n), f32),
+            pltpu.SemaphoreType.DMA((4,)),
+        ],
         compiler_params=params,
         name="mix",
     )(gathered)
@@ -587,7 +605,11 @@
         repeat_kernel,
         out_shape=jax.ShapeDtypeStruct((count_y,) + parts.shape[1:], f32),
         in_specs=vmem_specs(1),
-        out_specs=vmem_specs(1)[0],
+        out_specs=distant,
+        scratch_shapes=[
+            pltpu.VMEM((count_y // 4,) + parts.shape[1:], f32),
+            pltpu.SemaphoreType.DMA((4,)),
+        ],
         compiler_params=params,
         name="repeat",
     )(parts)

time: 122 us -> 122 us (level)
  no operation moved by 1% of the time
where the time goes in v6:
time: 122 us; the launch traced here: 120 us
  starting transfers between devices  69.1 us (57%)
  blocking collectives  22.2 us (18%)
  waiting for transfers between devices  14.2 us (12%)
  Pallas kernels  13.3 us (11%)
    all_to_all x2, starting transfers between devices, exchange(): lax.all_to_all(values, axis, 0, 0, tiled=True, axis_index_groups=groups)  23.6 us
    all_to_all x1, blocking collectives, exchange(): lax.all_to_all(values, axis, 0, 0, tiled=True, axis_index_groups=groups)  22.2 us
    ppermute x2, starting transfers between devices, local(): from_right = lax.ppermute(to_left, 'sx', backward_x)  13.9 us
    ppermute x2, starting transfers between devices, local(): from_left = lax.ppermute(to_right, 'sx', forward_x)  13.8 us
    all_to_all x2, waiting for transfers between devices, exchange(): lax.all_to_all(values, axis, 0, 0, tiled=True, axis_index_groups=groups)  7.85 us
    ppermute x1, starting transfers between devices, local(): other = lax.ppermute(mine, 'sx', swap)  6.69 us
    ppermute x2, waiting for transfers between devices, local(): from_right = lax.ppermute(to_left, 'sx', backward_x)  5.77 us
    ppermute x1, starting transfers between devices, local(): above = lax.ppermute(lower, 'sy', forward_y)  4.58 us
  transfers between devices with their start and end apart: 11, of which 5 were waited for; matrix products, arithmetic and copies ran while one was open for 0% of the time, Pallas kernels for 4%

profile of v6, /device:TPU:1, one launch (start us, length us, event | category | flops | bytes accessed | tf_op | source)
XLA Modules:
  0.0 119.7 jit_solution(15992123153797811418)
XLA Ops:
  0.6 1.0 split.1
  1.6 1.3 %collective-permute-start.1 = (f32[4,64,128]{2,1,0:T(8,128)S(1)}, f32[4,64,128]{2,1,0:T(8,128)S(1)}, u32[]{:S(2)}, u32[]{:S(2)}) collective-permute-start(f32[4,64,128]{2,1,0:T(8,128)S(1)} %get-tuple-element.35.after.upper), channel_id=1, source_target_pairs={{32,0},{64,32},{96,64},{128,96},{160,128},{192,160},{224,192},{256... | collective-permute-start | bytes 393224 | tf_op jit(solution)/shard_map/ppermute | solution.py:507
  2.9 4.6 %collective-permute-start = (f32[4,64,128]{2,1,0:T(8,128)S(1)}, f32[4,64,128]{2,1,0:T(8,128)S(1)}, u32[]{:S(2)}, u32[]{:S(2)}) collective-permute-start(f32[4,64,128]{2,1,0:T(8,128)S(1)} %get-tuple-element.36.lower), channel_id=1, source_target_pairs={{0,32},{32,64},{64,96},{96,128},{128,160},{160,192},{192,224},{224... | collective-permute-start | bytes 393224 | tf_op jit(solution)/shard_map/ppermute | solution.py:506
  7.5 1.6 %prepare.1 = (f32[2,2,128,128]{3,2,1,0:T(8,128)S(1)}, bf16[4,2,256,256]{3,2,1,0:T(8,128)(2,1)S(1)}, f32[2,128,128]{2,1,0:T(8,128)S(1)}, f32[1,128]{1,0:T(1,128)S(1)}) custom-call(f32[4,64,128]{2,1,0:T(8,128)S(1)} %get-tuple-element.35.after.upper, f32[2,8]{1,0:T(2,128)} %bitcast.15, f32[2,128,128]{2,1,0:T(8,128)} %mean_in.1, f32[8,2,128,128]{3,2,1,0:T(8,128)} %basis_in.1, ...), custom_call_target="tpu_custom_call" | custom-call | tf_op jit(solution)/shard_map/prepare/pallas_call | solution.py:509
  9.1 0.0 collective-permute-done.1.below
  9.1 0.3 collective-permute-done.above
  9.4 0.1 pack.1
  9.6 5.9 %collective-permute-start.2 = (f32[4,128,128]{2,1,0:T(8,128)S(1)}, f32[4,128,128]{2,1,0:T(8,128)S(1)}, u32[]{:S(2)}, u32[]{:S(2)}) collective-permute-start(f32[4,128,128]{2,1,0:T(8,128)S(1)} %get-tuple-element.43), channel_id=1, source_target_pairs={{0,1},{1,2},{2,3},{3,4},{4,5},{5,6},{6,7},{7,8},{8,9},{9,10},{10,1... | collective-permute-start | bytes 786440 | tf_op jit(solution)/shard_map/ppermute | solution.py:543
  15.5 12.0 %collective-permute-start.3 = (f32[4,128,128]{2,1,0:T(8,128)S(1)}, f32[4,128,128]{2,1,0:T(8,128)S(1)}, u32[]{:S(2)}, u32[]{:S(2)}) collective-permute-start(f32[4,128,128]{2,1,0:T(8,128)S(1)} %get-tuple-element.44), channel_id=1, source_target_pairs={{1,0},{2,1},{3,2},{4,3},{5,4},{6,5},{7,6},{8,7},{9,8},{10,9},{11,1... | collective-permute-start | bytes 786440 | tf_op jit(solution)/shard_map/ppermute | solution.py:544
  27.5 0.0 collective-permute-done.2.from_left
  27.5 1.1 collective-permute-done.3.from_right
  28.6 3.7 %model.1 = (f32[576,1,128]{2,1,0:T(1,128)S(1)}, f32[2,2,2,128,128]{4,3,2,1,0:T(8,128)S(1)}) custom-call(s32[2,2]{1,0:T(2,128)} %bitcast.13, f32[4,64,128]{2,1,0:T(8,128)S(1)} %get-tuple-element.35.after.upper, f32[4,64,128]{2,1,0:T(8,128)S(1)} %get-tuple-element.36.lower, f32[4,64,128]{2,1,0:T(8,128)S(1)} %collective-permute-done.above, ...), custom_call_target="tpu_custom_call" | custom-call | tf_op jit(solution)/shard_map/model/pallas_call | solution.py:546
  32.3 22.2 %all_to_all.15.gathered = f32[576,1,128]{2,1,0:T(1,128)S(1)} all-to-all(f32[576,1,128]{2,1,0:T(1,128)S(1)} %get-tuple-element.49), channel_id=1, replica_groups={{0,1,32,33,64,65,96,97,128,129,160,161,192,193,224,225,256,257,288,289,..., dimensions={0} | all-to-all | bytes 589824 | tf_op jit(solution)/shard_map/all_to_all | solution.py:469
  54.6 1.1 mix.1
  55.7 18.9 %all-to-all-start.1 = ((f32[16,4,8,128]{3,2,1,0:T(8,128)}), f32[16,4,8,128]{3,2,1,0:T(8,128)S(1)}, u32[]{:S(2)}, u32[]{:S(2)}) async-start(f32[16,4,8,128]{3,2,1,0:T(8,128)} %mix.1), calls=%async_computation.1 | async-start | bytes 524288 | tf_op jit(solution)/shard_map/all_to_all | solution.py:469
  74.6 1.1 deposit.1
  75.7 1.3 %collective-permute-start.4 = (f32[4,64,256]{2,1,0:T(8,128)S(1)}, f32[4,64,256]{2,1,0:T(8,128)S(1)}, u32[]{:S(2)}, u32[]{:S(2)}) collective-permute-start(f32[4,64,256]{2,1,0:T(8,128)S(1)} %get-tuple-element.51), channel_id=1, source_target_pairs={{32,0},{64,32},{96,64},{128,96},{160,128},{192,160},{224,192},{256... | collective-permute-start | bytes 786440 | tf_op jit(solution)/shard_map/ppermute | solution.py:602
  77.0 4.0 %collective-permute-start.5 = (f32[4,64,256]{2,1,0:T(8,128)S(1)}, f32[4,64,256]{2,1,0:T(8,128)S(1)}, u32[]{:S(2)}, u32[]{:S(2)}) collective-permute-start(f32[4,64,256]{2,1,0:T(8,128)S(1)} %get-tuple-element.52), channel_id=1, source_target_pairs={{0,32},{32,64},{64,96},{96,128},{128,160},{160,192},{192,224},{224... | collective-permute-start | bytes 786440 | tf_op jit(solution)/shard_map/ppermute | solution.py:603
  81.0 7.8 %all-to-all-done.1.parts = f32[16,4,8,128]{3,2,1,0:T(8,128)S(1)} async-done(((f32[16,4,8,128]{3,2,1,0:T(8,128)}), f32[16,4,8,128]{3,2,1,0:T(8,128)S(1)}, u32[]{:S(2)}, u32[]{:S(2)}) %all-to-all-start.1) | async-done | bytes 262176 | tf_op jit(solution)/shard_map/all_to_all | solution.py:469
  88.8 0.8 repeat.1
  89.7 0.0 copy-start
  89.7 0.0 collective-permute-done.4.from_below
  89.7 0.0 collective-permute-done.5.from_above
  89.7 4.7 %all-to-all-start.2 = ((f32[32,4,8,128]{3,2,1,0:T(8,128)}), f32[32,4,8,128]{3,2,1,0:T(8,128)S(1)}, u32[]{:S(2)}, u32[]{:S(2)}) async-start(f32[32,4,8,128]{3,2,1,0:T(8,128)} %repeat.1), calls=%async_computation.2 | async-start | bytes 1048576 | tf_op jit(solution)/shard_map/all_to_all | solution.py:469
  94.4 0.1 merge.1
  94.5 7.8 %collective-permute-start.6 = (f32[4,64,128]{2,1,0:T(8,128)S(1)}, f32[4,64,128]{2,1,0:T(8,128)S(1)}, u32[]{:S(2)}, u32[]{:S(2)}) collective-permute-start(f32[4,64,128]{2,1,0:T(8,128)S(1)} %get-tuple-element.57), channel_id=1, source_target_pairs={{0,1},{1,2},{2,3},{3,4},{4,5},{5,6},{6,7},{7,8},{8,9},{9,10},{10,1... | collective-permute-start | bytes 393224 | tf_op jit(solution)/shard_map/ppermute | solution.py:626
  102.3 1.9 %collective-permute-start.7 = (f32[4,64,128]{2,1,0:T(8,128)S(1)}, f32[4,64,128]{2,1,0:T(8,128)S(1)}, u32[]{:S(2)}, u32[]{:S(2)}) collective-permute-start(f32[4,64,128]{2,1,0:T(8,128)S(1)} %get-tuple-element.58), channel_id=1, source_target_pairs={{1,0},{2,1},{3,2},{4,3},{5,4},{6,5},{7,6},{8,7},{9,8},{10,9},{11,1... | collective-permute-start | bytes 393224 | tf_op jit(solution)/shard_map/ppermute | solution.py:627
  104.3 0.0 collective-permute-done.6.from_left
  104.3 4.6 %collective-permute-done.7.from_right = f32[4,64,128]{2,1,0:T(8,128)S(1)} collective-permute-done((f32[4,64,128]{2,1,0:T(8,128)S(1)}, f32[4,64,128]{2,1,0:T(8,128)S(1)}, u32[]{:S(2)}, u32[]{:S(2)}) %collective-permute-start.7) | collective-permute-done | bytes 131104 | tf_op jit(solution)/shard_map/ppermute | solution.py:627
  108.9 0.0 all-to-all-done.2.mine
  108.9 6.7 %collective-permute-start.8 = (f32[32,4,8,128]{3,2,1,0:T(8,128)S(1)}, f32[32,4,8,128]{3,2,1,0:T(8,128)S(1)}, u32[]{:S(2)}, u32[]{:S(2)}) collective-permute-start(f32[32,4,8,128]{3,2,1,0:T(8,128)S(1)} %all-to-all-done.2.mine), channel_id=1, source_target_pairs={{0,1},{1,0},{2,3},{3,2},{4,5},{5,4},{6,7},{7,6},{8,9},{9,8},{10,11... | collective-permute-start | bytes 1572872 | tf_op jit(solution)/shard_map/ppermute | solution.py:638
  115.6 0.0 copy-done
  115.6 0.5 own_half.1
  116.1 0.8 finish.1
  116.9 0.2 collective-permute-done.8.other
  117.1 2.5 %orthonormal.1 = f32[8,2,16,8,128]{4,3,2,1,0:T(8,128)} custom-call(s32[1]{0:T(128)} %bitcast.5.core, f32[32,4,8,128]{3,2,1,0:T(8,128)S(1)} %collective-permute-done.8.other, f32[4,32,8,128]{3,2,1,0:T(8,128)S(1)} %get-tuple-element.65.own_pairs, f32[4,32,8,128]{3,2,1,0:T(8,128)S(1)} %get-tuple-element.66.base_pairs, f32[36,8,128]{2,1,0:T(8,128)S(1)} %get-tuple-element.67.sums_in), custom_call_target="tpu_custom_call" | custom-call | tf_op jit(solution)/shard_map/orthonormal/pallas_call | solution.py:659
Async XLA Ops:
  1.6 7.5 %collective-permute-start.1 = (f32[4,64,128]{2,1,0:T(8,128)S(1)}, f32[4,64,128]{2,1,0:T(8,128)S(1)}, u32[]{:S(2)}, u32[]{:S(2)}) collective-permute-start(f32[4,64,128]{2,1,0:T(8,128)S(1)} %get-tuple-element.35.after.upper), channel_id=1, source_target_pairs={{32,0},{64,32},{96,64},{128,96},{160,128},{192,160},{224,192},{256... | collective-permute-start | bytes 393224 | tf_op jit(solution)/shard_map/ppermute | solution.py:507
  2.9 6.5 %collective-permute-start = (f32[4,64,128]{2,1,0:T(8,128)S(1)}, f32[4,64,128]{2,1,0:T(8,128)S(1)}, u32[]{:S(2)}, u32[]{:S(2)}) collective-permute-start(f32[4,64,128]{2,1,0:T(8,128)S(1)} %get-tuple-element.36.lower), channel_id=1, source_target_pairs={{0,32},{32,64},{64,96},{96,128},{128,160},{160,192},{192,224},{224... | collective-permute-start | bytes 393224 | tf_op jit(solution)/shard_map/ppermute | solution.py:506
  9.6 17.9 %collective-permute-start.2 = (f32[4,128,128]{2,1,0:T(8,128)S(1)}, f32[4,128,128]{2,1,0:T(8,128)S(1)}, u32[]{:S(2)}, u32[]{:S(2)}) collective-permute-start(f32[4,128,128]{2,1,0:T(8,128)S(1)} %get-tuple-element.43), channel_id=1, source_target_pairs={{0,1},{1,2},{2,3},{3,4},{4,5},{5,6},{6,7},{7,8},{8,9},{9,10},{10,1... | collective-permute-start | bytes 786440 | tf_op jit(solution)/shard_map/ppermute | solution.py:543
  15.5 13.1 %collective-permute-start.3 = (f32[4,128,128]{2,1,0:T(8,128)S(1)}, f32[4,128,128]{2,1,0:T(8,128)S(1)}, u32[]{:S(2)}, u32[]{:S(2)}) collective-permute-start(f32[4,128,128]{2,1,0:T(8,128)S(1)} %get-tuple-element.44), channel_id=1, source_target_pairs={{1,0},{2,1},{3,2},{4,3},{5,4},{6,5},{7,6},{8,7},{9,8},{10,9},{11,1... | collective-permute-start | bytes 786440 | tf_op jit(solution)/shard_map/ppermute | solution.py:544
  55.7 33.1 %all-to-all-start.1 = ((f32[16,4,8,128]{3,2,1,0:T(8,128)}), f32[16,4,8,128]{3,2,1,0:T(8,128)S(1)}, u32[]{:S(2)}, u32[]{:S(2)}) async-start(f32[16,4,8,128]{3,2,1,0:T(8,128)} %mix.1), calls=%async_computation.1 | async-start | bytes 524288 | tf_op jit(solution)/shard_map/all_to_all | solution.py:469
  75.7 14.0 %collective-permute-start.4 = (f32[4,64,256]{2,1,0:T(8,128)S(1)}, f32[4,64,256]{2,1,0:T(8,128)S(1)}, u32[]{:S(2)}, u32[]{:S(2)}) collective-permute-start(f32[4,64,256]{2,1,0:T(8,128)S(1)} %get-tuple-element.51), channel_id=1, source_target_pairs={{32,0},{64,32},{96,64},{128,96},{160,128},{192,160},{224,192},{256... | collective-permute-start | bytes 786440 | tf_op jit(solution)/shard_map/ppermute | solution.py:602
  77.0 12.7 %collective-permute-start.5 = (f32[4,64,256]{2,1,0:T(8,128)S(1)}, f32[4,64,256]{2,1,0:T(8,128)S(1)}, u32[]{:S(2)}, u32[]{:S(2)}) collective-permute-start(f32[4,64,256]{2,1,0:T(8,128)S(1)} %get-tuple-element.52), channel_id=1, source_target_pairs={{0,32},{32,64},{64,96},{96,128},{128,160},{160,192},{192,224},{224... | collective-permute-start | bytes 786440 | tf_op jit(solution)/shard_map/ppermute | solution.py:603
  89.7 26.0 %copy-start = (f32[8,2,128,128]{3,2,1,0:T(8,128)S(1)}, f32[8,2,128,128]{3,2,1,0:T(8,128)}, u32[]{:S(2)}) copy-start(f32[8,2,128,128]{3,2,1,0:T(8,128)} %basis_in.1) | copy-start | bytes 3145732
  89.7 19.2 %all-to-all-start.2 = ((f32[32,4,8,128]{3,2,1,0:T(8,128)}), f32[32,4,8,128]{3,2,1,0:T(8,128)S(1)}, u32[]{:S(2)}, u32[]{:S(2)}) async-start(f32[32,4,8,128]{3,2,1,0:T(8,128)} %repeat.1), calls=%async_computation.2 | async-start | bytes 1048576 | tf_op jit(solution)/shard_map/all_to_all | solution.py:469
  94.5 9.8 %collective-permute-start.6 = (f32[4,64,128]{2,1,0:T(8,128)S(1)}, f32[4,64,128]{2,1,0:T(8,128)S(1)}, u32[]{:S(2)}, u32[]{:S(2)}) collective-permute-start(f32[4,64,128]{2,1,0:T(8,128)S(1)} %get-tuple-element.57), channel_id=1, source_target_pairs={{0,1},{1,2},{2,3},{3,4},{4,5},{5,6},{6,7},{7,8},{8,9},{9,10},{10,1... | collective-permute-start | bytes 393224 | tf_op jit(solution)/shard_map/ppermute | solution.py:626
  102.3 6.6 %collective-permute-start.7 = (f32[4,64,128]{2,1,0:T(8,128)S(1)}, f32[4,64,128]{2,1,0:T(8,128)S(1)}, u32[]{:S(2)}, u32[]{:S(2)}) collective-permute-start(f32[4,64,128]{2,1,0:T(8,128)S(1)} %get-tuple-element.58), channel_id=1, source_target_pairs={{1,0},{2,1},{3,2},{4,3},{5,4},{6,5},{7,6},{8,7},{9,8},{10,9},{11,1... | collective-permute-start | bytes 393224 | tf_op jit(solution)/shard_map/ppermute | solution.py:627
  108.9 8.2 %collective-permute-start.8 = (f32[32,4,8,128]{3,2,1,0:T(8,128)S(1)}, f32[32,4,8,128]{3,2,1,0:T(8,128)S(1)}, u32[]{:S(2)}, u32[]{:S(2)}) collective-permute-start(f32[32,4,8,128]{3,2,1,0:T(8,128)S(1)} %all-to-all-done.2.mine), channel_id=1, source_target_pairs={{0,1},{1,0},{2,3},{3,2},{4,5},{5,4},{6,7},{7,6},{8,9},{9,8},{10,11... | collective-permute-start | bytes 1572872 | tf_op jit(solution)/shard_map/ppermute | solution.py:638
